TPU v7x, 32 devices: a whole 2x2x4 slice. The times are simulated.
32 devices in a mesh: space: 4 (over x, core), tm: 8 (over z, y).
Axes of the slice: x: 2, y: 2, z: 4, core: 2. Of those that a mesh axis runs over, the one named last changes fastest.
Arguments:
- snapshots: bfloat16 [4096, 65536], P('tm', 'space'), may hold values from -24 to 24
- freq_bins: int32 [2], replicated, may hold values from 1 to 127
Outputs:
- gram_matrix: float32 [2, 64, 64], replicated
- whitened: float32 [2, 64, 65536], P(None, None, ('space', 'tm'))
All inputs are finite; a program needn't handle non-finite values.
Results may differ from a plain program's by a relative error of at most 0.0041.
Values may be sent and summed in bfloat16 or wider, within the bound.
No kernel may reach another device: no remote copies, remote signals or barrier semaphores. Data moves between devices by JAX's collectives and lax.ppermute only.
A program may use at most 128 MiB of HBM per device.

v0:
```python
import jax
import jax.numpy as jnp
from jax import lax
from jax.sharding import PartitionSpec as P

NFFT = 256
HOP = 128
NF = 2


ridge_term = 0.01


def passed_along(array, axis, by):
    devices = lax.axis_size(axis)
    return lax.ppermute(array, axis, [(i, (i + by) % devices) for i in range(devices)])


def make_table(freq_bins):
    sample = jnp.arange(NFFT, dtype=jnp.int32)
    sample_f = sample.astype(jnp.float32)
    hann_taper = 0.5 - 0.5 * jnp.cos(2.0 * jnp.pi * sample_f / NFFT)
    window = hann_taper / jnp.sqrt(jnp.sum(hann_taper * hann_taper))
    phase_idx = freq_bins[:, None] * sample[None, :] % NFFT
    angles = 2.0 * jnp.pi * phase_idx.astype(jnp.float32) / NFFT
    table = jnp.stack([window * jnp.cos(angles), -window * jnp.sin(angles)], axis=1)
    return table.astype(jnp.bfloat16)


def on_device(snapshots, freq_bins):
    points = snapshots.shape[1]
    block_count = snapshots.shape[0] // HOP
    table_rows = make_table(freq_bins).reshape(NF * 2, NFFT)
    first_table = table_rows[:, :HOP]
    second_table = table_rows[:, HOP:]
    halves = snapshots.reshape(block_count, HOP, points)
    lead_part = jnp.einsum("ct,htp->chp", first_table, halves, preferred_element_type=jnp.float32)
    trail_part = jnp.einsum("ct,htp->chp", second_table, halves, preferred_element_type=jnp.float32)
    incoming = passed_along(trail_part[:, :1], "tm", -1)
    trail_own = trail_part[:, 1:]
    coeffs = lead_part + jnp.concatenate([trail_own, incoming], axis=1)
    slice_width = points // lax.axis_size("tm")
    position = lax.axis_index("tm") * slice_width
    local_cols = lax.dynamic_slice_in_dim(
        lax.all_gather(coeffs, "tm", axis=1, tiled=True), position, slice_width, 2
    )
    all_blocks_count = local_cols.shape[1]
    columns = local_cols.reshape(NF, 2 * all_blocks_count, slice_width)
    grid_total = points * lax.axis_size("space")
    partial_value = (
        jnp.einsum("fcp,fdp->fcd", columns, columns, precision=lax.Precision.HIGHEST) / grid_total
    )
    gram_matrix = lax.psum(partial_value, ("space", "tm"))
    identity = jnp.eye(2 * all_blocks_count, dtype=jnp.float32)
    factor = jnp.linalg.cholesky(gram_matrix + ridge_term * identity[None])
    whitened = lax.linalg.triangular_solve(factor, columns, left_side=True, lower=True)
    return (gram_matrix, whitened)


def solution(mesh):
    placed = (P("tm", "space"), P())
    return jax.shard_map(
        on_device,
        mesh=mesh,
        in_specs=placed,
        out_specs=(P(), P(None, None, ("space", "tm"))),
        check_vma=False,
    )
```

profile of v0, /device:TPU:0, one launch (start us, length us, event | category | flops | bytes accessed | tf_op | source)
XLA Modules:
  0.0 232.3 jit_solution(7412217076847700622)
XLA Ops:
  7.2 0.0 all-gather.2.cloned.1.call-start
  7.2 0.6 multiply_reduce_fusion
  8.6 0.8 multiply_convert_fusion.1
  9.4 0.0 copy-start
  9.4 8.2 %fusion.6 = f32[4,4,16384]{2,0,1:T(4,128)S(1)} fusion(bf16[4,128,16384]{2,1,0:T(8,128)(2,1)} %bitcast.24, bf16[4,256]{1,0:T(4,128)(2,1)S(1)} %convert_element_type.35), kind=kOutput, calls=%fused_computation.23 | convolution fusion | flops 67108864 | bytes 17826816 | tf_op jit(solution)/shard_map/ct,htp->chp/dot_general | solution.py:38
  17.7 6.1 %collective-permute-start = (f32[4,1,16384]{2,0,1:T(4,128)S(1)}, f32[4,1,16384]{2,0,1:T(4,128)S(1)}, u32[]{:S(2)}, u32[]{:S(2)}) collective-permute-start(f32[4,1,16384]{2,0,1:T(4,128)S(1)} %slice.29), channel_id=1, source_target_pairs={{0,7},{1,0},{2,1},{3,2},{4,3},{5,4},{6,5},{7,6},{8,15},{9,8},{10,9... | collective-permute-start | bytes 786440 | tf_op jit(solution)/shard_map/ppermute | solution.py:16
  23.7 0.1 slice.28
  23.8 5.5 %collective-permute-done = f32[4,1,16384]{2,0,1:T(4,128)S(1)} collective-permute-done((f32[4,1,16384]{2,0,1:T(4,128)S(1)}, f32[4,1,16384]{2,0,1:T(4,128)S(1)}, u32[]{:S(2)}, u32[]{:S(2)}) %collective-permute-start) | collective-permute-done | bytes 262176 | tf_op jit(solution)/shard_map/ppermute | solution.py:16
  29.3 0.0 copy-done
  29.3 3.3 %maximum_add_fusion = f32[4,4,16384]{2,0,1:T(4,128)} fusion(f32[4,1,16384]{2,0,1:T(4,128)S(1)} %collective-permute-done, f32[4,3,16384]{2,0,1:T(4,128)S(1)} %slice.28, bf16[4,128,16384]{2,1,0:T(8,128)(2,1)S(1)} %bitcast.25, bf16[4,256]{1,0:T(4,128)(2,1)S(1)} %convert_element_type.35), kind=kOutput, calls=%fused_computation.1 | convolution fusion | flops 67633152 | bytes 18875392 | tf_op jit(solution)/shard_map/ct,htp->chp/dot_general | solution.py:37
  32.6 0.0 all-gather.2.cloned.1.call-update
  32.6 0.1 copy.36
  32.7 126.4 %all-gather.2.cloned.1.call-done = f32[4,32,16384]{2,0,1:T(4,128)} async-done(((f32[4,4,16384]{2,0,1:T(4,128)}), f32[4,32,16384]{2,0,1:T(4,128)}) %all-gather.2.cloned.1.call-update) | async-done | bytes 8388624 | tf_op jit(solution)/shard_map/all_gather | solution.py:45
  159.1 1.3 constant_dynamic-slice_fusion
  160.4 0.6 copy.42
  161.0 1.1 convolution_multiply_fusion
  162.1 38.7 %psum.7 = f32[2,64,64]{1,2,0:T(8,128)S(1)} all-reduce(f32[2,64,64]{1,2,0:T(8,128)S(1)} %convolution_multiply_fusion), channel_id=1, replica_groups=mesh['space'=4,'tm'=8] {'space','tm'}, use_global_device_ids=true, to_apply=%region_1.2 | all-reduce | flops 8192 | bytes 65536 | tf_op jit(solution)/shard_map/psum | solution.py:53
  200.8 0.7 copy.39
  201.5 0.1 copy.37
  201.6 11.7 %custom-call.7 = f32[2,64,64]{2,1,0:T(8,128)S(1)} custom-call(f32[2,64,64]{2,1,0:T(8,128)S(1)} %fusion.2), custom_call_target="Cholesky" | custom-call | tf_op jit(solution)/shard_map/jit(cholesky)/cholesky | solution.py:55
  213.4 0.1 compare_reduce_fusion
  213.5 0.1 select_bitcast_fusion
  213.6 9.8 %custom-call.8 = f32[2,1,64,64]{2,3,1,0:T(8,128)S(1)} custom-call(f32[2,1,64,64]{3,2,1,0:T(8,128)S(1)} %select_bitcast_fusion), custom_call_target="InvertDiagBlocksLowerTriangular" | custom-call | tf_op jit(solution)/shard_map/triangular_solve | solution.py:56
  223.4 2.0 fusion
  (11 shorter events, 0.2 us)
Async XLA Ops:
  7.2 151.9 %all-gather.2.cloned.1.call-start = ((), (), s32[]{:S(2)}) async-start(), calls=%async_computation | async-start | bytes 9437184 | tf_op jit(solution)/shard_map/all_gather | solution.py:45
  9.4 19.9 %copy-start = (bf16[512,16384]{1,0:T(8,128)(2,1)S(1)}, bf16[512,16384]{1,0:T(8,128)(2,1)}, u32[]{:S(2)}) copy-start(bf16[512,16384]{1,0:T(8,128)(2,1)} %param.2) | copy-start | bytes 50331652
  17.7 11.7 %collective-permute-start = (f32[4,1,16384]{2,0,1:T(4,128)S(1)}, f32[4,1,16384]{2,0,1:T(4,128)S(1)}, u32[]{:S(2)}, u32[]{:S(2)}) collective-permute-start(f32[4,1,16384]{2,0,1:T(4,128)S(1)} %slice.29), channel_id=1, source_target_pairs={{0,7},{1,0},{2,1},{3,2},{4,3},{5,4},{6,5},{7,6},{8,15},{9,8},{10,9... | collective-permute-start | bytes 786440 | tf_op jit(solution)/shard_map/ppermute | solution.py:16
Sparse Core Ops, SparseCore 0:
  32.7 126.3 all-gather.1
where the time goes:
time: 233 us; the launch traced here: 232 us
  waiting for transfers between devices  132 us (57%)
  blocking collectives  38.7 us (17%)
  other arithmetic  23.3 us (10%)
  between operations  14.8 us (6%)
  matrix products  14.6 us (6%)
  starting transfers between devices  6.12 us (3%)
  local copies, waits for them, and re-layouts  2.87 us (1%)
    all_gather x1, waiting for transfers between devices, on_device(): lax.all_gather(coeffs, 'tm', axis=1, tiled=True)  126 us
    psum x1, blocking collectives, on_device(): gram_matrix = lax.psum(partial_value, ('space', 'tm'))  38.7 us
    another operation x4, other arithmetic, on_device(): factor = jnp.linalg.cholesky(gram_matrix + ridge_term * identity[None])  11.9 us
    another operation x3, other arithmetic, on_device(): lax.linalg.triangular_solve(factor, columns, left_side=True, lower=True)  9.92 us
    dot_general x1, matrix products, on_device(): jnp.einsum('ct,htp->chp', second_table, halves, preferred_element_type=jn...  8.19 us
    ppermute x1, starting transfers between devices, passed_along(): lax.ppermute(array, axis, [(i, (i + by) % devices) for i in range(devices)])  6.09 us
    ppermute x1, waiting for transfers between devices, passed_along(): lax.ppermute(array, axis, [(i, (i + by) % devices) for i in range(devices)])  5.51 us
  transfers between devices with their start and end apart: 2, of which 2 were waited for; matrix products, arithmetic and copies ran while one was open for 0% of the time, Pallas kernels for 0%

commit v1 on v0

v1 whole, which is shorter than its diff:
```python
import math

import jax
import jax.numpy as jnp
import numpy as np
from jax import lax
from jax.experimental import pallas as pl
from jax.experimental.pallas import tpu as pltpu
from jax.sharding import PartitionSpec as P

NFFT = 256
HOP = 128
NF = 2
SERIES = 2 * NF
SUB = 8

ridge_term = 0.01


def window_norm():
    sample = np.arange(NFFT, dtype=np.float64)
    taper = 0.5 - 0.5 * np.cos(2.0 * np.pi * sample / NFFT)
    return float(np.sqrt(np.sum(taper * taper)))


def fill_table(freq_ref, shape, half_count):
    row = lax.broadcasted_iota(jnp.int32, shape, 0)
    col = lax.broadcasted_iota(jnp.int32, shape, 1)
    group = row // SERIES
    series = row % SERIES
    block = jnp.where(group == half_count, -1, group)
    half = col // HOP
    trailing = half == block + 1
    leading = half == block
    sample = col % HOP + jnp.where(trailing, HOP, 0)
    bins = jnp.where(series // 2 == 0, freq_ref[0], freq_ref[1])
    phase = (bins * sample + jnp.where(series % 2 == 1, NFFT // 4, 0)) % NFFT
    step = 2.0 * math.pi / NFFT
    taper = 0.5 - 0.5 * jnp.cos(step * sample.astype(jnp.float32))
    wave = jnp.cos(step * phase.astype(jnp.float32))
    value = taper * (1.0 / window_norm()) * wave
    used = (trailing | leading) & (group <= half_count)
    return jnp.where(used, value, 0.0).astype(jnp.bfloat16)


def block_sums(freq_bins, snapshots, shards):
    samples, points = snapshots.shape
    half_count = samples // HOP
    rows = SERIES * half_count
    width = points // shards
    fold = width // half_count
    table_rows = rows + SUB * 2

    def body(freq_ref, data_ref, out_ref, table_ref):
        @pl.when(pl.program_id(0) == 0)
        def _():
            table_ref[...] = fill_table(freq_ref, table_ref.shape, half_count)

        sums = jnp.dot(table_ref[...], data_ref[...], preferred_element_type=jnp.float32)
        out_ref[0, :, :width] = sums[:rows].astype(jnp.bfloat16)
        early = sums[rows : rows + SERIES]
        folded = jnp.concatenate(
            [early[:, k * fold : (k + 1) * fold] for k in range(half_count)], axis=0
        )
        out_ref[0, :, width:] = folded.astype(jnp.bfloat16)

    return pl.pallas_call(
        body,
        grid=(shards,),
        in_specs=[
            pl.BlockSpec(memory_space=pltpu.SMEM),
            pl.BlockSpec((samples, width), lambda d: (0, d)),
        ],
        out_specs=pl.BlockSpec((1, rows, width + fold), lambda d: (d, 0, 0)),
        out_shape=jax.ShapeDtypeStruct((shards, rows, width + fold), jnp.bfloat16),
        scratch_shapes=[pltpu.VMEM((table_rows, samples), jnp.bfloat16)],
        name="block_sums",
    )(freq_bins, snapshots)


def join_matrix(shards, half_count):
    rows = SERIES * half_count
    block_count = shards * half_count
    out = np.zeros((half_count, SERIES * block_count, 2 * shards * rows), np.float32)
    for k in range(half_count):
        for series in range(SERIES):
            for shard in range(shards):
                for j in range(half_count):
                    target = series * block_count + shard * half_count + j
                    out[k, target, shard * rows + j * SERIES + series] = 1.0
                    if j == half_count - 1:
                        after = (shard + 1) % shards
                        out[k, target, (shards + after) * rows + k * SERIES + series] = 1.0
    return jnp.asarray(out, jnp.bfloat16)


def join_and_gram(received, half_count, grid_total):
    shards, rows, span = received.shape
    width = span * half_count // (half_count + 1)
    fold = width // half_count
    total = shards * rows
    size = total // NF

    def body(join_ref, data_ref, columns_ref, gram_ref):
        folded = data_ref[:, :, width:].reshape(total, fold)
        for k in range(half_count):
            own = data_ref[:, :, k * fold : (k + 1) * fold].reshape(total, fold)
            both = jnp.concatenate([own, folded], axis=0)
            joined = jnp.dot(join_ref[k], both, preferred_element_type=jnp.float32)
            columns_ref[:, k * fold : (k + 1) * fold] = joined.astype(jnp.bfloat16)
        columns = columns_ref[...]
        products = lax.dot_general(
            columns, columns, (((1,), (1,)), ((), ())), preferred_element_type=jnp.float32
        )
        for f in range(NF):
            part = products[f * size : (f + 1) * size, f * size : (f + 1) * size]
            gram_ref[:, f * size : (f + 1) * size] = part * (1.0 / grid_total)

    return pl.pallas_call(
        body,
        out_shape=(
            jax.ShapeDtypeStruct((total, width), jnp.bfloat16),
            jax.ShapeDtypeStruct((size, NF * size), jnp.float32),
        ),
        name="join_and_gram",
    )(join_matrix(shards, half_count), received)


def exchange_sum(value, axis):
    devices = lax.axis_size(axis)
    step = 1
    while step < devices:
        value = value + lax.ppermute(value, axis, [(i, i ^ step) for i in range(devices)])
        step *= 2
    return value


def inverse_factor(gram_ref, work_ref, inverse_ref, size):
    lanes = NF * size
    row = lax.broadcasted_iota(jnp.int32, (size, lanes), 0)
    lane = lax.broadcasted_iota(jnp.int32, (size, lanes), 1) % size
    eye = jnp.where(row == lane, 1.0, 0.0)
    work_ref[...] = gram_ref[...] + ridge_term * eye
    inverse_ref[...] = eye
    sub = lax.broadcasted_iota(jnp.int32, (SUB, lanes), 0)
    for start in range(0, size, SUB):
        stop = start + SUB
        left = work_ref[start:, :]
        columns = []
        for m in range(SUB):
            columns.append(
                jnp.concatenate(
                    [
                        jnp.broadcast_to(
                            left[:, f * size + start + m : f * size + start + m + 1],
                            (size - start, size),
                        )
                        for f in range(NF)
                    ],
                    axis=1,
                )
            )

        def spread(array, i):
            return jnp.broadcast_to(array[i : i + 1, :], (SUB, lanes))

        d = [[spread(columns[j], i) for j in range(i + 1)] for i in range(SUB)]
        low = [[None] * SUB for _ in range(SUB)]
        for k in range(SUB):
            scale = lax.rsqrt(d[k][k])
            for j in range(k):
                low[k][j] = low[k][j] * scale
            low[k][k] = scale
            below = [d[i][k] * scale for i in range(k + 1, SUB)]
            for i in range(k + 1, SUB):
                x = below[i - k - 1]
                for j in range(k + 1, i + 1):
                    d[i][j] = d[i][j] - x * below[j - k - 1]
                for j in range(k + 1):
                    term = x * low[k][j]
                    low[i][j] = -term if low[i][j] is None else low[i][j] - term
        top = work_ref[start:stop, :]
        side = inverse_ref[start:stop, :]

        def solve_rows(block):
            source = [spread(block, m) for m in range(SUB)]
            solved = []
            for j in range(SUB):
                acc = low[j][0] * source[0]
                for m in range(1, j + 1):
                    acc = acc + low[j][m] * source[m]
                solved.append(acc)
            return solved

        def apply_transposed(solved):
            out = []
            for m in range(SUB):
                acc = low[m][m] * solved[m]
                for j in range(m + 1, SUB):
                    acc = acc + low[j][m] * solved[j]
                out.append(acc)
            return out

        solved_side = solve_rows(side)
        packed = solved_side[0]
        for j in range(1, SUB):
            packed = jnp.where(sub == j, solved_side[j], packed)
        inverse_ref[start:stop, :] = packed
        if stop < size:
            weights_top = apply_transposed(solve_rows(top))
            weights_side = apply_transposed(solved_side)
            for first in range(stop, size, SUB):
                rest = work_ref[first : first + SUB, :]
                rest_side = inverse_ref[first : first + SUB, :]
                for m in range(SUB):
                    column = columns[m][first - start : first - start + SUB]
                    rest = rest - column * weights_top[m]
                    rest_side = rest_side - column * weights_side[m]
                work_ref[first : first + SUB, :] = rest
                inverse_ref[first : first + SUB, :] = rest_side


def whiten(gram, columns):
    size = gram.shape[0]
    total, width = columns.shape
    chunk = min(width, 512)

    def body(gram_ref, columns_ref, gram_out, white_ref, work_ref, inverse_ref, left_ref):
        for f in range(NF):
            gram_out[f] = gram_ref[:, f * size : (f + 1) * size]
        inverse_factor(gram_ref, work_ref, inverse_ref, size)
        lane = lax.broadcasted_iota(jnp.int32, (size, NF * size), 1)
        for f in range(NF):
            own = jnp.where(lane // size == f, inverse_ref[...], 0.0)
            high = own.astype(jnp.bfloat16)
            rest = (own - high.astype(jnp.float32)).astype(jnp.bfloat16)
            left_ref[f * size : (f + 1) * size, : NF * size] = high
            left_ref[f * size : (f + 1) * size, NF * size :] = rest
        for first in range(0, width, chunk):
            part = columns_ref[:, first : first + chunk]
            both = jnp.concatenate([part, part], axis=0)
            done = jnp.dot(left_ref[...], both, preferred_element_type=jnp.float32)
            for f in range(NF):
                white_ref[f, :, first : first + chunk] = done[f * size : (f + 1) * size]

    return pl.pallas_call(
        body,
        out_shape=(
            jax.ShapeDtypeStruct((NF, size, size), jnp.float32),
            jax.ShapeDtypeStruct((NF, size, width), jnp.float32),
        ),
        scratch_shapes=[
            pltpu.VMEM((size, NF * size), jnp.float32),
            pltpu.VMEM((size, NF * size), jnp.float32),
            pltpu.VMEM((total, 2 * NF * size), jnp.bfloat16),
        ],
        name="whiten",
    )(gram, columns)


def on_device(snapshots, freq_bins):
    shards = lax.axis_size("tm")
    half_count = snapshots.shape[0] // HOP
    grid_total = snapshots.shape[1] * lax.axis_size("space")
    parts = block_sums(freq_bins, snapshots, shards)
    received = lax.all_to_all(parts, "tm", 0, 0, tiled=True)
    columns, gram = join_and_gram(received, half_count, grid_total)
    gram = exchange_sum(exchange_sum(gram, "space"), "tm")
    return whiten(gram, columns)


def solution(mesh):
    placed = (P("tm", "space"), P())
    return jax.shard_map(
        on_device,
        mesh=mesh,
        in_specs=placed,
        out_specs=(P(), P(None, None, ("space", "tm"))),
        check_vma=False,
    )
```

time: 233 us -> 62.6 us (0.27)
  waiting for transfers between devices: 132 us -> 13.6 us
  other arithmetic: 23.3 us -> 1.39 us
  Pallas kernels: 0 us -> 17.2 us
  matrix products: 14.6 us -> 0 us
  between operations: 14.8 us -> 0.64 us
  blocking collectives: 38.7 us -> 25.1 us
  local copies, waits for them, and re-layouts: 2.87 us -> 0 us
    all_gather x1 -> x0, waiting for transfers between devices: 126 us -> none  [on_device(): lax.all_gather(coeffs, 'tm', axis=1, tiled=True)]
    psum x1 -> x0, blocking collectives: 38.7 us -> none  [on_device(): gram_matrix = lax.psum(partial_value, ('space', 'tm'))]
    all_to_all x0 -> x1, blocking collectives: none -> 25.1 us  [on_device(): received = lax.all_to_all(parts, 'tm', 0, 0, tiled=True)]
    another operation x9 -> x0, other arithmetic: 22.6 us -> none  [the longest x4 11.9 us: on_device(): factor = jnp.linalg.cholesky(gram_matrix + ridge_term * identity[None])]
    pallas_call x0 -> x3, Pallas kernels: none -> 17.2 us  [the longest x1 10.5 us: block_sums(): pl.pallas_call(body, grid=(shards,), in_specs=[pl.BlockSpec(memory_space=...]
    dot_general x3 -> x0, matrix products: 12.5 us -> none  [the longest x1 8.19 us: on_device(): jnp.einsum('ct,htp->chp', second_table, halves, preferred_element_type=jn...]
    ppermute x1 -> x5, waiting for transfers between devices: 5.51 us -> 13.6 us  [exchange_sum(): lax.ppermute(value, axis, [(i, i ^ step) for i in range(devices)])]
    ppermute x1 -> x5, starting transfers between devices: 6.09 us -> 4.41 us  [exchange_sum(): lax.ppermute(value, axis, [(i, i ^ step) for i in range(devices)])]
  transfers between devices with their start and end apart: 2 -> 5, of which waited for: 2 -> 5; matrix products, arithmetic and copies ran while one was open for 0% -> 0% of each run, Pallas kernels for 0% -> 0%
where the time goes in v1:
time: 62.6 us; the launch traced here: 62.3 us
  blocking collectives  25.1 us (40%)
  Pallas kernels  17.2 us (27%)
  waiting for transfers between devices  13.6 us (22%)
  starting transfers between devices  4.41 us (7%)
  other arithmetic  1.39 us (2%)
  between operations  0.64 us (1%)
    all_to_all x1, blocking collectives, on_device(): received = lax.all_to_all(parts, 'tm', 0, 0, tiled=True)  25.1 us
    ppermute x5, waiting for transfers between devices, exchange_sum(): lax.ppermute(value, axis, [(i, i ^ step) for i in range(devices)])  13.6 us
    pallas_call x1, Pallas kernels, block_sums(): pl.pallas_call(body, grid=(shards,), in_specs=[pl.BlockSpec(memory_space=...  10.5 us
    ppermute x5, starting transfers between devices, exchange_sum(): lax.ppermute(value, axis, [(i, i ^ step) for i in range(devices)])  4.41 us
    pallas_call x1, Pallas kernels, whiten(): pl.pallas_call(body, out_shape=(jax.ShapeDtypeStruct((NF, size, size), jn...  4.26 us
    pallas_call x1, Pallas kernels, join_and_gram(): pl.pallas_call(body, out_shape=(jax.ShapeDtypeStruct((total, width), jnp....  2.39 us
    add x5, other arithmetic, exchange_sum(): value + lax.ppermute(value, axis, [(i, i ^ step) for i in range(devices)])  1.39 us
  transfers between devices with their start and end apart: 5, of which 5 were waited for; matrix products, arithmetic and copies ran while one was open for 0% of the time, Pallas kernels for 0%

profile of v1, /device:TPU:0, one launch (start us, length us, event | category | flops | bytes accessed | tf_op | source)
XLA Modules:
  0.0 62.3 jit_solution(12802953467646078006)
XLA Ops:
  0.6 10.5 %block_sums.1 = bf16[8,16,2560]{2,1,0:T(8,128)(2,1)} custom-call(s32[2]{0:T(128)} %freq_ref.1, bf16[512,16384]{1,0:T(8,128)(2,1)} %data_ref.1), custom_call_target="tpu_custom_call" | custom-call | tf_op jit(solution)/shard_map/block_sums/pallas_call | solution.py:67
  11.1 25.1 %all_to_all.5.data_ref = bf16[8,16,2560]{2,1,0:T(8,128)(2,1)} all-to-all(bf16[8,16,2560]{2,1,0:T(8,128)(2,1)} %block_sums.1), channel_id=1, replica_groups=mesh['space'=4,'tm'=8] {'tm'}, dimensions={0} | all-to-all | bytes 1310720 | tf_op jit(solution)/shard_map/all_to_all | solution.py:266
  36.2 2.4 %join_and_gram.1 = (bf16[128,2048]{1,0:T(8,128)(2,1)}, f32[64,128]{1,0:T(8,128)}) custom-call(bf16[4,128,256]{2,1,0:T(8,128)(2,1)} %constant.2.clone.join_ref, bf16[8,16,2560]{2,1,0:T(8,128)(2,1)} %all_to_all.5.data_ref), custom_call_target="tpu_custom_call" | custom-call | tf_op jit(solution)/shard_map/join_and_gram/pallas_call | solution.py:119
  38.6 0.0 collective-permute-start
  38.6 1.4 %collective-permute-done = f32[64,128]{1,0:T(8,128)S(1)} collective-permute-done((f32[64,128]{1,0:T(8,128)}, f32[64,128]{1,0:T(8,128)S(1)}, u32[]{:S(2)}, u32[]{:S(2)}) %collective-permute-start) | collective-permute-done | bytes 32800 | tf_op jit(solution)/shard_map/ppermute | solution.py:133
  40.0 0.8 %add.15 = f32[64,128]{1,0:T(8,128)S(1)} add(f32[64,128]{1,0:T(8,128)} %get-tuple-element.4, f32[64,128]{1,0:T(8,128)S(1)} %collective-permute-done) | non-fusion elementwise | flops 8192 | bytes 98304 | tf_op jit(solution)/shard_map/add | solution.py:133
  40.8 1.5 %collective-permute-start.1 = (f32[64,128]{1,0:T(8,128)S(1)}, f32[64,128]{1,0:T(8,128)S(1)}, u32[]{:S(2)}, u32[]{:S(2)}) collective-permute-start(f32[64,128]{1,0:T(8,128)S(1)} %add.15), channel_id=1, source_target_pairs={{0,16},{8,24},{16,0},{24,8},{1,17},{9,25},{17,1},{25,9},{2,18},{10... | collective-permute-start | bytes 98312 | tf_op jit(solution)/shard_map/ppermute | solution.py:133
  42.3 2.4 %collective-permute-done.1 = f32[64,128]{1,0:T(8,128)S(1)} collective-permute-done((f32[64,128]{1,0:T(8,128)S(1)}, f32[64,128]{1,0:T(8,128)S(1)}, u32[]{:S(2)}, u32[]{:S(2)}) %collective-permute-start.1) | collective-permute-done | bytes 32800 | tf_op jit(solution)/shard_map/ppermute | solution.py:133
  44.7 1.1 %collective-permute-start.2 = (f32[64,128]{1,0:T(8,128)S(1)}, f32[64,128]{1,0:T(8,128)S(1)}, u32[]{:S(2)}, u32[]{:S(2)}) collective-permute-start(f32[64,128]{1,0:T(8,128)S(1)} %add.16), channel_id=1, source_target_pairs={{0,1},{1,0},{2,3},{3,2},{4,5},{5,4},{6,7},{7,6},{8,9},{9,8},{10,11... | collective-permute-start | bytes 98312 | tf_op jit(solution)/shard_map/ppermute | solution.py:133
  45.8 2.8 %collective-permute-done.2 = f32[64,128]{1,0:T(8,128)S(1)} collective-permute-done((f32[64,128]{1,0:T(8,128)S(1)}, f32[64,128]{1,0:T(8,128)S(1)}, u32[]{:S(2)}, u32[]{:S(2)}) %collective-permute-start.2) | collective-permute-done | bytes 32800 | tf_op jit(solution)/shard_map/ppermute | solution.py:133
  48.6 0.9 %collective-permute-start.3 = (f32[64,128]{1,0:T(8,128)S(1)}, f32[64,128]{1,0:T(8,128)S(1)}, u32[]{:S(2)}, u32[]{:S(2)}) collective-permute-start(f32[64,128]{1,0:T(8,128)S(1)} %add.17), channel_id=1, source_target_pairs={{0,2},{1,3},{2,0},{3,1},{4,6},{5,7},{6,4},{7,5},{8,10},{9,11},{10,... | collective-permute-start | bytes 98312 | tf_op jit(solution)/shard_map/ppermute | solution.py:133
  49.6 3.0 %collective-permute-done.3 = f32[64,128]{1,0:T(8,128)S(1)} collective-permute-done((f32[64,128]{1,0:T(8,128)S(1)}, f32[64,128]{1,0:T(8,128)S(1)}, u32[]{:S(2)}, u32[]{:S(2)}) %collective-permute-start.3) | collective-permute-done | bytes 32800 | tf_op jit(solution)/shard_map/ppermute | solution.py:133
  52.6 0.9 %collective-permute-start.4 = (f32[64,128]{1,0:T(8,128)S(1)}, f32[64,128]{1,0:T(8,128)S(1)}, u32[]{:S(2)}, u32[]{:S(2)}) collective-permute-start(f32[64,128]{1,0:T(8,128)S(1)} %add.18), channel_id=1, source_target_pairs={{0,4},{1,5},{2,6},{3,7},{4,0},{5,1},{6,2},{7,3},{8,12},{9,13},{10,... | collective-permute-start | bytes 98312 | tf_op jit(solution)/shard_map/ppermute | solution.py:133
  53.5 3.9 %collective-permute-done.4 = f32[64,128]{1,0:T(8,128)S(1)} collective-permute-done((f32[64,128]{1,0:T(8,128)S(1)}, f32[64,128]{1,0:T(8,128)S(1)}, u32[]{:S(2)}, u32[]{:S(2)}) %collective-permute-start.4) | collective-permute-done | bytes 32800 | tf_op jit(solution)/shard_map/ppermute | solution.py:133
  57.4 0.6 add.19.gram_ref
  58.0 4.3 %whiten.1 = (f32[2,64,64]{2,1,0:T(8,128)}, f32[2,64,2048]{2,1,0:T(8,128)}) custom-call(f32[64,128]{1,0:T(8,128)} %add.19.gram_ref, bf16[128,2048]{1,0:T(8,128)(2,1)} %get-tuple-element.5.columns_ref), custom_call_target="tpu_custom_call" | custom-call | tf_op jit(solution)/shard_map/whiten/pallas_call | solution.py:246
  (3 shorter events, 0.0 us)
Async XLA Ops:
  38.6 1.4 %collective-permute-start = (f32[64,128]{1,0:T(8,128)}, f32[64,128]{1,0:T(8,128)S(1)}, u32[]{:S(2)}, u32[]{:S(2)}) collective-permute-start(f32[64,128]{1,0:T(8,128)} %get-tuple-element.4), channel_id=1, source_target_pairs={{0,8},{8,0},{16,24},{24,16},{1,9},{9,1},{17,25},{25,17},{2,10},{10... | collective-permute-start | bytes 98312 | tf_op jit(solution)/shard_map/ppermute | solution.py:133
  40.8 3.9 %collective-permute-start.1 = (f32[64,128]{1,0:T(8,128)S(1)}, f32[64,128]{1,0:T(8,128)S(1)}, u32[]{:S(2)}, u32[]{:S(2)}) collective-permute-start(f32[64,128]{1,0:T(8,128)S(1)} %add.15), channel_id=1, source_target_pairs={{0,16},{8,24},{16,0},{24,8},{1,17},{9,25},{17,1},{25,9},{2,18},{10... | collective-permute-start | bytes 98312 | tf_op jit(solution)/shard_map/ppermute | solution.py:133
  44.7 3.9 %collective-permute-start.2 = (f32[64,128]{1,0:T(8,128)S(1)}, f32[64,128]{1,0:T(8,128)S(1)}, u32[]{:S(2)}, u32[]{:S(2)}) collective-permute-start(f32[64,128]{1,0:T(8,128)S(1)} %add.16), channel_id=1, source_target_pairs={{0,1},{1,0},{2,3},{3,2},{4,5},{5,4},{6,7},{7,6},{8,9},{9,8},{10,11... | collective-permute-start | bytes 98312 | tf_op jit(solution)/shard_map/ppermute | solution.py:133
  48.6 3.9 %collective-permute-start.3 = (f32[64,128]{1,0:T(8,128)S(1)}, f32[64,128]{1,0:T(8,128)S(1)}, u32[]{:S(2)}, u32[]{:S(2)}) collective-permute-start(f32[64,128]{1,0:T(8,128)S(1)} %add.17), channel_id=1, source_target_pairs={{0,2},{1,3},{2,0},{3,1},{4,6},{5,7},{6,4},{7,5},{8,10},{9,11},{10,... | collective-permute-start | bytes 98312 | tf_op jit(solution)/shard_map/ppermute | solution.py:133
  52.6 4.8 %collective-permute-start.4 = (f32[64,128]{1,0:T(8,128)S(1)}, f32[64,128]{1,0:T(8,128)S(1)}, u32[]{:S(2)}, u32[]{:S(2)}) collective-permute-start(f32[64,128]{1,0:T(8,128)S(1)} %add.18), channel_id=1, source_target_pairs={{0,4},{1,5},{2,6},{3,7},{4,0},{5,1},{6,2},{7,3},{8,12},{9,13},{10,... | collective-permute-start | bytes 98312 | tf_op jit(solution)/shard_map/ppermute | solution.py:133

commit v2 on v1

--- a/solution.py
+++ b/solution.py
@@ -43,69 +43,95 @@
     return jnp.where(used, value, 0.0).astype(jnp.bfloat16)
 
 
-def block_sums(freq_bins, snapshots, shards):
+def block_sums(freq_bins, position, snapshots, shards, shifts):
     samples, points = snapshots.shape
     half_count = samples // HOP
     rows = SERIES * half_count
     width = points // shards
     fold = width // half_count
     table_rows = rows + SUB * 2
-
-    def body(freq_ref, data_ref, out_ref, table_ref):
-        @pl.when(pl.program_id(0) == 0)
-        def _():
-            table_ref[...] = fill_table(freq_ref, table_ref.shape, half_count)
-
-        sums = jnp.dot(table_ref[...], data_ref[...], preferred_element_type=jnp.float32)
-        out_ref[0, :, :width] = sums[:rows].astype(jnp.bfloat16)
-        early = sums[rows : rows + SERIES]
-        folded = jnp.concatenate(
-            [early[:, k * fold : (k + 1) * fold] for k in range(half_count)], axis=0
-        )
-        out_ref[0, :, width:] = folded.astype(jnp.bfloat16)
+    count = len(shifts)
+
+    def body(freq_ref, position_ref, data_ref, *refs):
+        outs, (join_ref, table_ref, buffer_ref, sems) = refs[:count], refs[count:]
+        copies = []
+        for i, shift in enumerate(shifts):
+            target = (position_ref[0] + shift) % shards
+            first = pl.multiple_of(target * width, width)
+            copies.append(
+                pltpu.make_async_copy(
+                    data_ref.at[:, pl.ds(first, width)], buffer_ref.at[i], sems.at[i]
+                )
+            )
+            copies[-1].start()
+        table_ref[...] = fill_table(freq_ref, table_ref.shape, half_count)
+        for k in range(half_count):
+            join_ref[k] = join_matrix(position_ref[0], shifts, k, half_count)
+        for copy, out_ref, i in zip(copies, outs, range(count)):
+            copy.wait()
+            sums = jnp.dot(table_ref[...], buffer_ref[i], preferred_element_type=jnp.float32)
+            out_ref[:, :width] = sums[:rows].astype(jnp.bfloat16)
+            early = sums[rows : rows + SERIES]
+            folded = jnp.concatenate(
+                [early[:, k * fold : (k + 1) * fold] for k in range(half_count)], axis=0
+            )
+            out_ref[:, width:] = folded.astype(jnp.bfloat16)
 
     return pl.pallas_call(
         body,
-        grid=(shards,),
         in_specs=[
             pl.BlockSpec(memory_space=pltpu.SMEM),
-            pl.BlockSpec((samples, width), lambda d: (0, d)),
+            pl.BlockSpec(memory_space=pltpu.SMEM),
+            pl.BlockSpec(memory_space=pl.ANY),
         ],
-        out_specs=pl.BlockSpec((1, rows, width + fold), lambda d: (d, 0, 0)),
-        out_shape=jax.ShapeDtypeStruct((shards, rows, width + fold), jnp.bfloat16),
-        scratch_shapes=[pltpu.VMEM((table_rows, samples), jnp.bfloat16)],
+        out_shape=tuple(pltpu.VMEM((rows, width + fold), jnp.bfloat16) for _ in shifts)
+        + (pltpu.VMEM((half_count, rows * shards, 2 * rows * shards), jnp.bfloat16),),
+        out_specs=tuple([pl.BlockSpec(memory_space=pltpu.VMEM)] * (count + 1)),
+        scratch_shapes=[
+            pltpu.VMEM((table_rows, samples), jnp.bfloat16),
+            pltpu.VMEM((count, samples, width), jnp.bfloat16),
+            pltpu.SemaphoreType.DMA((count,)),
+        ],
         name="block_sums",
-    )(freq_bins, snapshots)
-
-
-def join_matrix(shards, half_count):
+    )(freq_bins, position, snapshots)
+
+
+def join_matrix(position, shifts, k, half_count):
+    shards = len(shifts)
     rows = SERIES * half_count
-    block_count = shards * half_count
-    out = np.zeros((half_count, SERIES * block_count, 2 * shards * rows), np.float32)
-    for k in range(half_count):
-        for series in range(SERIES):
-            for shard in range(shards):
-                for j in range(half_count):
-                    target = series * block_count + shard * half_count + j
-                    out[k, target, shard * rows + j * SERIES + series] = 1.0
-                    if j == half_count - 1:
-                        after = (shard + 1) % shards
-                        out[k, target, (shards + after) * rows + k * SERIES + series] = 1.0
-    return jnp.asarray(out, jnp.bfloat16)
-
-
-def join_and_gram(received, half_count, grid_total):
-    shards, rows, span = received.shape
+    total = shards * rows
+    target = lax.broadcasted_iota(jnp.int32, (total, 1), 0)
+    series = target // (shards * half_count)
+    shard = target // half_count % shards
+    block = target % half_count
+    source = lax.broadcasted_iota(jnp.int32, (1, 2 * total), 1)
+    slot, row = source // rows % shards, source % rows
+    sender = jnp.zeros_like(source)
+    for i, shift in enumerate(shifts):
+        sender = jnp.where(slot == i, (position - shift + shards) % shards, sender)
+    folded = source >= total
+    code = jnp.where(folded, total, 0) + sender * rows + row
+    own = shard * rows + block * SERIES + series
+    after = (shard + 1) % shards
+    early = total + after * rows + k * SERIES + series
+    early = jnp.where(block == half_count - 1, early, -1)
+    return jnp.where((code == own) | (code == early), 1.0, 0.0).astype(jnp.bfloat16)
+
+
+def join_and_gram(received, joins, half_count, grid_total):
+    shards = len(received)
+    rows, span = received[0].shape
     width = span * half_count // (half_count + 1)
     fold = width // half_count
     total = shards * rows
     size = total // NF
 
-    def body(join_ref, data_ref, columns_ref, gram_ref):
-        folded = data_ref[:, :, width:].reshape(total, fold)
+    def body(join_ref, *refs):
+        parts, (columns_ref, gram_ref) = refs[:shards], refs[shards:]
+        folded = [part[:, width:] for part in parts]
         for k in range(half_count):
-            own = data_ref[:, :, k * fold : (k + 1) * fold].reshape(total, fold)
-            both = jnp.concatenate([own, folded], axis=0)
+            own = [part[:, k * fold : (k + 1) * fold] for part in parts]
+            both = jnp.concatenate(own + folded, axis=0)
             joined = jnp.dot(join_ref[k], both, preferred_element_type=jnp.float32)
             columns_ref[:, k * fold : (k + 1) * fold] = joined.astype(jnp.bfloat16)
         columns = columns_ref[...]
@@ -118,21 +144,54 @@
 
     return pl.pallas_call(
         body,
+        in_specs=[pl.BlockSpec(memory_space=pltpu.VMEM)] * (shards + 1),
         out_shape=(
-            jax.ShapeDtypeStruct((total, width), jnp.bfloat16),
-            jax.ShapeDtypeStruct((size, NF * size), jnp.float32),
+            pltpu.VMEM((total, width), jnp.bfloat16),
+            pltpu.VMEM((size, NF * size), jnp.float32),
         ),
+        out_specs=(pl.BlockSpec(memory_space=pltpu.VMEM),) * 2,
         name="join_and_gram",
-    )(join_matrix(shards, half_count), received)
-
-
-def exchange_sum(value, axis):
-    devices = lax.axis_size(axis)
-    step = 1
-    while step < devices:
-        value = value + lax.ppermute(value, axis, [(i, i ^ step) for i in range(devices)])
-        step *= 2
-    return value
+    )(near(joins), *[near(part) for part in received])
+
+
+def near(value):
+    return pltpu.with_memory_space_constraint(value, pltpu.VMEM)
+
+
+GRID = ("space", "tm")
+
+
+def swapped(value, flips):
+    wide, long = (lax.axis_size(name) for name in GRID)
+    pairs = [
+        (i * long + j, (i ^ flips[0]) * long + (j ^ flips[1]))
+        for i in range(wide)
+        for j in range(long)
+    ]
+    return lax.ppermute(value, GRID, pairs)
+
+
+def exchange_rounds():
+    bits = [(1 << k, 0) for k in range((lax.axis_size("space") - 1).bit_length())]
+    bits += [(0, 1 << k) for k in range((lax.axis_size("tm") - 1).bit_length())]
+    rounds, rest = [bits[:1]], bits[1:]
+    while rest:
+        rounds.append(rest[:2])
+        rest = rest[2:]
+    return rounds
+
+
+def peers_of(value, bits):
+    if len(bits) == 1:
+        return [swapped(value, bits[0])]
+    (a, b), (c, d) = bits
+    return [swapped(value, flips) for flips in ((a, b), (c, d), (a + c, b + d))]
+
+
+def add_up(values):
+    while len(values) > 1:
+        values = [values[i] + values[i + 1] for i in range(0, len(values), 2)]
+    return values[0]
 
 
 def inverse_factor(gram_ref, work_ref, inverse_ref, size):
@@ -220,12 +279,15 @@
                 inverse_ref[first : first + SUB, :] = rest_side
 
 
-def whiten(gram, columns):
-    size = gram.shape[0]
+def whiten(grams, columns):
+    count = len(grams)
+    size = grams[0].shape[0]
     total, width = columns.shape
     chunk = min(width, 512)
 
-    def body(gram_ref, columns_ref, gram_out, white_ref, work_ref, inverse_ref, left_ref):
+    def body(*refs):
+        columns_ref, gram_out, white_ref, gram_ref, work_ref, inverse_ref, left_ref = refs[count:]
+        gram_ref[...] = add_up([ref[...] for ref in refs[:count]])
         for f in range(NF):
             gram_out[f] = gram_ref[:, f * size : (f + 1) * size]
         inverse_factor(gram_ref, work_ref, inverse_ref, size)
@@ -245,6 +307,7 @@
 
     return pl.pallas_call(
         body,
+        in_specs=[pl.BlockSpec(memory_space=pltpu.VMEM)] * (count + 1),
         out_shape=(
             jax.ShapeDtypeStruct((NF, size, size), jnp.float32),
             jax.ShapeDtypeStruct((NF, size, width), jnp.float32),
@@ -252,21 +315,30 @@
         scratch_shapes=[
             pltpu.VMEM((size, NF * size), jnp.float32),
             pltpu.VMEM((size, NF * size), jnp.float32),
+            pltpu.VMEM((size, NF * size), jnp.float32),
             pltpu.VMEM((total, 2 * NF * size), jnp.bfloat16),
         ],
         name="whiten",
-    )(gram, columns)
+    )(*[near(gram) for gram in grams], near(columns))
 
 
 def on_device(snapshots, freq_bins):
     shards = lax.axis_size("tm")
     half_count = snapshots.shape[0] // HOP
     grid_total = snapshots.shape[1] * lax.axis_size("space")
-    parts = block_sums(freq_bins, snapshots, shards)
-    received = lax.all_to_all(parts, "tm", 0, 0, tiled=True)
-    columns, gram = join_and_gram(received, half_count, grid_total)
-    gram = exchange_sum(exchange_sum(gram, "space"), "tm")
-    return whiten(gram, columns)
+    position = lax.axis_index("tm").astype(jnp.int32)[None]
+    shifts = sorted(range(shards), key=lambda k: abs(k - shards // 2))
+    *parts, joins = block_sums(freq_bins, position, snapshots, shards, shifts)
+    received = []
+    for shift, part in zip(shifts, parts):
+        pairs = [(i, (i + shift) % shards) for i in range(shards)]
+        received.append(lax.ppermute(part, "tm", pairs) if shift else part)
+    columns, gram = join_and_gram(received, joins, half_count, grid_total)
+    grams = [gram]
+    for bits in exchange_rounds():
+        gram = add_up(grams)
+        grams = [gram] + peers_of(gram, bits)
+    return whiten(grams, columns)
 
 
 def solution(mesh):

time: 62.6 us -> 49.1 us (0.78)
  blocking collectives: 25.1 us -> 0 us
  starting transfers between devices: 4.41 us -> 25 us
  Pallas kernels: 17.2 us -> 10.9 us
  other arithmetic: 1.39 us -> 0.01 us
  waiting for transfers between devices: 13.6 us -> 12.5 us
    all_to_all x1 -> x0, blocking collectives: 25.1 us -> none  [on_device(): received = lax.all_to_all(parts, 'tm', 0, 0, tiled=True)]
    ppermute x5 -> x14, starting transfers between devices: 4.41 us -> 25 us  [the longest x7 16.3 us: on_device(): received.append(lax.ppermute(part, 'tm', pairs) if shift else part)]
    pallas_call x3, Pallas kernels: 17.2 us -> 10.9 us  [the longest x1 7.1 us: block_sums(): pl.pallas_call(body, in_specs=[pl.BlockSpec(memory_space=pltpu.SMEM), pl....]
    add x5 -> x2, other arithmetic: 1.39 us -> 0.01 us  [add_up(): values = [values[i] + values[i + 1] for i in range(0, len(values), 2)]]
    ppermute x5 -> x14, waiting for transfers between devices: 13.6 us -> 12.5 us  [the longest x7 8.74 us: swapped(): return lax.ppermute(value, GRID, pairs)]
  transfers between devices with their start and end apart: 5 -> 14, of which waited for: 5 -> 9; matrix products, arithmetic and copies ran while one was open for 0% -> 0% of each run, Pallas kernels for 0% -> 0%
where the time goes in v2:
time: 49.1 us; the launch traced here: 49 us
  starting transfers between devices  25 us (51%)
  waiting for transfers between devices  12.5 us (25%)
  Pallas kernels  10.9 us (22%)
  between operations  0.68 us (1%)
    ppermute x7, starting transfers between devices, on_device(): received.append(lax.ppermute(part, 'tm', pairs) if shift else part)  16.3 us
    ppermute x7, waiting for transfers between devices, swapped(): return lax.ppermute(value, GRID, pairs)  8.74 us
    ppermute x7, starting transfers between devices, swapped(): return lax.ppermute(value, GRID, pairs)  8.71 us
    pallas_call x1, Pallas kernels, block_sums(): pl.pallas_call(body, in_specs=[pl.BlockSpec(memory_space=pltpu.SMEM), pl....  7.1 us
    ppermute x7, waiting for transfers between devices, on_device(): received.append(lax.ppermute(part, 'tm', pairs) if shift else part)  3.72 us
    pallas_call x1, Pallas kernels, whiten(): pl.pallas_call(body, in_specs=[pl.BlockSpec(memory_space=pltpu.VMEM)] * (...  3.19 us
  transfers between devices with their start and end apart: 14, of which 9 were waited for; matrix products, arithmetic and copies ran while one was open for 0% of the time, Pallas kernels for 0%

profile of v2, /device:TPU:0, one launch (start us, length us, event | category | flops | bytes accessed | tf_op | source)
XLA Modules:
  0.0 49.0 jit_solution(3855374269077579867)
XLA Ops:
  0.6 7.1 %block_sums.1 = (bf16[16,2560]{1,0:T(8,128)(2,1)S(1)}, bf16[16,2560]{1,0:T(8,128)(2,1)S(1)}, bf16[16,2560]{1,0:T(8,128)(2,1)S(1)}, bf16[16,2560]{1,0:T(8,128)(2,...) custom-call(s32[2]{0:T(128)} %freq_ref.1, ...), custom_call_target="tpu_custom_call" | custom-call | tf_op jit(solution)/shard_map/block_sums/pallas_call | solution.py:80
  7.7 4.1 %collective-permute-start = (bf16[16,2560]{1,0:T(8,128)(2,1)S(1)}, bf16[16,2560]{1,0:T(8,128)(2,1)S(1)}, u32[]{:S(2)}, u32[]{:S(2)}) collective-permute-start(bf16[16,2560]{1,0:T(8,128)(2,1)S(1)} %get-tuple-element.14), channel_id=1, source_target_pairs={{0,4},{1,5},{2,6},{3,7},{4,0},{5,1},{6,2},{7,3},{8,12},{9,13},{10,... | collective-permute-start | bytes 245768 | tf_op jit(solution)/shard_map/ppermute | solution.py:335
  11.9 2.5 %collective-permute-start.1 = (bf16[16,2560]{1,0:T(8,128)(2,1)S(1)}, bf16[16,2560]{1,0:T(8,128)(2,1)S(1)}, u32[]{:S(2)}, u32[]{:S(2)}) collective-permute-start(bf16[16,2560]{1,0:T(8,128)(2,1)S(1)} %get-tuple-element.15), channel_id=1, source_target_pairs={{0,3},{1,4},{2,5},{3,6},{4,7},{5,0},{6,1},{7,2},{8,11},{9,12},{10,... | collective-permute-start | bytes 245768 | tf_op jit(solution)/shard_map/ppermute | solution.py:335
  14.4 1.3 %collective-permute-start.2 = (bf16[16,2560]{1,0:T(8,128)(2,1)S(1)}, bf16[16,2560]{1,0:T(8,128)(2,1)S(1)}, u32[]{:S(2)}, u32[]{:S(2)}) collective-permute-start(bf16[16,2560]{1,0:T(8,128)(2,1)S(1)} %get-tuple-element.16), channel_id=1, source_target_pairs={{0,5},{1,6},{2,7},{3,0},{4,1},{5,2},{6,3},{7,4},{8,13},{9,14},{10,... | collective-permute-start | bytes 245768 | tf_op jit(solution)/shard_map/ppermute | solution.py:335
  15.7 1.6 %collective-permute-start.3 = (bf16[16,2560]{1,0:T(8,128)(2,1)S(1)}, bf16[16,2560]{1,0:T(8,128)(2,1)S(1)}, u32[]{:S(2)}, u32[]{:S(2)}) collective-permute-start(bf16[16,2560]{1,0:T(8,128)(2,1)S(1)} %get-tuple-element.17), channel_id=1, source_target_pairs={{0,2},{1,3},{2,4},{3,5},{4,6},{5,7},{6,0},{7,1},{8,10},{9,11},{10,... | collective-permute-start | bytes 245768 | tf_op jit(solution)/shard_map/ppermute | solution.py:335
  17.3 2.2 %collective-permute-start.4 = (bf16[16,2560]{1,0:T(8,128)(2,1)S(1)}, bf16[16,2560]{1,0:T(8,128)(2,1)S(1)}, u32[]{:S(2)}, u32[]{:S(2)}) collective-permute-start(bf16[16,2560]{1,0:T(8,128)(2,1)S(1)} %get-tuple-element.18), channel_id=1, source_target_pairs={{0,6},{1,7},{2,0},{3,1},{4,2},{5,3},{6,4},{7,5},{8,14},{9,15},{10,... | collective-permute-start | bytes 245768 | tf_op jit(solution)/shard_map/ppermute | solution.py:335
  19.5 0.0 collective-permute-done.refs_0_
  19.5 2.4 %collective-permute-start.5 = (bf16[16,2560]{1,0:T(8,128)(2,1)S(1)}, bf16[16,2560]{1,0:T(8,128)(2,1)S(1)}, u32[]{:S(2)}, u32[]{:S(2)}) collective-permute-start(bf16[16,2560]{1,0:T(8,128)(2,1)S(1)} %get-tuple-element.19), channel_id=1, source_target_pairs={{0,1},{1,2},{2,3},{3,4},{4,5},{5,6},{6,7},{7,0},{8,9},{9,10},{10,1... | collective-permute-start | bytes 245768 | tf_op jit(solution)/shard_map/ppermute | solution.py:335
  21.9 0.3 collective-permute-done.1.refs_1_
  22.2 2.1 %collective-permute-start.6 = (bf16[16,2560]{1,0:T(8,128)(2,1)S(1)}, bf16[16,2560]{1,0:T(8,128)(2,1)S(1)}, u32[]{:S(2)}, u32[]{:S(2)}) collective-permute-start(bf16[16,2560]{1,0:T(8,128)(2,1)S(1)} %get-tuple-element.20), channel_id=1, source_target_pairs={{0,7},{1,0},{2,1},{3,2},{4,3},{5,4},{6,5},{7,6},{8,15},{9,8},{10,9... | collective-permute-start | bytes 245768 | tf_op jit(solution)/shard_map/ppermute | solution.py:335
  24.3 0.0 collective-permute-done.2.refs_2_
  24.3 0.0 collective-permute-done.3.refs_3_
  24.3 0.0 collective-permute-done.4.refs_4_
  24.3 2.7 %collective-permute-done.5.refs_5_ = bf16[16,2560]{1,0:T(8,128)(2,1)S(1)} collective-permute-done((bf16[16,2560]{1,0:T(8,128)(2,1)S(1)}, bf16[16,2560]{1,0:T(8,128)(2,1)S(1)}, u32[]{:S(2)}, u32[]{:S(2)}) %collective-permute-start.5) | collective-permute-done | bytes 81952 | tf_op jit(solution)/shard_map/ppermute | solution.py:335
  26.9 0.8 %collective-permute-done.6.refs_6_ = bf16[16,2560]{1,0:T(8,128)(2,1)S(1)} collective-permute-done((bf16[16,2560]{1,0:T(8,128)(2,1)S(1)}, bf16[16,2560]{1,0:T(8,128)(2,1)S(1)}, u32[]{:S(2)}, u32[]{:S(2)}) %collective-permute-start.6) | collective-permute-done | bytes 81952 | tf_op jit(solution)/shard_map/ppermute | solution.py:335
  27.7 0.6 %join_and_gram.1 = (bf16[128,2048]{1,0:T(8,128)(2,1)S(1)}, f32[64,128]{1,0:T(8,128)S(1)}) custom-call(bf16[4,128,256]{2,1,0:T(8,128)(2,1)S(1)} %get-tuple-element.13.join_ref, bf16[16,2560]{1,0:T(8,128)(2,1)S(1)} %collective-permute-done.refs_0_, bf16[16,2560]{1,0:T(8,128)(2,1)S(1)} %collective-permute-done.1.refs_1_, ...), custom_call_target="tpu_custom_call" | custom-call | tf_op jit(solution)/shard_map/join_and_gram/pallas_call | solution.py:145
  28.3 0.1 collective-permute-start.7
  28.4 1.2 %collective-permute-done.7 = f32[64,128]{1,0:T(8,128)S(1)} collective-permute-done((f32[64,128]{1,0:T(8,128)S(1)}, f32[64,128]{1,0:T(8,128)S(1)}, u32[]{:S(2)}, u32[]{:S(2)}) %collective-permute-start.7) | collective-permute-done | bytes 32800 | tf_op jit(solution)/shard_map/ppermute | solution.py:171
  29.6 1.0 %collective-permute-start.10 = (f32[64,128]{1,0:T(8,128)S(1)}, f32[64,128]{1,0:T(8,128)S(1)}, u32[]{:S(2)}, u32[]{:S(2)}) collective-permute-start(f32[64,128]{1,0:T(8,128)S(1)} %add.12), channel_id=1, source_target_pairs={{0,17},{1,16},{2,19},{3,18},{4,21},{5,20},{6,23},{7,22},{8,25},{9,... | collective-permute-start | bytes 98312 | tf_op jit(solution)/shard_map/ppermute | solution.py:171
  30.6 1.9 %collective-permute-start.9 = (f32[64,128]{1,0:T(8,128)S(1)}, f32[64,128]{1,0:T(8,128)S(1)}, u32[]{:S(2)}, u32[]{:S(2)}) collective-permute-start(f32[64,128]{1,0:T(8,128)S(1)} %add.12), channel_id=1, source_target_pairs={{0,1},{1,0},{2,3},{3,2},{4,5},{5,4},{6,7},{7,6},{8,9},{9,8},{10,11... | collective-permute-start | bytes 98312 | tf_op jit(solution)/shard_map/ppermute | solution.py:171
  32.5 0.5 %collective-permute-start.8 = (f32[64,128]{1,0:T(8,128)S(1)}, f32[64,128]{1,0:T(8,128)S(1)}, u32[]{:S(2)}, u32[]{:S(2)}) collective-permute-start(f32[64,128]{1,0:T(8,128)S(1)} %add.12), channel_id=1, source_target_pairs={{0,16},{1,17},{2,18},{3,19},{4,20},{5,21},{6,22},{7,23},{8,24},{9,... | collective-permute-start | bytes 98312 | tf_op jit(solution)/shard_map/ppermute | solution.py:171
  33.1 1.3 %collective-permute-done.10 = f32[64,128]{1,0:T(8,128)S(1)} collective-permute-done((f32[64,128]{1,0:T(8,128)S(1)}, f32[64,128]{1,0:T(8,128)S(1)}, u32[]{:S(2)}, u32[]{:S(2)}) %collective-permute-start.10) | collective-permute-done | bytes 32800 | tf_op jit(solution)/shard_map/ppermute | solution.py:171
  34.4 0.4 collective-permute-done.9
  34.7 1.7 %collective-permute-done.8 = f32[64,128]{1,0:T(8,128)S(1)} collective-permute-done((f32[64,128]{1,0:T(8,128)S(1)}, f32[64,128]{1,0:T(8,128)S(1)}, u32[]{:S(2)}, u32[]{:S(2)}) %collective-permute-start.8) | collective-permute-done | bytes 32800 | tf_op jit(solution)/shard_map/ppermute | solution.py:171
  36.5 4.5 %collective-permute-start.13 = (f32[64,128]{1,0:T(8,128)S(1)}, f32[64,128]{1,0:T(8,128)S(1)}, u32[]{:S(2)}, u32[]{:S(2)}) collective-permute-start(f32[64,128]{1,0:T(8,128)S(1)} %add_add_fusion.refs_0_), channel_id=1, source_target_pairs={{0,6},{1,7},{2,4},{3,5},{4,2},{5,3},{6,0},{7,1},{8,14},{9,15},{10,... | collective-permute-start | bytes 98312 | tf_op jit(solution)/shard_map/ppermute | solution.py:171
  41.0 0.0 collective-permute-start.12
  41.0 0.6 %collective-permute-start.11 = (f32[64,128]{1,0:T(8,128)S(1)}, f32[64,128]{1,0:T(8,128)S(1)}, u32[]{:S(2)}, u32[]{:S(2)}) collective-permute-start(f32[64,128]{1,0:T(8,128)S(1)} %add_add_fusion.refs_0_), channel_id=1, source_target_pairs={{0,2},{1,3},{2,0},{3,1},{4,6},{5,7},{6,4},{7,5},{8,10},{9,11},{10,... | collective-permute-start | bytes 98312 | tf_op jit(solution)/shard_map/ppermute | solution.py:171
  41.6 1.3 %collective-permute-done.13.refs_3_ = f32[64,128]{1,0:T(8,128)S(1)} collective-permute-done((f32[64,128]{1,0:T(8,128)S(1)}, f32[64,128]{1,0:T(8,128)S(1)}, u32[]{:S(2)}, u32[]{:S(2)}) %collective-permute-start.13) | collective-permute-done | bytes 32800 | tf_op jit(solution)/shard_map/ppermute | solution.py:171
  42.9 2.9 %collective-permute-done.12.refs_2_ = f32[64,128]{1,0:T(8,128)S(1)} collective-permute-done((f32[64,128]{1,0:T(8,128)S(1)}, f32[64,128]{1,0:T(8,128)S(1)}, u32[]{:S(2)}, u32[]{:S(2)}) %collective-permute-start.12) | collective-permute-done | bytes 32800 | tf_op jit(solution)/shard_map/ppermute | solution.py:171
  45.8 0.0 collective-permute-done.11.refs_1_
  45.8 3.2 %whiten.1 = (f32[2,64,64]{2,1,0:T(8,128)}, f32[2,64,2048]{2,1,0:T(8,128)}) custom-call(f32[64,128]{1,0:T(8,128)S(1)} %add_add_fusion.refs_0_, f32[64,128]{1,0:T(8,128)S(1)} %collective-permute-done.11.refs_1_, f32[64,128]{1,0:T(8,128)S(1)} %collective-permute-done.12.refs_2_, f32[64,128]{1,0:T(8,128)S(1)} %collective-permute-done.13.refs_3_, ...), custom_call_target="tpu_custom_call" | custom-call | tf_op jit(solution)/shard_map/whiten/pallas_call | solution.py:308
  (2 shorter events, 0.0 us)
Async XLA Ops:
  7.7 11.8 %collective-permute-start = (bf16[16,2560]{1,0:T(8,128)(2,1)S(1)}, bf16[16,2560]{1,0:T(8,128)(2,1)S(1)}, u32[]{:S(2)}, u32[]{:S(2)}) collective-permute-start(bf16[16,2560]{1,0:T(8,128)(2,1)S(1)} %get-tuple-element.14), channel_id=1, source_target_pairs={{0,4},{1,5},{2,6},{3,7},{4,0},{5,1},{6,2},{7,3},{8,12},{9,13},{10,... | collective-permute-start | bytes 245768 | tf_op jit(solution)/shard_map/ppermute | solution.py:335
  11.9 10.3 %collective-permute-start.1 = (bf16[16,2560]{1,0:T(8,128)(2,1)S(1)}, bf16[16,2560]{1,0:T(8,128)(2,1)S(1)}, u32[]{:S(2)}, u32[]{:S(2)}) collective-permute-start(bf16[16,2560]{1,0:T(8,128)(2,1)S(1)} %get-tuple-element.15), channel_id=1, source_target_pairs={{0,3},{1,4},{2,5},{3,6},{4,7},{5,0},{6,1},{7,2},{8,11},{9,12},{10,... | collective-permute-start | bytes 245768 | tf_op jit(solution)/shard_map/ppermute | solution.py:335
  14.4 9.9 %collective-permute-start.2 = (bf16[16,2560]{1,0:T(8,128)(2,1)S(1)}, bf16[16,2560]{1,0:T(8,128)(2,1)S(1)}, u32[]{:S(2)}, u32[]{:S(2)}) collective-permute-start(bf16[16,2560]{1,0:T(8,128)(2,1)S(1)} %get-tuple-element.16), channel_id=1, source_target_pairs={{0,5},{1,6},{2,7},{3,0},{4,1},{5,2},{6,3},{7,4},{8,13},{9,14},{10,... | collective-permute-start | bytes 245768 | tf_op jit(solution)/shard_map/ppermute | solution.py:335
  15.7 8.6 %collective-permute-start.3 = (bf16[16,2560]{1,0:T(8,128)(2,1)S(1)}, bf16[16,2560]{1,0:T(8,128)(2,1)S(1)}, u32[]{:S(2)}, u32[]{:S(2)}) collective-permute-start(bf16[16,2560]{1,0:T(8,128)(2,1)S(1)} %get-tuple-element.17), channel_id=1, source_target_pairs={{0,2},{1,3},{2,4},{3,5},{4,6},{5,7},{6,0},{7,1},{8,10},{9,11},{10,... | collective-permute-start | bytes 245768 | tf_op jit(solution)/shard_map/ppermute | solution.py:335
  17.3 7.0 %collective-permute-start.4 = (bf16[16,2560]{1,0:T(8,128)(2,1)S(1)}, bf16[16,2560]{1,0:T(8,128)(2,1)S(1)}, u32[]{:S(2)}, u32[]{:S(2)}) collective-permute-start(bf16[16,2560]{1,0:T(8,128)(2,1)S(1)} %get-tuple-element.18), channel_id=1, source_target_pairs={{0,6},{1,7},{2,0},{3,1},{4,2},{5,3},{6,4},{7,5},{8,14},{9,15},{10,... | collective-permute-start | bytes 245768 | tf_op jit(solution)/shard_map/ppermute | solution.py:335
  19.5 7.4 %collective-permute-start.5 = (bf16[16,2560]{1,0:T(8,128)(2,1)S(1)}, bf16[16,2560]{1,0:T(8,128)(2,1)S(1)}, u32[]{:S(2)}, u32[]{:S(2)}) collective-permute-start(bf16[16,2560]{1,0:T(8,128)(2,1)S(1)} %get-tuple-element.19), channel_id=1, source_target_pairs={{0,1},{1,2},{2,3},{3,4},{4,5},{5,6},{6,7},{7,0},{8,9},{9,10},{10,1... | collective-permute-start | bytes 245768 | tf_op jit(solution)/shard_map/ppermute | solution.py:335
  22.2 5.5 %collective-permute-start.6 = (bf16[16,2560]{1,0:T(8,128)(2,1)S(1)}, bf16[16,2560]{1,0:T(8,128)(2,1)S(1)}, u32[]{:S(2)}, u32[]{:S(2)}) collective-permute-start(bf16[16,2560]{1,0:T(8,128)(2,1)S(1)} %get-tuple-element.20), channel_id=1, source_target_pairs={{0,7},{1,0},{2,1},{3,2},{4,3},{5,4},{6,5},{7,6},{8,15},{9,8},{10,9... | collective-permute-start | bytes 245768 | tf_op jit(solution)/shard_map/ppermute | solution.py:335
  28.3 1.3 %collective-permute-start.7 = (f32[64,128]{1,0:T(8,128)S(1)}, f32[64,128]{1,0:T(8,128)S(1)}, u32[]{:S(2)}, u32[]{:S(2)}) collective-permute-start(f32[64,128]{1,0:T(8,128)S(1)} %get-tuple-element.22), channel_id=1, source_target_pairs={{0,8},{1,9},{2,10},{3,11},{4,12},{5,13},{6,14},{7,15},{8,0},{9,1},... | collective-permute-start | bytes 98312 | tf_op jit(solution)/shard_map/ppermute | solution.py:171
  29.6 4.8 %collective-permute-start.10 = (f32[64,128]{1,0:T(8,128)S(1)}, f32[64,128]{1,0:T(8,128)S(1)}, u32[]{:S(2)}, u32[]{:S(2)}) collective-permute-start(f32[64,128]{1,0:T(8,128)S(1)} %add.12), channel_id=1, source_target_pairs={{0,17},{1,16},{2,19},{3,18},{4,21},{5,20},{6,23},{7,22},{8,25},{9,... | collective-permute-start | bytes 98312 | tf_op jit(solution)/shard_map/ppermute | solution.py:171
  30.6 4.1 %collective-permute-start.9 = (f32[64,128]{1,0:T(8,128)S(1)}, f32[64,128]{1,0:T(8,128)S(1)}, u32[]{:S(2)}, u32[]{:S(2)}) collective-permute-start(f32[64,128]{1,0:T(8,128)S(1)} %add.12), channel_id=1, source_target_pairs={{0,1},{1,0},{2,3},{3,2},{4,5},{5,4},{6,7},{7,6},{8,9},{9,8},{10,11... | collective-permute-start | bytes 98312 | tf_op jit(solution)/shard_map/ppermute | solution.py:171
  32.5 3.9 %collective-permute-start.8 = (f32[64,128]{1,0:T(8,128)S(1)}, f32[64,128]{1,0:T(8,128)S(1)}, u32[]{:S(2)}, u32[]{:S(2)}) collective-permute-start(f32[64,128]{1,0:T(8,128)S(1)} %add.12), channel_id=1, source_target_pairs={{0,16},{1,17},{2,18},{3,19},{4,20},{5,21},{6,22},{7,23},{8,24},{9,... | collective-permute-start | bytes 98312 | tf_op jit(solution)/shard_map/ppermute | solution.py:171
  36.5 6.4 %collective-permute-start.13 = (f32[64,128]{1,0:T(8,128)S(1)}, f32[64,128]{1,0:T(8,128)S(1)}, u32[]{:S(2)}, u32[]{:S(2)}) collective-permute-start(f32[64,128]{1,0:T(8,128)S(1)} %add_add_fusion.refs_0_), channel_id=1, source_target_pairs={{0,6},{1,7},{2,4},{3,5},{4,2},{5,3},{6,0},{7,1},{8,14},{9,15},{10,... | collective-permute-start | bytes 98312 | tf_op jit(solution)/shard_map/ppermute | solution.py:171
  41.0 4.8 %collective-permute-start.12 = (f32[64,128]{1,0:T(8,128)S(1)}, f32[64,128]{1,0:T(8,128)S(1)}, u32[]{:S(2)}, u32[]{:S(2)}) collective-permute-start(f32[64,128]{1,0:T(8,128)S(1)} %add_add_fusion.refs_0_), channel_id=1, source_target_pairs={{0,4},{1,5},{2,6},{3,7},{4,0},{5,1},{6,2},{7,3},{8,12},{9,13},{10,... | collective-permute-start | bytes 98312 | tf_op jit(solution)/shard_map/ppermute | solution.py:171
  41.0 4.8 %collective-permute-start.11 = (f32[64,128]{1,0:T(8,128)S(1)}, f32[64,128]{1,0:T(8,128)S(1)}, u32[]{:S(2)}, u32[]{:S(2)}) collective-permute-start(f32[64,128]{1,0:T(8,128)S(1)} %add_add_fusion.refs_0_), channel_id=1, source_target_pairs={{0,2},{1,3},{2,0},{3,1},{4,6},{5,7},{6,4},{7,5},{8,10},{9,11},{10,... | collective-permute-start | bytes 98312 | tf_op jit(solution)/shard_map/ppermute | solution.py:171

commit v3 on v2

v3 whole, which is shorter than its diff:
```python
import math

import jax
import jax.numpy as jnp
import numpy as np
from jax import lax
from jax.experimental import pallas as pl
from jax.experimental.pallas import tpu as pltpu
from jax.sharding import PartitionSpec as P

NFFT = 256
HOP = 128
NF = 2
SERIES = 2 * NF
SUB = 8

ridge_term = 0.01


def window_norm():
    sample = np.arange(NFFT, dtype=np.float64)
    taper = 0.5 - 0.5 * np.cos(2.0 * np.pi * sample / NFFT)
    return float(np.sqrt(np.sum(taper * taper)))


def fill_table(freq_ref, table_ref, half_count):
    row = lax.broadcasted_iota(jnp.int32, (SUB, NFFT), 0)
    sample = lax.broadcasted_iota(jnp.int32, (SUB, NFFT), 1)
    series = row % SERIES
    bins = jnp.where(series // 2 == 0, freq_ref[0], freq_ref[1])
    phase = (bins * sample + jnp.where(series % 2 == 1, NFFT // 4, 0)) % NFFT
    step = 2.0 * math.pi / NFFT
    taper = 0.5 - 0.5 * jnp.cos(step * sample.astype(jnp.float32))
    value = taper * (1.0 / window_norm()) * jnp.cos(step * phase.astype(jnp.float32))
    leading, trailing = value[:, :HOP], value[:, HOP:]
    group_of = lax.broadcasted_iota(jnp.int32, (SUB, HOP), 0) // SERIES
    per_tile = SUB // SERIES
    for first in range(0, table_ref.shape[0], 2 * SUB):
        for half in range(half_count):
            tiles = []
            for start in (first // SERIES, first // SERIES + per_tile):
                group = group_of + start
                block = jnp.where(group == half_count, -1, group)
                tile = jnp.where(half == block, leading, 0.0)
                tile = jnp.where(half == block + 1, trailing, tile)
                tiles.append(jnp.where(group > half_count, 0.0, tile))
            packed = jnp.concatenate(tiles, axis=0).astype(jnp.bfloat16)
            table_ref[first : first + 2 * SUB, half * HOP : (half + 1) * HOP] = packed


def block_sums(freq_bins, position, snapshots, shards, shifts):
    samples, points = snapshots.shape
    half_count = samples // HOP
    rows = SERIES * half_count
    width = points // shards
    fold = width // half_count
    table_shape = (rows + SUB * 2, samples)
    count = len(shifts)

    def body(freq_ref, position_ref, data_ref, *refs):
        outs, (join_ref, table_ref, buffer_ref, sems) = refs[:count], refs[count:]
        copies = []
        for i, shift in enumerate(shifts):
            first = pl.multiple_of((position_ref[0] ^ shift) * width, width)
            copies.append(
                pltpu.make_async_copy(
                    data_ref.at[:, pl.ds(first, width)], buffer_ref.at[i], sems.at[i]
                )
            )
            copies[-1].start()
        fill_table(freq_ref, table_ref, half_count)
        for k in range(half_count):
            join_ref[k] = join_matrix(position_ref[0], shifts, k, half_count)
        for copy, out_ref, i in zip(copies, outs, range(count)):
            copy.wait()
            sums = jnp.dot(table_ref[...], buffer_ref[i], preferred_element_type=jnp.float32)
            out_ref[:, :width] = sums[:rows].astype(jnp.bfloat16)
            early = sums[rows : rows + SERIES]
            folded = jnp.concatenate(
                [early[:, k * fold : (k + 1) * fold] for k in range(half_count)], axis=0
            )
            out_ref[:, width:] = folded.astype(jnp.bfloat16)

    local = pl.BlockSpec(memory_space=pltpu.VMEM)
    shapes = [pltpu.VMEM((rows, width + fold), jnp.bfloat16) for _ in shifts]
    shapes.append(pltpu.VMEM((half_count, rows * shards, 2 * rows * shards), jnp.bfloat16))
    smem = pl.BlockSpec(memory_space=pltpu.SMEM)
    return pl.pallas_call(
        body,
        in_specs=[smem, smem, pl.BlockSpec(memory_space=pl.ANY)],
        out_shape=tuple(shapes),
        out_specs=(local,) * len(shapes),
        scratch_shapes=[
            pltpu.VMEM(table_shape, jnp.bfloat16),
            pltpu.VMEM((count, samples, width), jnp.bfloat16),
            pltpu.SemaphoreType.DMA((count,)),
        ],
        name="block_sums",
    )(freq_bins, position, snapshots)


def join_matrix(position, shifts, k, half_count):
    shards = len(shifts)
    rows = SERIES * half_count
    total = shards * rows
    target = lax.broadcasted_iota(jnp.int32, (total, 1), 0)
    series = target // (shards * half_count)
    shard = target // half_count % shards
    block = target % half_count
    source = lax.broadcasted_iota(jnp.int32, (1, 2 * total), 1)
    slot, row = source // rows % shards, source % rows
    sender = jnp.zeros_like(source)
    for i, shift in enumerate(shifts):
        sender = jnp.where(slot == i, position ^ shift, sender)
    folded = source >= total
    code = jnp.where(folded, total, 0) + sender * rows + row
    own = shard * rows + block * SERIES + series
    after = (shard + 1) % shards
    early = total + after * rows + k * SERIES + series
    early = jnp.where(block == half_count - 1, early, -1)
    return jnp.where((code == own) | (code == early), 1.0, 0.0).astype(jnp.bfloat16)


def join_and_gram(received, joins, half_count, grid_total):
    shards = len(received)
    rows, span = received[0].shape
    width = span * half_count // (half_count + 1)
    fold = width // half_count
    total = shards * rows
    size = total // NF

    def body(join_ref, *refs):
        parts, (columns_ref, gram_ref) = refs[:shards], refs[shards:]
        folded = [part[:, width:] for part in parts]
        for k in range(half_count):
            own = [part[:, k * fold : (k + 1) * fold] for part in parts]
            both = jnp.concatenate(own + folded, axis=0)
            joined = jnp.dot(join_ref[k], both, preferred_element_type=jnp.float32)
            columns_ref[:, k * fold : (k + 1) * fold] = joined.astype(jnp.bfloat16)
        columns = columns_ref[...]
        products = lax.dot_general(
            columns, columns, (((1,), (1,)), ((), ())), preferred_element_type=jnp.float32
        )
        for f in range(NF):
            part = products[f * size : (f + 1) * size, f * size : (f + 1) * size]
            gram_ref[:, f * size : (f + 1) * size] = part * (1.0 / grid_total)

    return pl.pallas_call(
        body,
        in_specs=[pl.BlockSpec(memory_space=pltpu.VMEM)] * (shards + 1),
        out_shape=(
            pltpu.VMEM((total, width), jnp.bfloat16),
            pltpu.VMEM((size, NF * size), jnp.float32),
        ),
        out_specs=(pl.BlockSpec(memory_space=pltpu.VMEM),) * 2,
        name="join_and_gram",
    )(near(joins), *[near(part) for part in received])


def near(value):
    return pltpu.with_memory_space_constraint(value, pltpu.VMEM)


def spread_order(shards):
    bits = (shards - 1).bit_length()
    order = [int(f"{k:0{bits}b}"[::-1], 2) for k in range(1, shards)]
    return order + [0]


GRID = ("space", "tm")


def swapped(value, flips):
    wide, long = (lax.axis_size(name) for name in GRID)
    pairs = [
        (i * long + j, (i ^ flips[0]) * long + (j ^ flips[1]))
        for i in range(wide)
        for j in range(long)
    ]
    return lax.ppermute(value, GRID, pairs)


def exchange_rounds():
    bits = [(1 << k, 0) for k in range((lax.axis_size("space") - 1).bit_length())]
    bits += [(0, 1 << k) for k in range((lax.axis_size("tm") - 1).bit_length())]
    rounds, rest = [bits[:1]], bits[1:]
    while rest:
        rounds.append(rest[:2])
        rest = rest[2:]
    return rounds


def peers_of(value, bits):
    if len(bits) == 1:
        return [swapped(value, bits[0])]
    (a, b), (c, d) = bits
    return [swapped(value, flips) for flips in ((a, b), (c, d), (a + c, b + d))]


def add_up(values):
    while len(values) > 1:
        values = [values[i] + values[i + 1] for i in range(0, len(values), 2)]
    return values[0]


def spread_row(block, i):
    return jnp.broadcast_to(block[i : i + 1, :], block.shape)


def block_inverse(d):
    low = [[None] * SUB for _ in range(SUB)]
    for k in range(SUB):
        scale = lax.rsqrt(d[k][k])
        for j in range(k):
            low[k][j] = low[k][j] * scale
        low[k][k] = scale
        below = [d[i][k] * scale for i in range(k + 1, SUB)]
        for i in range(k + 1, SUB):
            x = below[i - k - 1]
            for j in range(k + 1, i + 1):
                d[i][j] = d[i][j] - x * below[j - k - 1]
            for j in range(k + 1):
                term = x * low[k][j]
                low[i][j] = -term if low[i][j] is None else low[i][j] - term
    return low


def tree_sum(terms):
    while len(terms) > 1:
        pairs = [terms[i] + terms[i + 1] for i in range(0, len(terms) - 1, 2)]
        terms = pairs + terms[len(pairs) * 2 :]
    return terms[0]


def inverse_factor(gram, size):
    lanes = NF * size
    sub = lax.broadcasted_iota(jnp.int32, (SUB, lanes), 0)
    lane = lax.broadcasted_iota(jnp.int32, (SUB, lanes), 1)
    work, side = [], []
    for start in range(0, size, SUB):
        eye = jnp.where(lane % size == sub + start, 1.0, 0.0)
        work.append(gram[start : start + SUB, :] + ridge_term * eye)
        side.append(eye)
    done = []
    for step in range(size // SUB):
        start = step * SUB

        def column_of(block, m):
            first = jnp.broadcast_to(block[:, start + m : start + m + 1], (SUB, lanes))
            for f in range(1, NF):
                at = f * size + start + m
                other = jnp.broadcast_to(block[:, at : at + 1], (SUB, lanes))
                first = jnp.where(lane < f * size, first, other)
            return first

        columns = [[column_of(block, m) for m in range(SUB)] for block in work]
        head = columns[0]
        low = block_inverse(
            [[spread_row(head[j], i) for j in range(i + 1)] for i in range(SUB)]
        )

        def solve_rows(block):
            source = [spread_row(block, m) for m in range(SUB)]
            return [
                tree_sum([low[j][m] * source[m] for m in range(j + 1)]) for j in range(SUB)
            ]

        def apply_transposed(solved):
            return [
                tree_sum([low[j][m] * solved[j] for j in range(m, SUB)]) for m in range(SUB)
            ]

        solved_side = solve_rows(side[0])
        packed = solved_side[0]
        for j in range(1, SUB):
            packed = jnp.where(sub == j, solved_side[j], packed)
        done.append(packed)
        if len(work) > 1:
            top = apply_transposed(solve_rows(work[0]))
            top_side = apply_transposed(solved_side)
            work = [
                block - tree_sum([column[m] * top[m] for m in range(SUB)])
                for block, column in zip(work[1:], columns[1:])
            ]
            side = [
                block - tree_sum([column[m] * top_side[m] for m in range(SUB)])
                for block, column in zip(side[1:], columns[1:])
            ]
    return jnp.concatenate(done, axis=0)


def whiten(grams, columns):
    count = len(grams)
    size = grams[0].shape[0]
    total, width = columns.shape
    chunk = min(width, 512)
    chunks = width // chunk

    def body(*refs):
        columns_ref, gram_out, white_out, gram_ref, left_ref, white_ref, sems = refs[count:]
        total_gram = add_up([ref[...] for ref in refs[:count]])
        copies = []
        for f in range(NF):
            gram_ref[f] = total_gram[:, f * size : (f + 1) * size]
        copies.append(pltpu.make_async_copy(gram_ref, gram_out, sems.at[0]))
        copies[-1].start()
        inverse = inverse_factor(total_gram, size)
        lane = lax.broadcasted_iota(jnp.int32, (size, NF * size), 1)
        for f in range(NF):
            own = jnp.where(lane // size == f, inverse, 0.0)
            high = own.astype(jnp.bfloat16)
            rest = (own - high.astype(jnp.float32)).astype(jnp.bfloat16)
            left_ref[f * size : (f + 1) * size, : NF * size] = high
            left_ref[f * size : (f + 1) * size, NF * size :] = rest
        for k in range(chunks):
            here = pl.ds(k * chunk, chunk)
            part = columns_ref[:, here]
            both = jnp.concatenate([part, part], axis=0)
            done = jnp.dot(left_ref[...], both, preferred_element_type=jnp.float32)
            for f in range(NF):
                white_ref[f, :, here] = done[f * size : (f + 1) * size]
            copies.append(
                pltpu.make_async_copy(
                    white_ref.at[:, :, here], white_out.at[:, :, here], sems.at[k + 1]
                )
            )
            copies[-1].start()
        for copy in copies:
            copy.wait()

    return pl.pallas_call(
        body,
        in_specs=[pl.BlockSpec(memory_space=pltpu.VMEM)] * (count + 1),
        out_shape=(
            jax.ShapeDtypeStruct((NF, size, size), jnp.float32),
            jax.ShapeDtypeStruct((NF, size, width), jnp.float32),
        ),
        out_specs=(pl.BlockSpec(memory_space=pl.ANY),) * 2,
        scratch_shapes=[
            pltpu.VMEM((NF, size, size), jnp.float32),
            pltpu.VMEM((total, 2 * NF * size), jnp.bfloat16),
            pltpu.VMEM((NF, size, width), jnp.float32),
            pltpu.SemaphoreType.DMA((chunks + 1,)),
        ],
        name="whiten",
    )(*[near(gram) for gram in grams], near(columns))


def on_device(snapshots, freq_bins):
    shards = lax.axis_size("tm")
    half_count = snapshots.shape[0] // HOP
    grid_total = snapshots.shape[1] * lax.axis_size("space")
    position = lax.axis_index("tm").astype(jnp.int32)[None]
    shifts = spread_order(shards)
    *parts, joins = block_sums(freq_bins, position, snapshots, shards, shifts)
    received = []
    for shift, part in zip(shifts, parts):
        pairs = [(i, i ^ shift) for i in range(shards)]
        received.append(lax.ppermute(part, "tm", pairs) if shift else part)
    columns, gram = join_and_gram(received, joins, half_count, grid_total)
    grams = [gram]
    for bits in exchange_rounds():
        gram = add_up(grams)
        grams = [gram] + peers_of(gram, bits)
    return whiten(grams, columns)


def solution(mesh):
    placed = (P("tm", "space"), P())
    return jax.shard_map(
        on_device,
        mesh=mesh,
        in_specs=placed,
        out_specs=(P(), P(None, None, ("space", "tm"))),
        check_vma=False,
    )
```

time: 49.1 us -> 46.4 us (0.945)
  starting transfers between devices: 25 us -> 21.8 us
  waiting for transfers between devices: 12.5 us -> 13.2 us
    ppermute x7, starting transfers between devices: 16.3 us -> 13.8 us  [on_device(): received.append(lax.ppermute(part, 'tm', pairs) if shift else part)]
    ppermute x7, waiting for transfers between devices: 3.72 us -> 5.97 us  [on_device(): received.append(lax.ppermute(part, 'tm', pairs) if shift else part)]
    ppermute x7, waiting for transfers between devices: 8.74 us -> 7.22 us  [swapped(): return lax.ppermute(value, GRID, pairs)]
    ppermute x7, starting transfers between devices: 8.71 us -> 8.01 us  [swapped(): return lax.ppermute(value, GRID, pairs)]
  transfers between devices with their start and end apart: 14 -> 14, of which waited for: 9 -> 8; matrix products, arithmetic and copies ran while one was open for 0% -> 0% of each run, Pallas kernels for 0% -> 0%
where the time goes in v3:
time: 46.4 us; the launch traced here: 46.3 us
  starting transfers between devices  21.8 us (47%)
  waiting for transfers between devices  13.2 us (28%)
  Pallas kernels  10.6 us (23%)
  between operations  0.67 us (1%)
    ppermute x7, starting transfers between devices, on_device(): received.append(lax.ppermute(part, 'tm', pairs) if shift else part)  13.8 us
    ppermute x7, starting transfers between devices, swapped(): return lax.ppermute(value, GRID, pairs)  8.01 us
    ppermute x7, waiting for transfers between devices, swapped(): return lax.ppermute(value, GRID, pairs)  7.22 us
    pallas_call x1, Pallas kernels, block_sums(): pl.pallas_call(body, in_specs=[smem, smem, pl.BlockSpec(memory_space=pl.A...  7.09 us
    ppermute x7, waiting for transfers between devices, on_device(): received.append(lax.ppermute(part, 'tm', pairs) if shift else part)  5.97 us
    pallas_call x1, Pallas kernels, whiten(): pl.pallas_call(body, in_specs=[pl.BlockSpec(memory_space=pltpu.VMEM)] * (...  2.93 us
  transfers between devices with their start and end apart: 14, of which 8 were waited for; matrix products, arithmetic and copies ran while one was open for 0% of the time, Pallas kernels for 0%

profile of v3, /device:TPU:0, one launch (start us, length us, event | category | flops | bytes accessed | tf_op | source)
XLA Modules:
  0.0 46.3 jit_solution(10462898412237376162)
XLA Ops:
  0.6 7.1 %block_sums.1 = (bf16[16,2560]{1,0:T(8,128)(2,1)S(1)}, bf16[16,2560]{1,0:T(8,128)(2,1)S(1)}, bf16[16,2560]{1,0:T(8,128)(2,1)S(1)}, bf16[16,2560]{1,0:T(8,128)(2,...) custom-call(s32[2]{0:T(128)} %freq_ref.1, ...), custom_call_target="tpu_custom_call" | custom-call | tf_op jit(solution)/shard_map/block_sums/pallas_call | solution.py:88
  7.7 4.1 %collective-permute-start = (bf16[16,2560]{1,0:T(8,128)(2,1)S(1)}, bf16[16,2560]{1,0:T(8,128)(2,1)S(1)}, u32[]{:S(2)}, u32[]{:S(2)}) collective-permute-start(bf16[16,2560]{1,0:T(8,128)(2,1)S(1)} %get-tuple-element.14), channel_id=1, source_target_pairs={{0,4},{1,5},{2,6},{3,7},{4,0},{5,1},{6,2},{7,3},{8,12},{9,13},{10,... | collective-permute-start | bytes 245768 | tf_op jit(solution)/shard_map/ppermute | solution.py:359
  11.9 1.6 %collective-permute-start.1 = (bf16[16,2560]{1,0:T(8,128)(2,1)S(1)}, bf16[16,2560]{1,0:T(8,128)(2,1)S(1)}, u32[]{:S(2)}, u32[]{:S(2)}) collective-permute-start(bf16[16,2560]{1,0:T(8,128)(2,1)S(1)} %get-tuple-element.15), channel_id=1, source_target_pairs={{0,2},{1,3},{2,0},{3,1},{4,6},{5,7},{6,4},{7,5},{8,10},{9,11},{10,... | collective-permute-start | bytes 245768 | tf_op jit(solution)/shard_map/ppermute | solution.py:359
  13.4 0.0 collective-permute-start.2
  13.4 1.7 %collective-permute-start.3 = (bf16[16,2560]{1,0:T(8,128)(2,1)S(1)}, bf16[16,2560]{1,0:T(8,128)(2,1)S(1)}, u32[]{:S(2)}, u32[]{:S(2)}) collective-permute-start(bf16[16,2560]{1,0:T(8,128)(2,1)S(1)} %get-tuple-element.17), channel_id=1, source_target_pairs={{0,1},{1,0},{2,3},{3,2},{4,5},{5,4},{6,7},{7,6},{8,9},{9,8},{10,11... | collective-permute-start | bytes 245768 | tf_op jit(solution)/shard_map/ppermute | solution.py:359
  15.2 1.6 %collective-permute-start.4 = (bf16[16,2560]{1,0:T(8,128)(2,1)S(1)}, bf16[16,2560]{1,0:T(8,128)(2,1)S(1)}, u32[]{:S(2)}, u32[]{:S(2)}) collective-permute-start(bf16[16,2560]{1,0:T(8,128)(2,1)S(1)} %get-tuple-element.18), channel_id=1, source_target_pairs={{0,5},{1,4},{2,7},{3,6},{4,1},{5,0},{6,3},{7,2},{8,13},{9,12},{10,... | collective-permute-start | bytes 245768 | tf_op jit(solution)/shard_map/ppermute | solution.py:359
  16.8 0.0 collective-permute-done.refs_0_
  16.8 3.4 %collective-permute-start.5 = (bf16[16,2560]{1,0:T(8,128)(2,1)S(1)}, bf16[16,2560]{1,0:T(8,128)(2,1)S(1)}, u32[]{:S(2)}, u32[]{:S(2)}) collective-permute-start(bf16[16,2560]{1,0:T(8,128)(2,1)S(1)} %get-tuple-element.19), channel_id=1, source_target_pairs={{0,3},{1,2},{2,1},{3,0},{4,7},{5,6},{6,5},{7,4},{8,11},{9,10},{10,... | collective-permute-start | bytes 245768 | tf_op jit(solution)/shard_map/ppermute | solution.py:359
  20.3 0.0 collective-permute-done.1.refs_1_
  20.3 1.3 %collective-permute-start.6 = (bf16[16,2560]{1,0:T(8,128)(2,1)S(1)}, bf16[16,2560]{1,0:T(8,128)(2,1)S(1)}, u32[]{:S(2)}, u32[]{:S(2)}) collective-permute-start(bf16[16,2560]{1,0:T(8,128)(2,1)S(1)} %get-tuple-element.20), channel_id=1, source_target_pairs={{0,7},{1,6},{2,5},{3,4},{4,3},{5,2},{6,1},{7,0},{8,15},{9,14},{10,... | collective-permute-start | bytes 245768 | tf_op jit(solution)/shard_map/ppermute | solution.py:359
  21.5 0.0 collective-permute-done.2.refs_2_
  21.5 0.0 collective-permute-done.3.refs_3_
  21.5 4.2 %collective-permute-done.4.refs_4_ = bf16[16,2560]{1,0:T(8,128)(2,1)S(1)} collective-permute-done((bf16[16,2560]{1,0:T(8,128)(2,1)S(1)}, bf16[16,2560]{1,0:T(8,128)(2,1)S(1)}, u32[]{:S(2)}, u32[]{:S(2)}) %collective-permute-start.4) | collective-permute-done | bytes 81952 | tf_op jit(solution)/shard_map/ppermute | solution.py:359
  25.7 0.0 collective-permute-done.5.refs_5_
  25.7 1.7 %collective-permute-done.6.refs_6_ = bf16[16,2560]{1,0:T(8,128)(2,1)S(1)} collective-permute-done((bf16[16,2560]{1,0:T(8,128)(2,1)S(1)}, bf16[16,2560]{1,0:T(8,128)(2,1)S(1)}, u32[]{:S(2)}, u32[]{:S(2)}) %collective-permute-start.6) | collective-permute-done | bytes 81952 | tf_op jit(solution)/shard_map/ppermute | solution.py:359
  27.5 0.6 %join_and_gram.1 = (bf16[128,2048]{1,0:T(8,128)(2,1)S(1)}, f32[64,128]{1,0:T(8,128)S(1)}) custom-call(bf16[4,128,256]{2,1,0:T(8,128)(2,1)S(1)} %get-tuple-element.13.join_ref, bf16[16,2560]{1,0:T(8,128)(2,1)S(1)} %collective-permute-done.refs_0_, bf16[16,2560]{1,0:T(8,128)(2,1)S(1)} %collective-permute-done.1.refs_1_, ...), custom_call_target="tpu_custom_call" | custom-call | tf_op jit(solution)/shard_map/join_and_gram/pallas_call | solution.py:148
  28.1 0.1 collective-permute-start.7
  28.1 1.2 %collective-permute-done.7 = f32[64,128]{1,0:T(8,128)S(1)} collective-permute-done((f32[64,128]{1,0:T(8,128)S(1)}, f32[64,128]{1,0:T(8,128)S(1)}, u32[]{:S(2)}, u32[]{:S(2)}) %collective-permute-start.7) | collective-permute-done | bytes 32800 | tf_op jit(solution)/shard_map/ppermute | solution.py:180
  29.3 1.4 %collective-permute-start.10 = (f32[64,128]{1,0:T(8,128)S(1)}, f32[64,128]{1,0:T(8,128)S(1)}, u32[]{:S(2)}, u32[]{:S(2)}) collective-permute-start(f32[64,128]{1,0:T(8,128)S(1)} %add.12), channel_id=1, source_target_pairs={{0,17},{1,16},{2,19},{3,18},{4,21},{5,20},{6,23},{7,22},{8,25},{9,... | collective-permute-start | bytes 98312 | tf_op jit(solution)/shard_map/ppermute | solution.py:180
  30.8 1.5 %collective-permute-start.9 = (f32[64,128]{1,0:T(8,128)S(1)}, f32[64,128]{1,0:T(8,128)S(1)}, u32[]{:S(2)}, u32[]{:S(2)}) collective-permute-start(f32[64,128]{1,0:T(8,128)S(1)} %add.12), channel_id=1, source_target_pairs={{0,1},{1,0},{2,3},{3,2},{4,5},{5,4},{6,7},{7,6},{8,9},{9,8},{10,11... | collective-permute-start | bytes 98312 | tf_op jit(solution)/shard_map/ppermute | solution.py:180
  32.3 0.5 %collective-permute-start.8 = (f32[64,128]{1,0:T(8,128)S(1)}, f32[64,128]{1,0:T(8,128)S(1)}, u32[]{:S(2)}, u32[]{:S(2)}) collective-permute-start(f32[64,128]{1,0:T(8,128)S(1)} %add.12), channel_id=1, source_target_pairs={{0,16},{1,17},{2,18},{3,19},{4,20},{5,21},{6,22},{7,23},{8,24},{9,... | collective-permute-start | bytes 98312 | tf_op jit(solution)/shard_map/ppermute | solution.py:180
  32.8 1.3 %collective-permute-done.10 = f32[64,128]{1,0:T(8,128)S(1)} collective-permute-done((f32[64,128]{1,0:T(8,128)S(1)}, f32[64,128]{1,0:T(8,128)S(1)}, u32[]{:S(2)}, u32[]{:S(2)}) %collective-permute-start.10) | collective-permute-done | bytes 32800 | tf_op jit(solution)/shard_map/ppermute | solution.py:180
  34.2 0.5 %collective-permute-done.9 = f32[64,128]{1,0:T(8,128)S(1)} collective-permute-done((f32[64,128]{1,0:T(8,128)S(1)}, f32[64,128]{1,0:T(8,128)S(1)}, u32[]{:S(2)}, u32[]{:S(2)}) %collective-permute-start.9) | collective-permute-done | bytes 32800 | tf_op jit(solution)/shard_map/ppermute | solution.py:180
  34.7 1.5 %collective-permute-done.8 = f32[64,128]{1,0:T(8,128)S(1)} collective-permute-done((f32[64,128]{1,0:T(8,128)S(1)}, f32[64,128]{1,0:T(8,128)S(1)}, u32[]{:S(2)}, u32[]{:S(2)}) %collective-permute-start.8) | collective-permute-done | bytes 32800 | tf_op jit(solution)/shard_map/ppermute | solution.py:180
  36.2 2.2 %collective-permute-start.13 = (f32[64,128]{1,0:T(8,128)S(1)}, f32[64,128]{1,0:T(8,128)S(1)}, u32[]{:S(2)}, u32[]{:S(2)}) collective-permute-start(f32[64,128]{1,0:T(8,128)S(1)} %add_add_fusion.refs_0_), channel_id=1, source_target_pairs={{0,6},{1,7},{2,4},{3,5},{4,2},{5,3},{6,0},{7,1},{8,14},{9,15},{10,... | collective-permute-start | bytes 98312 | tf_op jit(solution)/shard_map/ppermute | solution.py:180
  38.4 0.7 %collective-permute-start.12 = (f32[64,128]{1,0:T(8,128)S(1)}, f32[64,128]{1,0:T(8,128)S(1)}, u32[]{:S(2)}, u32[]{:S(2)}) collective-permute-start(f32[64,128]{1,0:T(8,128)S(1)} %add_add_fusion.refs_0_), channel_id=1, source_target_pairs={{0,4},{1,5},{2,6},{3,7},{4,0},{5,1},{6,2},{7,3},{8,12},{9,13},{10,... | collective-permute-start | bytes 98312 | tf_op jit(solution)/shard_map/ppermute | solution.py:180
  39.1 1.6 %collective-permute-start.11 = (f32[64,128]{1,0:T(8,128)S(1)}, f32[64,128]{1,0:T(8,128)S(1)}, u32[]{:S(2)}, u32[]{:S(2)}) collective-permute-start(f32[64,128]{1,0:T(8,128)S(1)} %add_add_fusion.refs_0_), channel_id=1, source_target_pairs={{0,2},{1,3},{2,0},{3,1},{4,6},{5,7},{6,4},{7,5},{8,10},{9,11},{10,... | collective-permute-start | bytes 98312 | tf_op jit(solution)/shard_map/ppermute | solution.py:180
  40.7 1.3 %collective-permute-done.13.refs_3_ = f32[64,128]{1,0:T(8,128)S(1)} collective-permute-done((f32[64,128]{1,0:T(8,128)S(1)}, f32[64,128]{1,0:T(8,128)S(1)}, u32[]{:S(2)}, u32[]{:S(2)}) %collective-permute-start.13) | collective-permute-done | bytes 32800 | tf_op jit(solution)/shard_map/ppermute | solution.py:180
  42.0 1.3 %collective-permute-done.12.refs_2_ = f32[64,128]{1,0:T(8,128)S(1)} collective-permute-done((f32[64,128]{1,0:T(8,128)S(1)}, f32[64,128]{1,0:T(8,128)S(1)}, u32[]{:S(2)}, u32[]{:S(2)}) %collective-permute-start.12) | collective-permute-done | bytes 32800 | tf_op jit(solution)/shard_map/ppermute | solution.py:180
  43.3 0.0 collective-permute-done.11.refs_1_
  43.3 2.9 %whiten.1 = (f32[2,64,64]{2,1,0:T(8,128)}, f32[2,64,2048]{2,1,0:T(8,128)}) custom-call(f32[64,128]{1,0:T(8,128)S(1)} %add_add_fusion.refs_0_, f32[64,128]{1,0:T(8,128)S(1)} %collective-permute-done.11.refs_1_, f32[64,128]{1,0:T(8,128)S(1)} %collective-permute-done.12.refs_2_, f32[64,128]{1,0:T(8,128)S(1)} %collective-permute-done.13.refs_3_, ...), custom_call_target="tpu_custom_call" | custom-call | tf_op jit(solution)/shard_map/whiten/pallas_call | solution.py:331
  (2 shorter events, 0.0 us)
Async XLA Ops:
  7.7 9.1 %collective-permute-start = (bf16[16,2560]{1,0:T(8,128)(2,1)S(1)}, bf16[16,2560]{1,0:T(8,128)(2,1)S(1)}, u32[]{:S(2)}, u32[]{:S(2)}) collective-permute-start(bf16[16,2560]{1,0:T(8,128)(2,1)S(1)} %get-tuple-element.14), channel_id=1, source_target_pairs={{0,4},{1,5},{2,6},{3,7},{4,0},{5,1},{6,2},{7,3},{8,12},{9,13},{10,... | collective-permute-start | bytes 245768 | tf_op jit(solution)/shard_map/ppermute | solution.py:359
  11.9 8.4 %collective-permute-start.1 = (bf16[16,2560]{1,0:T(8,128)(2,1)S(1)}, bf16[16,2560]{1,0:T(8,128)(2,1)S(1)}, u32[]{:S(2)}, u32[]{:S(2)}) collective-permute-start(bf16[16,2560]{1,0:T(8,128)(2,1)S(1)} %get-tuple-element.15), channel_id=1, source_target_pairs={{0,2},{1,3},{2,0},{3,1},{4,6},{5,7},{6,4},{7,5},{8,10},{9,11},{10,... | collective-permute-start | bytes 245768 | tf_op jit(solution)/shard_map/ppermute | solution.py:359
  13.4 8.1 %collective-permute-start.2 = (bf16[16,2560]{1,0:T(8,128)(2,1)S(1)}, bf16[16,2560]{1,0:T(8,128)(2,1)S(1)}, u32[]{:S(2)}, u32[]{:S(2)}) collective-permute-start(bf16[16,2560]{1,0:T(8,128)(2,1)S(1)} %get-tuple-element.16), channel_id=1, source_target_pairs={{0,6},{1,7},{2,4},{3,5},{4,2},{5,3},{6,0},{7,1},{8,14},{9,15},{10,... | collective-permute-start | bytes 245768 | tf_op jit(solution)/shard_map/ppermute | solution.py:359
  13.4 8.1 %collective-permute-start.3 = (bf16[16,2560]{1,0:T(8,128)(2,1)S(1)}, bf16[16,2560]{1,0:T(8,128)(2,1)S(1)}, u32[]{:S(2)}, u32[]{:S(2)}) collective-permute-start(bf16[16,2560]{1,0:T(8,128)(2,1)S(1)} %get-tuple-element.17), channel_id=1, source_target_pairs={{0,1},{1,0},{2,3},{3,2},{4,5},{5,4},{6,7},{7,6},{8,9},{9,8},{10,11... | collective-permute-start | bytes 245768 | tf_op jit(solution)/shard_map/ppermute | solution.py:359
  15.2 10.6 %collective-permute-start.4 = (bf16[16,2560]{1,0:T(8,128)(2,1)S(1)}, bf16[16,2560]{1,0:T(8,128)(2,1)S(1)}, u32[]{:S(2)}, u32[]{:S(2)}) collective-permute-start(bf16[16,2560]{1,0:T(8,128)(2,1)S(1)} %get-tuple-element.18), channel_id=1, source_target_pairs={{0,5},{1,4},{2,7},{3,6},{4,1},{5,0},{6,3},{7,2},{8,13},{9,12},{10,... | collective-permute-start | bytes 245768 | tf_op jit(solution)/shard_map/ppermute | solution.py:359
  16.8 8.9 %collective-permute-start.5 = (bf16[16,2560]{1,0:T(8,128)(2,1)S(1)}, bf16[16,2560]{1,0:T(8,128)(2,1)S(1)}, u32[]{:S(2)}, u32[]{:S(2)}) collective-permute-start(bf16[16,2560]{1,0:T(8,128)(2,1)S(1)} %get-tuple-element.19), channel_id=1, source_target_pairs={{0,3},{1,2},{2,1},{3,0},{4,7},{5,6},{6,5},{7,4},{8,11},{9,10},{10,... | collective-permute-start | bytes 245768 | tf_op jit(solution)/shard_map/ppermute | solution.py:359
  20.3 7.2 %collective-permute-start.6 = (bf16[16,2560]{1,0:T(8,128)(2,1)S(1)}, bf16[16,2560]{1,0:T(8,128)(2,1)S(1)}, u32[]{:S(2)}, u32[]{:S(2)}) collective-permute-start(bf16[16,2560]{1,0:T(8,128)(2,1)S(1)} %get-tuple-element.20), channel_id=1, source_target_pairs={{0,7},{1,6},{2,5},{3,4},{4,3},{5,2},{6,1},{7,0},{8,15},{9,14},{10,... | collective-permute-start | bytes 245768 | tf_op jit(solution)/shard_map/ppermute | solution.py:359
  28.1 1.3 %collective-permute-start.7 = (f32[64,128]{1,0:T(8,128)S(1)}, f32[64,128]{1,0:T(8,128)S(1)}, u32[]{:S(2)}, u32[]{:S(2)}) collective-permute-start(f32[64,128]{1,0:T(8,128)S(1)} %get-tuple-element.22), channel_id=1, source_target_pairs={{0,8},{1,9},{2,10},{3,11},{4,12},{5,13},{6,14},{7,15},{8,0},{9,1},... | collective-permute-start | bytes 98312 | tf_op jit(solution)/shard_map/ppermute | solution.py:180
  29.3 4.8 %collective-permute-start.10 = (f32[64,128]{1,0:T(8,128)S(1)}, f32[64,128]{1,0:T(8,128)S(1)}, u32[]{:S(2)}, u32[]{:S(2)}) collective-permute-start(f32[64,128]{1,0:T(8,128)S(1)} %add.12), channel_id=1, source_target_pairs={{0,17},{1,16},{2,19},{3,18},{4,21},{5,20},{6,23},{7,22},{8,25},{9,... | collective-permute-start | bytes 98312 | tf_op jit(solution)/shard_map/ppermute | solution.py:180
  30.8 3.9 %collective-permute-start.9 = (f32[64,128]{1,0:T(8,128)S(1)}, f32[64,128]{1,0:T(8,128)S(1)}, u32[]{:S(2)}, u32[]{:S(2)}) collective-permute-start(f32[64,128]{1,0:T(8,128)S(1)} %add.12), channel_id=1, source_target_pairs={{0,1},{1,0},{2,3},{3,2},{4,5},{5,4},{6,7},{7,6},{8,9},{9,8},{10,11... | collective-permute-start | bytes 98312 | tf_op jit(solution)/shard_map/ppermute | solution.py:180
  32.3 3.9 %collective-permute-start.8 = (f32[64,128]{1,0:T(8,128)S(1)}, f32[64,128]{1,0:T(8,128)S(1)}, u32[]{:S(2)}, u32[]{:S(2)}) collective-permute-start(f32[64,128]{1,0:T(8,128)S(1)} %add.12), channel_id=1, source_target_pairs={{0,16},{1,17},{2,18},{3,19},{4,20},{5,21},{6,22},{7,23},{8,24},{9,... | collective-permute-start | bytes 98312 | tf_op jit(solution)/shard_map/ppermute | solution.py:180
  36.2 5.8 %collective-permute-start.13 = (f32[64,128]{1,0:T(8,128)S(1)}, f32[64,128]{1,0:T(8,128)S(1)}, u32[]{:S(2)}, u32[]{:S(2)}) collective-permute-start(f32[64,128]{1,0:T(8,128)S(1)} %add_add_fusion.refs_0_), channel_id=1, source_target_pairs={{0,6},{1,7},{2,4},{3,5},{4,2},{5,3},{6,0},{7,1},{8,14},{9,15},{10,... | collective-permute-start | bytes 98312 | tf_op jit(solution)/shard_map/ppermute | solution.py:180
  38.4 4.9 %collective-permute-start.12 = (f32[64,128]{1,0:T(8,128)S(1)}, f32[64,128]{1,0:T(8,128)S(1)}, u32[]{:S(2)}, u32[]{:S(2)}) collective-permute-start(f32[64,128]{1,0:T(8,128)S(1)} %add_add_fusion.refs_0_), channel_id=1, source_target_pairs={{0,4},{1,5},{2,6},{3,7},{4,0},{5,1},{6,2},{7,3},{8,12},{9,13},{10,... | collective-permute-start | bytes 98312 | tf_op jit(solution)/shard_map/ppermute | solution.py:180
  39.1 4.3 %collective-permute-start.11 = (f32[64,128]{1,0:T(8,128)S(1)}, f32[64,128]{1,0:T(8,128)S(1)}, u32[]{:S(2)}, u32[]{:S(2)}) collective-permute-start(f32[64,128]{1,0:T(8,128)S(1)} %add_add_fusion.refs_0_), channel_id=1, source_target_pairs={{0,2},{1,3},{2,0},{3,1},{4,6},{5,7},{6,4},{7,5},{8,10},{9,11},{10,... | collective-permute-start | bytes 98312 | tf_op jit(solution)/shard_map/ppermute | solution.py:180

commit v4 on v3

--- a/solution.py
+++ b/solution.py
@@ -181,20 +181,16 @@
 
 
 def exchange_rounds():
-    bits = [(1 << k, 0) for k in range((lax.axis_size("space") - 1).bit_length())]
+    cross = 1
+    bits = [(1 << k, 0) for k in range(1, (lax.axis_size("space") - 1).bit_length())]
     bits += [(0, 1 << k) for k in range((lax.axis_size("tm") - 1).bit_length())]
-    rounds, rest = [bits[:1]], bits[1:]
-    while rest:
-        rounds.append(rest[:2])
-        rest = rest[2:]
+    rounds = [[(cross, 0)]]
+    while bits:
+        (a, b), (c, d) = bits[0], bits[1] if len(bits) > 1 else (0, 0)
+        flips = [(a, b), (c, d), (a + c, b + d)] if len(bits) > 1 else [(a, b)]
+        rounds.append([(cross + i, j) for i, j in flips])
+        bits = bits[2:]
     return rounds
-
-
-def peers_of(value, bits):
-    if len(bits) == 1:
-        return [swapped(value, bits[0])]
-    (a, b), (c, d) = bits
-    return [swapped(value, flips) for flips in ((a, b), (c, d), (a + c, b + d))]
 
 
 def add_up(values):
@@ -359,9 +355,9 @@
         received.append(lax.ppermute(part, "tm", pairs) if shift else part)
     columns, gram = join_and_gram(received, joins, half_count, grid_total)
     grams = [gram]
-    for bits in exchange_rounds():
+    for flips in exchange_rounds():
         gram = add_up(grams)
-        grams = [gram] + peers_of(gram, bits)
+        grams = [gram] + [swapped(gram, flip) for flip in flips]
     return whiten(grams, columns)
 
 

time: 46.4 us -> 45.2 us (0.974)
  starting transfers between devices: 21.8 us -> 20.8 us
  waiting for transfers between devices: 13.2 us -> 12.6 us
    ppermute x7, starting transfers between devices: 8.01 us -> 6.99 us  [swapped(): return lax.ppermute(value, GRID, pairs)]
    ppermute x7, waiting for transfers between devices: 7.22 us -> 6.62 us  [swapped(): return lax.ppermute(value, GRID, pairs)]
  transfers between devices with their start and end apart: 14 -> 14, of which waited for: 8 -> 9; matrix products, arithmetic and copies ran while one was open for 0% -> 0% of each run, Pallas kernels for 0% -> 0%
where the time goes in v4:
time: 45.2 us; the launch traced here: 44.6 us
  starting transfers between devices  20.8 us (46%)
  waiting for transfers between devices  12.6 us (28%)
  Pallas kernels  10.6 us (23%)
  between operations  0.67 us (1%)
    ppermute x7, starting transfers between devices, on_device(): received.append(lax.ppermute(part, 'tm', pairs) if shift else part)  13.8 us
    pallas_call x1, Pallas kernels, block_sums(): pl.pallas_call(body, in_specs=[smem, smem, pl.BlockSpec(memory_space=pl.A...  7.09 us
    ppermute x7, starting transfers between devices, swapped(): return lax.ppermute(value, GRID, pairs)  6.99 us
    ppermute x7, waiting for transfers between devices, swapped(): return lax.ppermute(value, GRID, pairs)  6.62 us
    ppermute x7, waiting for transfers between devices, on_device(): received.append(lax.ppermute(part, 'tm', pairs) if shift else part)  5.97 us
    pallas_call x1, Pallas kernels, whiten(): pl.pallas_call(body, in_specs=[pl.BlockSpec(memory_space=pltpu.VMEM)] * (...  2.93 us
  transfers between devices with their start and end apart: 14, of which 9 were waited for; matrix products, arithmetic and copies ran while one was open for 0% of the time, Pallas kernels for 0%

profile of v4, /device:TPU:0, one launch (start us, length us, event | category | flops | bytes accessed | tf_op | source)
XLA Modules:
  0.0 44.6 jit_solution(18269695073042676217)
XLA Ops:
  0.6 7.1 %block_sums.1 = (bf16[16,2560]{1,0:T(8,128)(2,1)S(1)}, bf16[16,2560]{1,0:T(8,128)(2,1)S(1)}, bf16[16,2560]{1,0:T(8,128)(2,1)S(1)}, bf16[16,2560]{1,0:T(8,128)(2,...) custom-call(s32[2]{0:T(128)} %freq_ref.1, ...), custom_call_target="tpu_custom_call" | custom-call | tf_op jit(solution)/shard_map/block_sums/pallas_call | solution.py:88
  7.7 4.1 %collective-permute-start = (bf16[16,2560]{1,0:T(8,128)(2,1)S(1)}, bf16[16,2560]{1,0:T(8,128)(2,1)S(1)}, u32[]{:S(2)}, u32[]{:S(2)}) collective-permute-start(bf16[16,2560]{1,0:T(8,128)(2,1)S(1)} %get-tuple-element.14), channel_id=1, source_target_pairs={{0,4},{1,5},{2,6},{3,7},{4,0},{5,1},{6,2},{7,3},{8,12},{9,13},{10,... | collective-permute-start | bytes 245768 | tf_op jit(solution)/shard_map/ppermute | solution.py:355
  11.9 1.6 %collective-permute-start.1 = (bf16[16,2560]{1,0:T(8,128)(2,1)S(1)}, bf16[16,2560]{1,0:T(8,128)(2,1)S(1)}, u32[]{:S(2)}, u32[]{:S(2)}) collective-permute-start(bf16[16,2560]{1,0:T(8,128)(2,1)S(1)} %get-tuple-element.15), channel_id=1, source_target_pairs={{0,2},{1,3},{2,0},{3,1},{4,6},{5,7},{6,4},{7,5},{8,10},{9,11},{10,... | collective-permute-start | bytes 245768 | tf_op jit(solution)/shard_map/ppermute | solution.py:355
  13.4 0.0 collective-permute-start.2
  13.4 1.7 %collective-permute-start.3 = (bf16[16,2560]{1,0:T(8,128)(2,1)S(1)}, bf16[16,2560]{1,0:T(8,128)(2,1)S(1)}, u32[]{:S(2)}, u32[]{:S(2)}) collective-permute-start(bf16[16,2560]{1,0:T(8,128)(2,1)S(1)} %get-tuple-element.17), channel_id=1, source_target_pairs={{0,1},{1,0},{2,3},{3,2},{4,5},{5,4},{6,7},{7,6},{8,9},{9,8},{10,11... | collective-permute-start | bytes 245768 | tf_op jit(solution)/shard_map/ppermute | solution.py:355
  15.2 1.6 %collective-permute-start.4 = (bf16[16,2560]{1,0:T(8,128)(2,1)S(1)}, bf16[16,2560]{1,0:T(8,128)(2,1)S(1)}, u32[]{:S(2)}, u32[]{:S(2)}) collective-permute-start(bf16[16,2560]{1,0:T(8,128)(2,1)S(1)} %get-tuple-element.18), channel_id=1, source_target_pairs={{0,5},{1,4},{2,7},{3,6},{4,1},{5,0},{6,3},{7,2},{8,13},{9,12},{10,... | collective-permute-start | bytes 245768 | tf_op jit(solution)/shard_map/ppermute | solution.py:355
  16.8 0.0 collective-permute-done.refs_0_
  16.8 3.4 %collective-permute-start.5 = (bf16[16,2560]{1,0:T(8,128)(2,1)S(1)}, bf16[16,2560]{1,0:T(8,128)(2,1)S(1)}, u32[]{:S(2)}, u32[]{:S(2)}) collective-permute-start(bf16[16,2560]{1,0:T(8,128)(2,1)S(1)} %get-tuple-element.19), channel_id=1, source_target_pairs={{0,3},{1,2},{2,1},{3,0},{4,7},{5,6},{6,5},{7,4},{8,11},{9,10},{10,... | collective-permute-start | bytes 245768 | tf_op jit(solution)/shard_map/ppermute | solution.py:355
  20.3 0.0 collective-permute-done.1.refs_1_
  20.3 1.3 %collective-permute-start.6 = (bf16[16,2560]{1,0:T(8,128)(2,1)S(1)}, bf16[16,2560]{1,0:T(8,128)(2,1)S(1)}, u32[]{:S(2)}, u32[]{:S(2)}) collective-permute-start(bf16[16,2560]{1,0:T(8,128)(2,1)S(1)} %get-tuple-element.20), channel_id=1, source_target_pairs={{0,7},{1,6},{2,5},{3,4},{4,3},{5,2},{6,1},{7,0},{8,15},{9,14},{10,... | collective-permute-start | bytes 245768 | tf_op jit(solution)/shard_map/ppermute | solution.py:355
  21.5 0.0 collective-permute-done.2.refs_2_
  21.5 0.0 collective-permute-done.3.refs_3_
  21.5 4.2 %collective-permute-done.4.refs_4_ = bf16[16,2560]{1,0:T(8,128)(2,1)S(1)} collective-permute-done((bf16[16,2560]{1,0:T(8,128)(2,1)S(1)}, bf16[16,2560]{1,0:T(8,128)(2,1)S(1)}, u32[]{:S(2)}, u32[]{:S(2)}) %collective-permute-start.4) | collective-permute-done | bytes 81952 | tf_op jit(solution)/shard_map/ppermute | solution.py:355
  25.7 0.0 collective-permute-done.5.refs_5_
  25.7 1.7 %collective-permute-done.6.refs_6_ = bf16[16,2560]{1,0:T(8,128)(2,1)S(1)} collective-permute-done((bf16[16,2560]{1,0:T(8,128)(2,1)S(1)}, bf16[16,2560]{1,0:T(8,128)(2,1)S(1)}, u32[]{:S(2)}, u32[]{:S(2)}) %collective-permute-start.6) | collective-permute-done | bytes 81952 | tf_op jit(solution)/shard_map/ppermute | solution.py:355
  27.5 0.6 %join_and_gram.1 = (bf16[128,2048]{1,0:T(8,128)(2,1)S(1)}, f32[64,128]{1,0:T(8,128)S(1)}) custom-call(bf16[4,128,256]{2,1,0:T(8,128)(2,1)S(1)} %get-tuple-element.13.join_ref, bf16[16,2560]{1,0:T(8,128)(2,1)S(1)} %collective-permute-done.refs_0_, bf16[16,2560]{1,0:T(8,128)(2,1)S(1)} %collective-permute-done.1.refs_1_, ...), custom_call_target="tpu_custom_call" | custom-call | tf_op jit(solution)/shard_map/join_and_gram/pallas_call | solution.py:148
  28.1 0.1 collective-permute-start.7
  28.1 1.2 %collective-permute-done.7 = f32[64,128]{1,0:T(8,128)S(1)} collective-permute-done((f32[64,128]{1,0:T(8,128)S(1)}, f32[64,128]{1,0:T(8,128)S(1)}, u32[]{:S(2)}, u32[]{:S(2)}) %collective-permute-start.7) | collective-permute-done | bytes 32800 | tf_op jit(solution)/shard_map/ppermute | solution.py:180
  29.3 1.2 %collective-permute-start.10 = (f32[64,128]{1,0:T(8,128)S(1)}, f32[64,128]{1,0:T(8,128)S(1)}, u32[]{:S(2)}, u32[]{:S(2)}) collective-permute-start(f32[64,128]{1,0:T(8,128)S(1)} %add.12), channel_id=1, source_target_pairs={{0,25},{1,24},{2,27},{3,26},{4,29},{5,28},{6,31},{7,30},{8,17},{9,... | collective-permute-start | bytes 98312 | tf_op jit(solution)/shard_map/ppermute | solution.py:180
  30.6 1.5 %collective-permute-start.9 = (f32[64,128]{1,0:T(8,128)S(1)}, f32[64,128]{1,0:T(8,128)S(1)}, u32[]{:S(2)}, u32[]{:S(2)}) collective-permute-start(f32[64,128]{1,0:T(8,128)S(1)} %add.12), channel_id=1, source_target_pairs={{0,9},{1,8},{2,11},{3,10},{4,13},{5,12},{6,15},{7,14},{8,1},{9,0},... | collective-permute-start | bytes 98312 | tf_op jit(solution)/shard_map/ppermute | solution.py:180
  32.0 0.3 collective-permute-start.8
  32.3 1.3 %collective-permute-done.10 = f32[64,128]{1,0:T(8,128)S(1)} collective-permute-done((f32[64,128]{1,0:T(8,128)S(1)}, f32[64,128]{1,0:T(8,128)S(1)}, u32[]{:S(2)}, u32[]{:S(2)}) %collective-permute-start.10) | collective-permute-done | bytes 32800 | tf_op jit(solution)/shard_map/ppermute | solution.py:180
  33.6 0.9 %collective-permute-done.9 = f32[64,128]{1,0:T(8,128)S(1)} collective-permute-done((f32[64,128]{1,0:T(8,128)S(1)}, f32[64,128]{1,0:T(8,128)S(1)}, u32[]{:S(2)}, u32[]{:S(2)}) %collective-permute-start.9) | collective-permute-done | bytes 32800 | tf_op jit(solution)/shard_map/ppermute | solution.py:180
  34.5 0.9 %collective-permute-done.8 = f32[64,128]{1,0:T(8,128)S(1)} collective-permute-done((f32[64,128]{1,0:T(8,128)S(1)}, f32[64,128]{1,0:T(8,128)S(1)}, u32[]{:S(2)}, u32[]{:S(2)}) %collective-permute-start.8) | collective-permute-done | bytes 32800 | tf_op jit(solution)/shard_map/ppermute | solution.py:180
  35.4 1.9 %collective-permute-start.13 = (f32[64,128]{1,0:T(8,128)S(1)}, f32[64,128]{1,0:T(8,128)S(1)}, u32[]{:S(2)}, u32[]{:S(2)}) collective-permute-start(f32[64,128]{1,0:T(8,128)S(1)} %add_add_fusion.refs_0_), channel_id=1, source_target_pairs={{0,14},{1,15},{2,12},{3,13},{4,10},{5,11},{6,8},{7,9},{8,6},{9,7},... | collective-permute-start | bytes 98312 | tf_op jit(solution)/shard_map/ppermute | solution.py:180
  37.3 0.7 %collective-permute-start.12 = (f32[64,128]{1,0:T(8,128)S(1)}, f32[64,128]{1,0:T(8,128)S(1)}, u32[]{:S(2)}, u32[]{:S(2)}) collective-permute-start(f32[64,128]{1,0:T(8,128)S(1)} %add_add_fusion.refs_0_), channel_id=1, source_target_pairs={{0,12},{1,13},{2,14},{3,15},{4,8},{5,9},{6,10},{7,11},{8,4},{9,5},... | collective-permute-start | bytes 98312 | tf_op jit(solution)/shard_map/ppermute | solution.py:180
  38.0 1.3 %collective-permute-start.11 = (f32[64,128]{1,0:T(8,128)S(1)}, f32[64,128]{1,0:T(8,128)S(1)}, u32[]{:S(2)}, u32[]{:S(2)}) collective-permute-start(f32[64,128]{1,0:T(8,128)S(1)} %add_add_fusion.refs_0_), channel_id=1, source_target_pairs={{0,10},{1,11},{2,8},{3,9},{4,14},{5,15},{6,12},{7,13},{8,2},{9,3},... | collective-permute-start | bytes 98312 | tf_op jit(solution)/shard_map/ppermute | solution.py:180
  39.3 1.3 %collective-permute-done.13.refs_3_ = f32[64,128]{1,0:T(8,128)S(1)} collective-permute-done((f32[64,128]{1,0:T(8,128)S(1)}, f32[64,128]{1,0:T(8,128)S(1)}, u32[]{:S(2)}, u32[]{:S(2)}) %collective-permute-start.13) | collective-permute-done | bytes 32800 | tf_op jit(solution)/shard_map/ppermute | solution.py:180
  40.6 1.1 %collective-permute-done.12.refs_2_ = f32[64,128]{1,0:T(8,128)S(1)} collective-permute-done((f32[64,128]{1,0:T(8,128)S(1)}, f32[64,128]{1,0:T(8,128)S(1)}, u32[]{:S(2)}, u32[]{:S(2)}) %collective-permute-start.12) | collective-permute-done | bytes 32800 | tf_op jit(solution)/shard_map/ppermute | solution.py:180
  41.7 0.1 collective-permute-done.11.refs_1_
  41.7 2.9 %whiten.1 = (f32[2,64,64]{2,1,0:T(8,128)}, f32[2,64,2048]{2,1,0:T(8,128)}) custom-call(f32[64,128]{1,0:T(8,128)S(1)} %add_add_fusion.refs_0_, f32[64,128]{1,0:T(8,128)S(1)} %collective-permute-done.11.refs_1_, f32[64,128]{1,0:T(8,128)S(1)} %collective-permute-done.12.refs_2_, f32[64,128]{1,0:T(8,128)S(1)} %collective-permute-done.13.refs_3_, ...), custom_call_target="tpu_custom_call" | custom-call | tf_op jit(solution)/shard_map/whiten/pallas_call | solution.py:327
  (2 shorter events, 0.0 us)
Async XLA Ops:
  7.7 9.1 %collective-permute-start = (bf16[16,2560]{1,0:T(8,128)(2,1)S(1)}, bf16[16,2560]{1,0:T(8,128)(2,1)S(1)}, u32[]{:S(2)}, u32[]{:S(2)}) collective-permute-start(bf16[16,2560]{1,0:T(8,128)(2,1)S(1)} %get-tuple-element.14), channel_id=1, source_target_pairs={{0,4},{1,5},{2,6},{3,7},{4,0},{5,1},{6,2},{7,3},{8,12},{9,13},{10,... | collective-permute-start | bytes 245768 | tf_op jit(solution)/shard_map/ppermute | solution.py:355
  11.9 8.4 %collective-permute-start.1 = (bf16[16,2560]{1,0:T(8,128)(2,1)S(1)}, bf16[16,2560]{1,0:T(8,128)(2,1)S(1)}, u32[]{:S(2)}, u32[]{:S(2)}) collective-permute-start(bf16[16,2560]{1,0:T(8,128)(2,1)S(1)} %get-tuple-element.15), channel_id=1, source_target_pairs={{0,2},{1,3},{2,0},{3,1},{4,6},{5,7},{6,4},{7,5},{8,10},{9,11},{10,... | collective-permute-start | bytes 245768 | tf_op jit(solution)/shard_map/ppermute | solution.py:355
  13.4 8.1 %collective-permute-start.2 = (bf16[16,2560]{1,0:T(8,128)(2,1)S(1)}, bf16[16,2560]{1,0:T(8,128)(2,1)S(1)}, u32[]{:S(2)}, u32[]{:S(2)}) collective-permute-start(bf16[16,2560]{1,0:T(8,128)(2,1)S(1)} %get-tuple-element.16), channel_id=1, source_target_pairs={{0,6},{1,7},{2,4},{3,5},{4,2},{5,3},{6,0},{7,1},{8,14},{9,15},{10,... | collective-permute-start | bytes 245768 | tf_op jit(solution)/shard_map/ppermute | solution.py:355
  13.4 8.1 %collective-permute-start.3 = (bf16[16,2560]{1,0:T(8,128)(2,1)S(1)}, bf16[16,2560]{1,0:T(8,128)(2,1)S(1)}, u32[]{:S(2)}, u32[]{:S(2)}) collective-permute-start(bf16[16,2560]{1,0:T(8,128)(2,1)S(1)} %get-tuple-element.17), channel_id=1, source_target_pairs={{0,1},{1,0},{2,3},{3,2},{4,5},{5,4},{6,7},{7,6},{8,9},{9,8},{10,11... | collective-permute-start | bytes 245768 | tf_op jit(solution)/shard_map/ppermute | solution.py:355
  15.2 10.6 %collective-permute-start.4 = (bf16[16,2560]{1,0:T(8,128)(2,1)S(1)}, bf16[16,2560]{1,0:T(8,128)(2,1)S(1)}, u32[]{:S(2)}, u32[]{:S(2)}) collective-permute-start(bf16[16,2560]{1,0:T(8,128)(2,1)S(1)} %get-tuple-element.18), channel_id=1, source_target_pairs={{0,5},{1,4},{2,7},{3,6},{4,1},{5,0},{6,3},{7,2},{8,13},{9,12},{10,... | collective-permute-start | bytes 245768 | tf_op jit(solution)/shard_map/ppermute | solution.py:355
  16.8 8.9 %collective-permute-start.5 = (bf16[16,2560]{1,0:T(8,128)(2,1)S(1)}, bf16[16,2560]{1,0:T(8,128)(2,1)S(1)}, u32[]{:S(2)}, u32[]{:S(2)}) collective-permute-start(bf16[16,2560]{1,0:T(8,128)(2,1)S(1)} %get-tuple-element.19), channel_id=1, source_target_pairs={{0,3},{1,2},{2,1},{3,0},{4,7},{5,6},{6,5},{7,4},{8,11},{9,10},{10,... | collective-permute-start | bytes 245768 | tf_op jit(solution)/shard_map/ppermute | solution.py:355
  20.3 7.2 %collective-permute-start.6 = (bf16[16,2560]{1,0:T(8,128)(2,1)S(1)}, bf16[16,2560]{1,0:T(8,128)(2,1)S(1)}, u32[]{:S(2)}, u32[]{:S(2)}) collective-permute-start(bf16[16,2560]{1,0:T(8,128)(2,1)S(1)} %get-tuple-element.20), channel_id=1, source_target_pairs={{0,7},{1,6},{2,5},{3,4},{4,3},{5,2},{6,1},{7,0},{8,15},{9,14},{10,... | collective-permute-start | bytes 245768 | tf_op jit(solution)/shard_map/ppermute | solution.py:355
  28.1 1.3 %collective-permute-start.7 = (f32[64,128]{1,0:T(8,128)S(1)}, f32[64,128]{1,0:T(8,128)S(1)}, u32[]{:S(2)}, u32[]{:S(2)}) collective-permute-start(f32[64,128]{1,0:T(8,128)S(1)} %get-tuple-element.22), channel_id=1, source_target_pairs={{0,8},{1,9},{2,10},{3,11},{4,12},{5,13},{6,14},{7,15},{8,0},{9,1},... | collective-permute-start | bytes 98312 | tf_op jit(solution)/shard_map/ppermute | solution.py:180
  29.3 4.2 %collective-permute-start.10 = (f32[64,128]{1,0:T(8,128)S(1)}, f32[64,128]{1,0:T(8,128)S(1)}, u32[]{:S(2)}, u32[]{:S(2)}) collective-permute-start(f32[64,128]{1,0:T(8,128)S(1)} %add.12), channel_id=1, source_target_pairs={{0,25},{1,24},{2,27},{3,26},{4,29},{5,28},{6,31},{7,30},{8,17},{9,... | collective-permute-start | bytes 98312 | tf_op jit(solution)/shard_map/ppermute | solution.py:180
  30.6 4.0 %collective-permute-start.9 = (f32[64,128]{1,0:T(8,128)S(1)}, f32[64,128]{1,0:T(8,128)S(1)}, u32[]{:S(2)}, u32[]{:S(2)}) collective-permute-start(f32[64,128]{1,0:T(8,128)S(1)} %add.12), channel_id=1, source_target_pairs={{0,9},{1,8},{2,11},{3,10},{4,13},{5,12},{6,15},{7,14},{8,1},{9,0},... | collective-permute-start | bytes 98312 | tf_op jit(solution)/shard_map/ppermute | solution.py:180
  32.0 3.3 %collective-permute-start.8 = (f32[64,128]{1,0:T(8,128)S(1)}, f32[64,128]{1,0:T(8,128)S(1)}, u32[]{:S(2)}, u32[]{:S(2)}) collective-permute-start(f32[64,128]{1,0:T(8,128)S(1)} %add.12), channel_id=1, source_target_pairs={{0,24},{1,25},{2,26},{3,27},{4,28},{5,29},{6,30},{7,31},{8,16},{9,... | collective-permute-start | bytes 98312 | tf_op jit(solution)/shard_map/ppermute | solution.py:180
  35.4 5.2 %collective-permute-start.13 = (f32[64,128]{1,0:T(8,128)S(1)}, f32[64,128]{1,0:T(8,128)S(1)}, u32[]{:S(2)}, u32[]{:S(2)}) collective-permute-start(f32[64,128]{1,0:T(8,128)S(1)} %add_add_fusion.refs_0_), channel_id=1, source_target_pairs={{0,14},{1,15},{2,12},{3,13},{4,10},{5,11},{6,8},{7,9},{8,6},{9,7},... | collective-permute-start | bytes 98312 | tf_op jit(solution)/shard_map/ppermute | solution.py:180
  37.3 4.3 %collective-permute-start.12 = (f32[64,128]{1,0:T(8,128)S(1)}, f32[64,128]{1,0:T(8,128)S(1)}, u32[]{:S(2)}, u32[]{:S(2)}) collective-permute-start(f32[64,128]{1,0:T(8,128)S(1)} %add_add_fusion.refs_0_), channel_id=1, source_target_pairs={{0,12},{1,13},{2,14},{3,15},{4,8},{5,9},{6,10},{7,11},{8,4},{9,5},... | collective-permute-start | bytes 98312 | tf_op jit(solution)/shard_map/ppermute | solution.py:180
  38.0 3.7 %collective-permute-start.11 = (f32[64,128]{1,0:T(8,128)S(1)}, f32[64,128]{1,0:T(8,128)S(1)}, u32[]{:S(2)}, u32[]{:S(2)}) collective-permute-start(f32[64,128]{1,0:T(8,128)S(1)} %add_add_fusion.refs_0_), channel_id=1, source_target_pairs={{0,10},{1,11},{2,8},{3,9},{4,14},{5,15},{6,12},{7,13},{8,2},{9,3},... | collective-permute-start | bytes 98312 | tf_op jit(solution)/shard_map/ppermute | solution.py:180

commit v5 on v4

--- a/solution.py
+++ b/solution.py
@@ -161,10 +161,18 @@
     return pltpu.with_memory_space_constraint(value, pltpu.VMEM)
 
 
+def reversed_bits(count):
+    bits = (count - 1).bit_length()
+    return [int(f"{k:0{bits}b}"[::-1], 2) for k in range(1, count)] + [0]
+
+
 def spread_order(shards):
-    bits = (shards - 1).bit_length()
-    order = [int(f"{k:0{bits}b}"[::-1], 2) for k in range(1, shards)]
-    return order + [0]
+    half = shards // 2
+    far = [half + k for k in reversed_bits(half)]
+    order = []
+    for k in range(half):
+        order += [far[k], (k + 1) % half]
+    return order
 
 
 GRID = ("space", "tm")

time: 45.2 us -> 44.6 us (0.987)
    ppermute x7, waiting for transfers between devices: 5.97 us -> 5.15 us  [on_device(): received.append(lax.ppermute(part, 'tm', pairs) if shift else part)]
    ppermute x7, waiting for transfers between devices: 6.62 us -> 7.1 us  [swapped(): return lax.ppermute(value, GRID, pairs)]
  transfers between devices with their start and end apart: 14 -> 14, of which waited for: 9 -> 10; matrix products, arithmetic and copies ran while one was open for 0% -> 0% of each run, Pallas kernels for 0% -> 0%
where the time goes in v5:
time: 44.6 us; the launch traced here: 44.4 us
  starting transfers between devices  20.9 us (47%)
  waiting for transfers between devices  12.3 us (28%)
  Pallas kernels  10.6 us (24%)
  between operations  0.68 us (2%)
    ppermute x7, starting transfers between devices, on_device(): received.append(lax.ppermute(part, 'tm', pairs) if shift else part)  13.9 us
    ppermute x7, waiting for transfers between devices, swapped(): return lax.ppermute(value, GRID, pairs)  7.1 us
    pallas_call x1, Pallas kernels, block_sums(): pl.pallas_call(body, in_specs=[smem, smem, pl.BlockSpec(memory_space=pl.A...  7.09 us
    ppermute x7, starting transfers between devices, swapped(): return lax.ppermute(value, GRID, pairs)  6.99 us
    ppermute x7, waiting for transfers between devices, on_device(): received.append(lax.ppermute(part, 'tm', pairs) if shift else part)  5.15 us
    pallas_call x1, Pallas kernels, whiten(): pl.pallas_call(body, in_specs=[pl.BlockSpec(memory_space=pltpu.VMEM)] * (...  2.93 us
  transfers between devices with their start and end apart: 14, of which 10 were waited for; matrix products, arithmetic and copies ran while one was open for 0% of the time, Pallas kernels for 0%

profile of v5, /device:TPU:0, one launch (start us, length us, event | category | flops | bytes accessed | tf_op | source)
XLA Modules:
  0.0 44.4 jit_solution(13409106844718157779)
XLA Ops:
  0.6 7.1 %block_sums.1 = (bf16[16,2560]{1,0:T(8,128)(2,1)S(1)}, bf16[16,2560]{1,0:T(8,128)(2,1)S(1)}, bf16[16,2560]{1,0:T(8,128)(2,1)S(1)}, bf16[16,2560]{1,0:T(8,128)(2,...) custom-call(s32[2]{0:T(128)} %freq_ref.1, ...), custom_call_target="tpu_custom_call" | custom-call | tf_op jit(solution)/shard_map/block_sums/pallas_call | solution.py:88
  7.7 5.1 %collective-permute-start = (bf16[16,2560]{1,0:T(8,128)(2,1)S(1)}, bf16[16,2560]{1,0:T(8,128)(2,1)S(1)}, u32[]{:S(2)}, u32[]{:S(2)}) collective-permute-start(bf16[16,2560]{1,0:T(8,128)(2,1)S(1)} %get-tuple-element.14), channel_id=1, source_target_pairs={{0,6},{1,7},{2,4},{3,5},{4,2},{5,3},{6,0},{7,1},{8,14},{9,15},{10,... | collective-permute-start | bytes 245768 | tf_op jit(solution)/shard_map/ppermute | solution.py:363
  12.9 1.5 %collective-permute-start.1 = (bf16[16,2560]{1,0:T(8,128)(2,1)S(1)}, bf16[16,2560]{1,0:T(8,128)(2,1)S(1)}, u32[]{:S(2)}, u32[]{:S(2)}) collective-permute-start(bf16[16,2560]{1,0:T(8,128)(2,1)S(1)} %get-tuple-element.15), channel_id=1, source_target_pairs={{0,1},{1,0},{2,3},{3,2},{4,5},{5,4},{6,7},{7,6},{8,9},{9,8},{10,11... | collective-permute-start | bytes 245768 | tf_op jit(solution)/shard_map/ppermute | solution.py:363
  14.4 0.0 collective-permute-start.2
  14.4 0.6 %collective-permute-start.3 = (bf16[16,2560]{1,0:T(8,128)(2,1)S(1)}, bf16[16,2560]{1,0:T(8,128)(2,1)S(1)}, u32[]{:S(2)}, u32[]{:S(2)}) collective-permute-start(bf16[16,2560]{1,0:T(8,128)(2,1)S(1)} %get-tuple-element.17), channel_id=1, source_target_pairs={{0,2},{1,3},{2,0},{3,1},{4,6},{5,7},{6,4},{7,5},{8,10},{9,11},{10,... | collective-permute-start | bytes 245768 | tf_op jit(solution)/shard_map/ppermute | solution.py:363
  15.0 4.7 %collective-permute-start.4 = (bf16[16,2560]{1,0:T(8,128)(2,1)S(1)}, bf16[16,2560]{1,0:T(8,128)(2,1)S(1)}, u32[]{:S(2)}, u32[]{:S(2)}) collective-permute-start(bf16[16,2560]{1,0:T(8,128)(2,1)S(1)} %get-tuple-element.18), channel_id=1, source_target_pairs={{0,7},{1,6},{2,5},{3,4},{4,3},{5,2},{6,1},{7,0},{8,15},{9,14},{10,... | collective-permute-start | bytes 245768 | tf_op jit(solution)/shard_map/ppermute | solution.py:363
  19.7 0.0 collective-permute-done.refs_0_
  19.7 0.0 collective-permute-start.5
  19.7 0.0 collective-permute-done.1.refs_1_
  19.7 1.9 %collective-permute-start.6 = (bf16[16,2560]{1,0:T(8,128)(2,1)S(1)}, bf16[16,2560]{1,0:T(8,128)(2,1)S(1)}, u32[]{:S(2)}, u32[]{:S(2)}) collective-permute-start(bf16[16,2560]{1,0:T(8,128)(2,1)S(1)} %get-tuple-element.20), channel_id=1, source_target_pairs={{0,4},{1,5},{2,6},{3,7},{4,0},{5,1},{6,2},{7,3},{8,12},{9,13},{10,... | collective-permute-start | bytes 245768 | tf_op jit(solution)/shard_map/ppermute | solution.py:363
  21.6 1.0 %collective-permute-done.2.refs_2_ = bf16[16,2560]{1,0:T(8,128)(2,1)S(1)} collective-permute-done((bf16[16,2560]{1,0:T(8,128)(2,1)S(1)}, bf16[16,2560]{1,0:T(8,128)(2,1)S(1)}, u32[]{:S(2)}, u32[]{:S(2)}) %collective-permute-start.2) | collective-permute-done | bytes 81952 | tf_op jit(solution)/shard_map/ppermute | solution.py:363
  22.6 0.0 collective-permute-done.3.refs_3_
  22.6 1.8 %collective-permute-done.4.refs_4_ = bf16[16,2560]{1,0:T(8,128)(2,1)S(1)} collective-permute-done((bf16[16,2560]{1,0:T(8,128)(2,1)S(1)}, bf16[16,2560]{1,0:T(8,128)(2,1)S(1)}, u32[]{:S(2)}, u32[]{:S(2)}) %collective-permute-start.4) | collective-permute-done | bytes 81952 | tf_op jit(solution)/shard_map/ppermute | solution.py:363
  24.4 1.0 %collective-permute-done.5.refs_5_ = bf16[16,2560]{1,0:T(8,128)(2,1)S(1)} collective-permute-done((bf16[16,2560]{1,0:T(8,128)(2,1)S(1)}, bf16[16,2560]{1,0:T(8,128)(2,1)S(1)}, u32[]{:S(2)}, u32[]{:S(2)}) %collective-permute-start.5) | collective-permute-done | bytes 81952 | tf_op jit(solution)/shard_map/ppermute | solution.py:363
  25.4 1.4 %collective-permute-done.6.refs_6_ = bf16[16,2560]{1,0:T(8,128)(2,1)S(1)} collective-permute-done((bf16[16,2560]{1,0:T(8,128)(2,1)S(1)}, bf16[16,2560]{1,0:T(8,128)(2,1)S(1)}, u32[]{:S(2)}, u32[]{:S(2)}) %collective-permute-start.6) | collective-permute-done | bytes 81952 | tf_op jit(solution)/shard_map/ppermute | solution.py:363
  26.8 0.6 %join_and_gram.1 = (bf16[128,2048]{1,0:T(8,128)(2,1)S(1)}, f32[64,128]{1,0:T(8,128)S(1)}) custom-call(bf16[4,128,256]{2,1,0:T(8,128)(2,1)S(1)} %get-tuple-element.13.join_ref, bf16[16,2560]{1,0:T(8,128)(2,1)S(1)} %collective-permute-done.refs_0_, bf16[16,2560]{1,0:T(8,128)(2,1)S(1)} %collective-permute-done.1.refs_1_, ...), custom_call_target="tpu_custom_call" | custom-call | tf_op jit(solution)/shard_map/join_and_gram/pallas_call | solution.py:148
  27.3 0.1 collective-permute-start.7
  27.4 1.2 %collective-permute-done.7 = f32[64,128]{1,0:T(8,128)S(1)} collective-permute-done((f32[64,128]{1,0:T(8,128)S(1)}, f32[64,128]{1,0:T(8,128)S(1)}, u32[]{:S(2)}, u32[]{:S(2)}) %collective-permute-start.7) | collective-permute-done | bytes 32800 | tf_op jit(solution)/shard_map/ppermute | solution.py:188
  28.6 2.2 %collective-permute-start.10 = (f32[64,128]{1,0:T(8,128)S(1)}, f32[64,128]{1,0:T(8,128)S(1)}, u32[]{:S(2)}, u32[]{:S(2)}) collective-permute-start(f32[64,128]{1,0:T(8,128)S(1)} %add.12), channel_id=1, source_target_pairs={{0,25},{1,24},{2,27},{3,26},{4,29},{5,28},{6,31},{7,30},{8,17},{9,... | collective-permute-start | bytes 98312 | tf_op jit(solution)/shard_map/ppermute | solution.py:188
  30.8 0.5 %collective-permute-start.9 = (f32[64,128]{1,0:T(8,128)S(1)}, f32[64,128]{1,0:T(8,128)S(1)}, u32[]{:S(2)}, u32[]{:S(2)}) collective-permute-start(f32[64,128]{1,0:T(8,128)S(1)} %add.12), channel_id=1, source_target_pairs={{0,9},{1,8},{2,11},{3,10},{4,13},{5,12},{6,15},{7,14},{8,1},{9,0},... | collective-permute-start | bytes 98312 | tf_op jit(solution)/shard_map/ppermute | solution.py:188
  31.3 0.3 collective-permute-start.8
  31.6 1.3 %collective-permute-done.10 = f32[64,128]{1,0:T(8,128)S(1)} collective-permute-done((f32[64,128]{1,0:T(8,128)S(1)}, f32[64,128]{1,0:T(8,128)S(1)}, u32[]{:S(2)}, u32[]{:S(2)}) %collective-permute-start.10) | collective-permute-done | bytes 32800 | tf_op jit(solution)/shard_map/ppermute | solution.py:188
  32.9 1.3 %collective-permute-done.9 = f32[64,128]{1,0:T(8,128)S(1)} collective-permute-done((f32[64,128]{1,0:T(8,128)S(1)}, f32[64,128]{1,0:T(8,128)S(1)}, u32[]{:S(2)}, u32[]{:S(2)}) %collective-permute-start.9) | collective-permute-done | bytes 32800 | tf_op jit(solution)/shard_map/ppermute | solution.py:188
  34.2 0.5 %collective-permute-done.8 = f32[64,128]{1,0:T(8,128)S(1)} collective-permute-done((f32[64,128]{1,0:T(8,128)S(1)}, f32[64,128]{1,0:T(8,128)S(1)}, u32[]{:S(2)}, u32[]{:S(2)}) %collective-permute-start.8) | collective-permute-done | bytes 32800 | tf_op jit(solution)/shard_map/ppermute | solution.py:188
  34.7 2.6 %collective-permute-start.13 = (f32[64,128]{1,0:T(8,128)S(1)}, f32[64,128]{1,0:T(8,128)S(1)}, u32[]{:S(2)}, u32[]{:S(2)}) collective-permute-start(f32[64,128]{1,0:T(8,128)S(1)} %add_add_fusion.refs_0_), channel_id=1, source_target_pairs={{0,14},{1,15},{2,12},{3,13},{4,10},{5,11},{6,8},{7,9},{8,6},{9,7},... | collective-permute-start | bytes 98312 | tf_op jit(solution)/shard_map/ppermute | solution.py:188
  37.2 0.0 collective-permute-start.12
  37.2 1.4 %collective-permute-start.11 = (f32[64,128]{1,0:T(8,128)S(1)}, f32[64,128]{1,0:T(8,128)S(1)}, u32[]{:S(2)}, u32[]{:S(2)}) collective-permute-start(f32[64,128]{1,0:T(8,128)S(1)} %add_add_fusion.refs_0_), channel_id=1, source_target_pairs={{0,10},{1,11},{2,8},{3,9},{4,14},{5,15},{6,12},{7,13},{8,2},{9,3},... | collective-permute-start | bytes 98312 | tf_op jit(solution)/shard_map/ppermute | solution.py:188
  38.6 1.3 %collective-permute-done.13.refs_3_ = f32[64,128]{1,0:T(8,128)S(1)} collective-permute-done((f32[64,128]{1,0:T(8,128)S(1)}, f32[64,128]{1,0:T(8,128)S(1)}, u32[]{:S(2)}, u32[]{:S(2)}) %collective-permute-start.13) | collective-permute-done | bytes 32800 | tf_op jit(solution)/shard_map/ppermute | solution.py:188
  39.9 1.6 %collective-permute-done.12.refs_2_ = f32[64,128]{1,0:T(8,128)S(1)} collective-permute-done((f32[64,128]{1,0:T(8,128)S(1)}, f32[64,128]{1,0:T(8,128)S(1)}, u32[]{:S(2)}, u32[]{:S(2)}) %collective-permute-start.12) | collective-permute-done | bytes 32800 | tf_op jit(solution)/shard_map/ppermute | solution.py:188
  41.5 0.0 collective-permute-done.11.refs_1_
  41.5 2.9 %whiten.1 = (f32[2,64,64]{2,1,0:T(8,128)}, f32[2,64,2048]{2,1,0:T(8,128)}) custom-call(f32[64,128]{1,0:T(8,128)S(1)} %add_add_fusion.refs_0_, f32[64,128]{1,0:T(8,128)S(1)} %collective-permute-done.11.refs_1_, f32[64,128]{1,0:T(8,128)S(1)} %collective-permute-done.12.refs_2_, f32[64,128]{1,0:T(8,128)S(1)} %collective-permute-done.13.refs_3_, ...), custom_call_target="tpu_custom_call" | custom-call | tf_op jit(solution)/shard_map/whiten/pallas_call | solution.py:335
  (2 shorter events, 0.0 us)
Async XLA Ops:
  7.7 12.0 %collective-permute-start = (bf16[16,2560]{1,0:T(8,128)(2,1)S(1)}, bf16[16,2560]{1,0:T(8,128)(2,1)S(1)}, u32[]{:S(2)}, u32[]{:S(2)}) collective-permute-start(bf16[16,2560]{1,0:T(8,128)(2,1)S(1)} %get-tuple-element.14), channel_id=1, source_target_pairs={{0,6},{1,7},{2,4},{3,5},{4,2},{5,3},{6,0},{7,1},{8,14},{9,15},{10,... | collective-permute-start | bytes 245768 | tf_op jit(solution)/shard_map/ppermute | solution.py:363
  12.9 6.8 %collective-permute-start.1 = (bf16[16,2560]{1,0:T(8,128)(2,1)S(1)}, bf16[16,2560]{1,0:T(8,128)(2,1)S(1)}, u32[]{:S(2)}, u32[]{:S(2)}) collective-permute-start(bf16[16,2560]{1,0:T(8,128)(2,1)S(1)} %get-tuple-element.15), channel_id=1, source_target_pairs={{0,1},{1,0},{2,3},{3,2},{4,5},{5,4},{6,7},{7,6},{8,9},{9,8},{10,11... | collective-permute-start | bytes 245768 | tf_op jit(solution)/shard_map/ppermute | solution.py:363
  14.4 8.2 %collective-permute-start.2 = (bf16[16,2560]{1,0:T(8,128)(2,1)S(1)}, bf16[16,2560]{1,0:T(8,128)(2,1)S(1)}, u32[]{:S(2)}, u32[]{:S(2)}) collective-permute-start(bf16[16,2560]{1,0:T(8,128)(2,1)S(1)} %get-tuple-element.16), channel_id=1, source_target_pairs={{0,5},{1,4},{2,7},{3,6},{4,1},{5,0},{6,3},{7,2},{8,13},{9,12},{10,... | collective-permute-start | bytes 245768 | tf_op jit(solution)/shard_map/ppermute | solution.py:363
  14.4 8.2 %collective-permute-start.3 = (bf16[16,2560]{1,0:T(8,128)(2,1)S(1)}, bf16[16,2560]{1,0:T(8,128)(2,1)S(1)}, u32[]{:S(2)}, u32[]{:S(2)}) collective-permute-start(bf16[16,2560]{1,0:T(8,128)(2,1)S(1)} %get-tuple-element.17), channel_id=1, source_target_pairs={{0,2},{1,3},{2,0},{3,1},{4,6},{5,7},{6,4},{7,5},{8,10},{9,11},{10,... | collective-permute-start | bytes 245768 | tf_op jit(solution)/shard_map/ppermute | solution.py:363
  15.0 9.4 %collective-permute-start.4 = (bf16[16,2560]{1,0:T(8,128)(2,1)S(1)}, bf16[16,2560]{1,0:T(8,128)(2,1)S(1)}, u32[]{:S(2)}, u32[]{:S(2)}) collective-permute-start(bf16[16,2560]{1,0:T(8,128)(2,1)S(1)} %get-tuple-element.18), channel_id=1, source_target_pairs={{0,7},{1,6},{2,5},{3,4},{4,3},{5,2},{6,1},{7,0},{8,15},{9,14},{10,... | collective-permute-start | bytes 245768 | tf_op jit(solution)/shard_map/ppermute | solution.py:363
  19.7 5.7 %collective-permute-start.5 = (bf16[16,2560]{1,0:T(8,128)(2,1)S(1)}, bf16[16,2560]{1,0:T(8,128)(2,1)S(1)}, u32[]{:S(2)}, u32[]{:S(2)}) collective-permute-start(bf16[16,2560]{1,0:T(8,128)(2,1)S(1)} %get-tuple-element.19), channel_id=1, source_target_pairs={{0,3},{1,2},{2,1},{3,0},{4,7},{5,6},{6,5},{7,4},{8,11},{9,10},{10,... | collective-permute-start | bytes 245768 | tf_op jit(solution)/shard_map/ppermute | solution.py:363
  19.7 7.1 %collective-permute-start.6 = (bf16[16,2560]{1,0:T(8,128)(2,1)S(1)}, bf16[16,2560]{1,0:T(8,128)(2,1)S(1)}, u32[]{:S(2)}, u32[]{:S(2)}) collective-permute-start(bf16[16,2560]{1,0:T(8,128)(2,1)S(1)} %get-tuple-element.20), channel_id=1, source_target_pairs={{0,4},{1,5},{2,6},{3,7},{4,0},{5,1},{6,2},{7,3},{8,12},{9,13},{10,... | collective-permute-start | bytes 245768 | tf_op jit(solution)/shard_map/ppermute | solution.py:363
  27.3 1.3 %collective-permute-start.7 = (f32[64,128]{1,0:T(8,128)S(1)}, f32[64,128]{1,0:T(8,128)S(1)}, u32[]{:S(2)}, u32[]{:S(2)}) collective-permute-start(f32[64,128]{1,0:T(8,128)S(1)} %get-tuple-element.22), channel_id=1, source_target_pairs={{0,8},{1,9},{2,10},{3,11},{4,12},{5,13},{6,14},{7,15},{8,0},{9,1},... | collective-permute-start | bytes 98312 | tf_op jit(solution)/shard_map/ppermute | solution.py:188
  28.6 4.2 %collective-permute-start.10 = (f32[64,128]{1,0:T(8,128)S(1)}, f32[64,128]{1,0:T(8,128)S(1)}, u32[]{:S(2)}, u32[]{:S(2)}) collective-permute-start(f32[64,128]{1,0:T(8,128)S(1)} %add.12), channel_id=1, source_target_pairs={{0,25},{1,24},{2,27},{3,26},{4,29},{5,28},{6,31},{7,30},{8,17},{9,... | collective-permute-start | bytes 98312 | tf_op jit(solution)/shard_map/ppermute | solution.py:188
  30.8 3.3 %collective-permute-start.9 = (f32[64,128]{1,0:T(8,128)S(1)}, f32[64,128]{1,0:T(8,128)S(1)}, u32[]{:S(2)}, u32[]{:S(2)}) collective-permute-start(f32[64,128]{1,0:T(8,128)S(1)} %add.12), channel_id=1, source_target_pairs={{0,9},{1,8},{2,11},{3,10},{4,13},{5,12},{6,15},{7,14},{8,1},{9,0},... | collective-permute-start | bytes 98312 | tf_op jit(solution)/shard_map/ppermute | solution.py:188
  31.3 3.3 %collective-permute-start.8 = (f32[64,128]{1,0:T(8,128)S(1)}, f32[64,128]{1,0:T(8,128)S(1)}, u32[]{:S(2)}, u32[]{:S(2)}) collective-permute-start(f32[64,128]{1,0:T(8,128)S(1)} %add.12), channel_id=1, source_target_pairs={{0,24},{1,25},{2,26},{3,27},{4,28},{5,29},{6,30},{7,31},{8,16},{9,... | collective-permute-start | bytes 98312 | tf_op jit(solution)/shard_map/ppermute | solution.py:188
  34.7 5.2 %collective-permute-start.13 = (f32[64,128]{1,0:T(8,128)S(1)}, f32[64,128]{1,0:T(8,128)S(1)}, u32[]{:S(2)}, u32[]{:S(2)}) collective-permute-start(f32[64,128]{1,0:T(8,128)S(1)} %add_add_fusion.refs_0_), channel_id=1, source_target_pairs={{0,14},{1,15},{2,12},{3,13},{4,10},{5,11},{6,8},{7,9},{8,6},{9,7},... | collective-permute-start | bytes 98312 | tf_op jit(solution)/shard_map/ppermute | solution.py:188
  37.2 4.2 %collective-permute-start.12 = (f32[64,128]{1,0:T(8,128)S(1)}, f32[64,128]{1,0:T(8,128)S(1)}, u32[]{:S(2)}, u32[]{:S(2)}) collective-permute-start(f32[64,128]{1,0:T(8,128)S(1)} %add_add_fusion.refs_0_), channel_id=1, source_target_pairs={{0,12},{1,13},{2,14},{3,15},{4,8},{5,9},{6,10},{7,11},{8,4},{9,5},... | collective-permute-start | bytes 98312 | tf_op jit(solution)/shard_map/ppermute | solution.py:188
  37.2 4.2 %collective-permute-start.11 = (f32[64,128]{1,0:T(8,128)S(1)}, f32[64,128]{1,0:T(8,128)S(1)}, u32[]{:S(2)}, u32[]{:S(2)}) collective-permute-start(f32[64,128]{1,0:T(8,128)S(1)} %add_add_fusion.refs_0_), channel_id=1, source_target_pairs={{0,10},{1,11},{2,8},{3,9},{4,14},{5,15},{6,12},{7,13},{8,2},{9,3},... | collective-permute-start | bytes 98312 | tf_op jit(solution)/shard_map/ppermute | solution.py:188

commit v6 on v5

--- a/solution.py
+++ b/solution.py
@@ -195,7 +195,7 @@
     rounds = [[(cross, 0)]]
     while bits:
         (a, b), (c, d) = bits[0], bits[1] if len(bits) > 1 else (0, 0)
-        flips = [(a, b), (c, d), (a + c, b + d)] if len(bits) > 1 else [(a, b)]
+        flips = [(a, b), (a + c, b + d), (c, d)] if len(bits) > 1 else [(a, b)]
         rounds.append([(cross + i, j) for i, j in flips])
         bits = bits[2:]
     return rounds

time: 44.6 us -> 44.3 us (level)
  starting transfers between devices: 20.9 us -> 20 us
  waiting for transfers between devices: 12.3 us -> 12.8 us
    ppermute x7, starting transfers between devices: 6.99 us -> 6.13 us  [swapped(): return lax.ppermute(value, GRID, pairs)]
    ppermute x7, waiting for transfers between devices: 7.1 us -> 7.67 us  [swapped(): return lax.ppermute(value, GRID, pairs)]
  transfers between devices with their start and end apart: 14 -> 14, of which waited for: 10 -> 11; matrix products, arithmetic and copies ran while one was open for 0% -> 0% of each run, Pallas kernels for 0% -> 0%
where the time goes in v6:
time: 44.3 us; the launch traced here: 44.1 us
  starting transfers between devices  20 us (45%)
  waiting for transfers between devices  12.8 us (29%)
  Pallas kernels  10.6 us (24%)
  between operations  0.68 us (2%)
    ppermute x7, starting transfers between devices, on_device(): received.append(lax.ppermute(part, 'tm', pairs) if shift else part)  13.9 us
    ppermute x7, waiting for transfers between devices, swapped(): return lax.ppermute(value, GRID, pairs)  7.67 us
    pallas_call x1, Pallas kernels, block_sums(): pl.pallas_call(body, in_specs=[smem, smem, pl.BlockSpec(memory_space=pl.A...  7.09 us
    ppermute x7, starting transfers between devices, swapped(): return lax.ppermute(value, GRID, pairs)  6.13 us
    ppermute x7, waiting for transfers between devices, on_device(): received.append(lax.ppermute(part, 'tm', pairs) if shift else part)  5.15 us
    pallas_call x1, Pallas kernels, whiten(): pl.pallas_call(body, in_specs=[pl.BlockSpec(memory_space=pltpu.VMEM)] * (...  2.93 us
  transfers between devices with their start and end apart: 14, of which 11 were waited for; matrix products, arithmetic and copies ran while one was open for 0% of the time, Pallas kernels for 0%

profile of v6, /device:TPU:0, one launch (start us, length us, event | category | flops | bytes accessed | tf_op | source)
XLA Modules:
  0.0 44.1 jit_solution(18175896329723016655)
XLA Ops:
  0.6 7.1 %block_sums.1 = (bf16[16,2560]{1,0:T(8,128)(2,1)S(1)}, bf16[16,2560]{1,0:T(8,128)(2,1)S(1)}, bf16[16,2560]{1,0:T(8,128)(2,1)S(1)}, bf16[16,2560]{1,0:T(8,128)(2,...) custom-call(s32[2]{0:T(128)} %freq_ref.1, ...), custom_call_target="tpu_custom_call" | custom-call | tf_op jit(solution)/shard_map/block_sums/pallas_call | solution.py:88
  7.7 5.1 %collective-permute-start = (bf16[16,2560]{1,0:T(8,128)(2,1)S(1)}, bf16[16,2560]{1,0:T(8,128)(2,1)S(1)}, u32[]{:S(2)}, u32[]{:S(2)}) collective-permute-start(bf16[16,2560]{1,0:T(8,128)(2,1)S(1)} %get-tuple-element.14), channel_id=1, source_target_pairs={{0,6},{1,7},{2,4},{3,5},{4,2},{5,3},{6,0},{7,1},{8,14},{9,15},{10,... | collective-permute-start | bytes 245768 | tf_op jit(solution)/shard_map/ppermute | solution.py:363
  12.9 1.5 %collective-permute-start.1 = (bf16[16,2560]{1,0:T(8,128)(2,1)S(1)}, bf16[16,2560]{1,0:T(8,128)(2,1)S(1)}, u32[]{:S(2)}, u32[]{:S(2)}) collective-permute-start(bf16[16,2560]{1,0:T(8,128)(2,1)S(1)} %get-tuple-element.15), channel_id=1, source_target_pairs={{0,1},{1,0},{2,3},{3,2},{4,5},{5,4},{6,7},{7,6},{8,9},{9,8},{10,11... | collective-permute-start | bytes 245768 | tf_op jit(solution)/shard_map/ppermute | solution.py:363
  14.4 0.0 collective-permute-start.2
  14.4 0.6 %collective-permute-start.3 = (bf16[16,2560]{1,0:T(8,128)(2,1)S(1)}, bf16[16,2560]{1,0:T(8,128)(2,1)S(1)}, u32[]{:S(2)}, u32[]{:S(2)}) collective-permute-start(bf16[16,2560]{1,0:T(8,128)(2,1)S(1)} %get-tuple-element.17), channel_id=1, source_target_pairs={{0,2},{1,3},{2,0},{3,1},{4,6},{5,7},{6,4},{7,5},{8,10},{9,11},{10,... | collective-permute-start | bytes 245768 | tf_op jit(solution)/shard_map/ppermute | solution.py:363
  15.0 4.7 %collective-permute-start.4 = (bf16[16,2560]{1,0:T(8,128)(2,1)S(1)}, bf16[16,2560]{1,0:T(8,128)(2,1)S(1)}, u32[]{:S(2)}, u32[]{:S(2)}) collective-permute-start(bf16[16,2560]{1,0:T(8,128)(2,1)S(1)} %get-tuple-element.18), channel_id=1, source_target_pairs={{0,7},{1,6},{2,5},{3,4},{4,3},{5,2},{6,1},{7,0},{8,15},{9,14},{10,... | collective-permute-start | bytes 245768 | tf_op jit(solution)/shard_map/ppermute | solution.py:363
  19.7 0.0 collective-permute-done.refs_0_
  19.7 0.0 collective-permute-start.5
  19.7 0.0 collective-permute-done.1.refs_1_
  19.7 1.9 %collective-permute-start.6 = (bf16[16,2560]{1,0:T(8,128)(2,1)S(1)}, bf16[16,2560]{1,0:T(8,128)(2,1)S(1)}, u32[]{:S(2)}, u32[]{:S(2)}) collective-permute-start(bf16[16,2560]{1,0:T(8,128)(2,1)S(1)} %get-tuple-element.20), channel_id=1, source_target_pairs={{0,4},{1,5},{2,6},{3,7},{4,0},{5,1},{6,2},{7,3},{8,12},{9,13},{10,... | collective-permute-start | bytes 245768 | tf_op jit(solution)/shard_map/ppermute | solution.py:363
  21.6 1.0 %collective-permute-done.2.refs_2_ = bf16[16,2560]{1,0:T(8,128)(2,1)S(1)} collective-permute-done((bf16[16,2560]{1,0:T(8,128)(2,1)S(1)}, bf16[16,2560]{1,0:T(8,128)(2,1)S(1)}, u32[]{:S(2)}, u32[]{:S(2)}) %collective-permute-start.2) | collective-permute-done | bytes 81952 | tf_op jit(solution)/shard_map/ppermute | solution.py:363
  22.6 0.0 collective-permute-done.3.refs_3_
  22.6 1.8 %collective-permute-done.4.refs_4_ = bf16[16,2560]{1,0:T(8,128)(2,1)S(1)} collective-permute-done((bf16[16,2560]{1,0:T(8,128)(2,1)S(1)}, bf16[16,2560]{1,0:T(8,128)(2,1)S(1)}, u32[]{:S(2)}, u32[]{:S(2)}) %collective-permute-start.4) | collective-permute-done | bytes 81952 | tf_op jit(solution)/shard_map/ppermute | solution.py:363
  24.4 1.0 %collective-permute-done.5.refs_5_ = bf16[16,2560]{1,0:T(8,128)(2,1)S(1)} collective-permute-done((bf16[16,2560]{1,0:T(8,128)(2,1)S(1)}, bf16[16,2560]{1,0:T(8,128)(2,1)S(1)}, u32[]{:S(2)}, u32[]{:S(2)}) %collective-permute-start.5) | collective-permute-done | bytes 81952 | tf_op jit(solution)/shard_map/ppermute | solution.py:363
  25.4 1.4 %collective-permute-done.6.refs_6_ = bf16[16,2560]{1,0:T(8,128)(2,1)S(1)} collective-permute-done((bf16[16,2560]{1,0:T(8,128)(2,1)S(1)}, bf16[16,2560]{1,0:T(8,128)(2,1)S(1)}, u32[]{:S(2)}, u32[]{:S(2)}) %collective-permute-start.6) | collective-permute-done | bytes 81952 | tf_op jit(solution)/shard_map/ppermute | solution.py:363
  26.8 0.6 %join_and_gram.1 = (bf16[128,2048]{1,0:T(8,128)(2,1)S(1)}, f32[64,128]{1,0:T(8,128)S(1)}) custom-call(bf16[4,128,256]{2,1,0:T(8,128)(2,1)S(1)} %get-tuple-element.13.join_ref, bf16[16,2560]{1,0:T(8,128)(2,1)S(1)} %collective-permute-done.refs_0_, bf16[16,2560]{1,0:T(8,128)(2,1)S(1)} %collective-permute-done.1.refs_1_, ...), custom_call_target="tpu_custom_call" | custom-call | tf_op jit(solution)/shard_map/join_and_gram/pallas_call | solution.py:148
  27.3 0.1 collective-permute-start.7
  27.4 1.2 %collective-permute-done.7 = f32[64,128]{1,0:T(8,128)S(1)} collective-permute-done((f32[64,128]{1,0:T(8,128)S(1)}, f32[64,128]{1,0:T(8,128)S(1)}, u32[]{:S(2)}, u32[]{:S(2)}) %collective-permute-start.7) | collective-permute-done | bytes 32800 | tf_op jit(solution)/shard_map/ppermute | solution.py:188
  28.6 1.3 %collective-permute-start.10 = (f32[64,128]{1,0:T(8,128)S(1)}, f32[64,128]{1,0:T(8,128)S(1)}, u32[]{:S(2)}, u32[]{:S(2)}) collective-permute-start(f32[64,128]{1,0:T(8,128)S(1)} %add.12), channel_id=1, source_target_pairs={{0,9},{1,8},{2,11},{3,10},{4,13},{5,12},{6,15},{7,14},{8,1},{9,0},... | collective-permute-start | bytes 98312 | tf_op jit(solution)/shard_map/ppermute | solution.py:188
  29.9 1.4 %collective-permute-start.9 = (f32[64,128]{1,0:T(8,128)S(1)}, f32[64,128]{1,0:T(8,128)S(1)}, u32[]{:S(2)}, u32[]{:S(2)}) collective-permute-start(f32[64,128]{1,0:T(8,128)S(1)} %add.12), channel_id=1, source_target_pairs={{0,25},{1,24},{2,27},{3,26},{4,29},{5,28},{6,31},{7,30},{8,17},{9,... | collective-permute-start | bytes 98312 | tf_op jit(solution)/shard_map/ppermute | solution.py:188
  31.3 0.3 collective-permute-start.8
  31.6 0.4 collective-permute-done.10
  32.0 2.2 %collective-permute-done.9 = f32[64,128]{1,0:T(8,128)S(1)} collective-permute-done((f32[64,128]{1,0:T(8,128)S(1)}, f32[64,128]{1,0:T(8,128)S(1)}, u32[]{:S(2)}, u32[]{:S(2)}) %collective-permute-start.9) | collective-permute-done | bytes 32800 | tf_op jit(solution)/shard_map/ppermute | solution.py:188
  34.1 0.5 %collective-permute-done.8 = f32[64,128]{1,0:T(8,128)S(1)} collective-permute-done((f32[64,128]{1,0:T(8,128)S(1)}, f32[64,128]{1,0:T(8,128)S(1)}, u32[]{:S(2)}, u32[]{:S(2)}) %collective-permute-start.8) | collective-permute-done | bytes 32800 | tf_op jit(solution)/shard_map/ppermute | solution.py:188
  34.7 0.4 collective-permute-start.13
  35.0 2.3 %collective-permute-start.12 = (f32[64,128]{1,0:T(8,128)S(1)}, f32[64,128]{1,0:T(8,128)S(1)}, u32[]{:S(2)}, u32[]{:S(2)}) collective-permute-start(f32[64,128]{1,0:T(8,128)S(1)} %add_add_fusion.refs_0_), channel_id=1, source_target_pairs={{0,14},{1,15},{2,12},{3,13},{4,10},{5,11},{6,8},{7,9},{8,6},{9,7},... | collective-permute-start | bytes 98312 | tf_op jit(solution)/shard_map/ppermute | solution.py:188
  37.3 0.4 collective-permute-start.11
  37.7 2.0 %collective-permute-done.13.refs_3_ = f32[64,128]{1,0:T(8,128)S(1)} collective-permute-done((f32[64,128]{1,0:T(8,128)S(1)}, f32[64,128]{1,0:T(8,128)S(1)}, u32[]{:S(2)}, u32[]{:S(2)}) %collective-permute-start.13) | collective-permute-done | bytes 32800 | tf_op jit(solution)/shard_map/ppermute | solution.py:188
  39.7 0.5 %collective-permute-done.12.refs_2_ = f32[64,128]{1,0:T(8,128)S(1)} collective-permute-done((f32[64,128]{1,0:T(8,128)S(1)}, f32[64,128]{1,0:T(8,128)S(1)}, u32[]{:S(2)}, u32[]{:S(2)}) %collective-permute-start.12) | collective-permute-done | bytes 32800 | tf_op jit(solution)/shard_map/ppermute | solution.py:188
  40.2 0.9 %collective-permute-done.11.refs_1_ = f32[64,128]{1,0:T(8,128)S(1)} collective-permute-done((f32[64,128]{1,0:T(8,128)S(1)}, f32[64,128]{1,0:T(8,128)S(1)}, u32[]{:S(2)}, u32[]{:S(2)}) %collective-permute-start.11) | collective-permute-done | bytes 32800 | tf_op jit(solution)/shard_map/ppermute | solution.py:188
  41.2 2.9 %whiten.1 = (f32[2,64,64]{2,1,0:T(8,128)}, f32[2,64,2048]{2,1,0:T(8,128)}) custom-call(f32[64,128]{1,0:T(8,128)S(1)} %add_add_fusion.refs_0_, f32[64,128]{1,0:T(8,128)S(1)} %collective-permute-done.11.refs_1_, f32[64,128]{1,0:T(8,128)S(1)} %collective-permute-done.12.refs_2_, f32[64,128]{1,0:T(8,128)S(1)} %collective-permute-done.13.refs_3_, ...), custom_call_target="tpu_custom_call" | custom-call | tf_op jit(solution)/shard_map/whiten/pallas_call | solution.py:335
  (2 shorter events, 0.0 us)
Async XLA Ops:
  7.7 12.0 %collective-permute-start = (bf16[16,2560]{1,0:T(8,128)(2,1)S(1)}, bf16[16,2560]{1,0:T(8,128)(2,1)S(1)}, u32[]{:S(2)}, u32[]{:S(2)}) collective-permute-start(bf16[16,2560]{1,0:T(8,128)(2,1)S(1)} %get-tuple-element.14), channel_id=1, source_target_pairs={{0,6},{1,7},{2,4},{3,5},{4,2},{5,3},{6,0},{7,1},{8,14},{9,15},{10,... | collective-permute-start | bytes 245768 | tf_op jit(solution)/shard_map/ppermute | solution.py:363
  12.9 6.8 %collective-permute-start.1 = (bf16[16,2560]{1,0:T(8,128)(2,1)S(1)}, bf16[16,2560]{1,0:T(8,128)(2,1)S(1)}, u32[]{:S(2)}, u32[]{:S(2)}) collective-permute-start(bf16[16,2560]{1,0:T(8,128)(2,1)S(1)} %get-tuple-element.15), channel_id=1, source_target_pairs={{0,1},{1,0},{2,3},{3,2},{4,5},{5,4},{6,7},{7,6},{8,9},{9,8},{10,11... | collective-permute-start | bytes 245768 | tf_op jit(solution)/shard_map/ppermute | solution.py:363
  14.4 8.2 %collective-permute-start.2 = (bf16[16,2560]{1,0:T(8,128)(2,1)S(1)}, bf16[16,2560]{1,0:T(8,128)(2,1)S(1)}, u32[]{:S(2)}, u32[]{:S(2)}) collective-permute-start(bf16[16,2560]{1,0:T(8,128)(2,1)S(1)} %get-tuple-element.16), channel_id=1, source_target_pairs={{0,5},{1,4},{2,7},{3,6},{4,1},{5,0},{6,3},{7,2},{8,13},{9,12},{10,... | collective-permute-start | bytes 245768 | tf_op jit(solution)/shard_map/ppermute | solution.py:363
  14.4 8.2 %collective-permute-start.3 = (bf16[16,2560]{1,0:T(8,128)(2,1)S(1)}, bf16[16,2560]{1,0:T(8,128)(2,1)S(1)}, u32[]{:S(2)}, u32[]{:S(2)}) collective-permute-start(bf16[16,2560]{1,0:T(8,128)(2,1)S(1)} %get-tuple-element.17), channel_id=1, source_target_pairs={{0,2},{1,3},{2,0},{3,1},{4,6},{5,7},{6,4},{7,5},{8,10},{9,11},{10,... | collective-permute-start | bytes 245768 | tf_op jit(solution)/shard_map/ppermute | solution.py:363
  15.0 9.4 %collective-permute-start.4 = (bf16[16,2560]{1,0:T(8,128)(2,1)S(1)}, bf16[16,2560]{1,0:T(8,128)(2,1)S(1)}, u32[]{:S(2)}, u32[]{:S(2)}) collective-permute-start(bf16[16,2560]{1,0:T(8,128)(2,1)S(1)} %get-tuple-element.18), channel_id=1, source_target_pairs={{0,7},{1,6},{2,5},{3,4},{4,3},{5,2},{6,1},{7,0},{8,15},{9,14},{10,... | collective-permute-start | bytes 245768 | tf_op jit(solution)/shard_map/ppermute | solution.py:363
  19.7 5.7 %collective-permute-start.5 = (bf16[16,2560]{1,0:T(8,128)(2,1)S(1)}, bf16[16,2560]{1,0:T(8,128)(2,1)S(1)}, u32[]{:S(2)}, u32[]{:S(2)}) collective-permute-start(bf16[16,2560]{1,0:T(8,128)(2,1)S(1)} %get-tuple-element.19), channel_id=1, source_target_pairs={{0,3},{1,2},{2,1},{3,0},{4,7},{5,6},{6,5},{7,4},{8,11},{9,10},{10,... | collective-permute-start | bytes 245768 | tf_op jit(solution)/shard_map/ppermute | solution.py:363
  19.7 7.1 %collective-permute-start.6 = (bf16[16,2560]{1,0:T(8,128)(2,1)S(1)}, bf16[16,2560]{1,0:T(8,128)(2,1)S(1)}, u32[]{:S(2)}, u32[]{:S(2)}) collective-permute-start(bf16[16,2560]{1,0:T(8,128)(2,1)S(1)} %get-tuple-element.20), channel_id=1, source_target_pairs={{0,4},{1,5},{2,6},{3,7},{4,0},{5,1},{6,2},{7,3},{8,12},{9,13},{10,... | collective-permute-start | bytes 245768 | tf_op jit(solution)/shard_map/ppermute | solution.py:363
  27.3 1.3 %collective-permute-start.7 = (f32[64,128]{1,0:T(8,128)S(1)}, f32[64,128]{1,0:T(8,128)S(1)}, u32[]{:S(2)}, u32[]{:S(2)}) collective-permute-start(f32[64,128]{1,0:T(8,128)S(1)} %get-tuple-element.22), channel_id=1, source_target_pairs={{0,8},{1,9},{2,10},{3,11},{4,12},{5,13},{6,14},{7,15},{8,0},{9,1},... | collective-permute-start | bytes 98312 | tf_op jit(solution)/shard_map/ppermute | solution.py:188
  28.6 3.3 %collective-permute-start.10 = (f32[64,128]{1,0:T(8,128)S(1)}, f32[64,128]{1,0:T(8,128)S(1)}, u32[]{:S(2)}, u32[]{:S(2)}) collective-permute-start(f32[64,128]{1,0:T(8,128)S(1)} %add.12), channel_id=1, source_target_pairs={{0,9},{1,8},{2,11},{3,10},{4,13},{5,12},{6,15},{7,14},{8,1},{9,0},... | collective-permute-start | bytes 98312 | tf_op jit(solution)/shard_map/ppermute | solution.py:188
  29.9 4.2 %collective-permute-start.9 = (f32[64,128]{1,0:T(8,128)S(1)}, f32[64,128]{1,0:T(8,128)S(1)}, u32[]{:S(2)}, u32[]{:S(2)}) collective-permute-start(f32[64,128]{1,0:T(8,128)S(1)} %add.12), channel_id=1, source_target_pairs={{0,25},{1,24},{2,27},{3,26},{4,29},{5,28},{6,31},{7,30},{8,17},{9,... | collective-permute-start | bytes 98312 | tf_op jit(solution)/shard_map/ppermute | solution.py:188
  31.3 3.3 %collective-permute-start.8 = (f32[64,128]{1,0:T(8,128)S(1)}, f32[64,128]{1,0:T(8,128)S(1)}, u32[]{:S(2)}, u32[]{:S(2)}) collective-permute-start(f32[64,128]{1,0:T(8,128)S(1)} %add.12), channel_id=1, source_target_pairs={{0,24},{1,25},{2,26},{3,27},{4,28},{5,29},{6,30},{7,31},{8,16},{9,... | collective-permute-start | bytes 98312 | tf_op jit(solution)/shard_map/ppermute | solution.py:188
  34.7 5.1 %collective-permute-start.13 = (f32[64,128]{1,0:T(8,128)S(1)}, f32[64,128]{1,0:T(8,128)S(1)}, u32[]{:S(2)}, u32[]{:S(2)}) collective-permute-start(f32[64,128]{1,0:T(8,128)S(1)} %add_add_fusion.refs_0_), channel_id=1, source_target_pairs={{0,12},{1,13},{2,14},{3,15},{4,8},{5,9},{6,10},{7,11},{8,4},{9,5},... | collective-permute-start | bytes 98312 | tf_op jit(solution)/shard_map/ppermute | solution.py:188
  35.0 5.2 %collective-permute-start.12 = (f32[64,128]{1,0:T(8,128)S(1)}, f32[64,128]{1,0:T(8,128)S(1)}, u32[]{:S(2)}, u32[]{:S(2)}) collective-permute-start(f32[64,128]{1,0:T(8,128)S(1)} %add_add_fusion.refs_0_), channel_id=1, source_target_pairs={{0,14},{1,15},{2,12},{3,13},{4,10},{5,11},{6,8},{7,9},{8,6},{9,7},... | collective-permute-start | bytes 98312 | tf_op jit(solution)/shard_map/ppermute | solution.py:188
  37.3 3.9 %collective-permute-start.11 = (f32[64,128]{1,0:T(8,128)S(1)}, f32[64,128]{1,0:T(8,128)S(1)}, u32[]{:S(2)}, u32[]{:S(2)}) collective-permute-start(f32[64,128]{1,0:T(8,128)S(1)} %add_add_fusion.refs_0_), channel_id=1, source_target_pairs={{0,10},{1,11},{2,8},{3,9},{4,14},{5,15},{6,12},{7,13},{8,2},{9,3},... | collective-permute-start | bytes 98312 | tf_op jit(solution)/shard_map/ppermute | solution.py:188

commit v7 on v6

--- a/solution.py
+++ b/solution.py
@@ -48,7 +48,7 @@
             table_ref[first : first + 2 * SUB, half * HOP : (half + 1) * HOP] = packed
 
 
-def block_sums(freq_bins, position, snapshots, shards, shifts):
+def block_sums(freq_bins, position, snapshots, shards, shifts, table=None, join_shifts=()):
     samples, points = snapshots.shape
     half_count = samples // HOP
     rows = SERIES * half_count
@@ -56,9 +56,11 @@
     fold = width // half_count
     table_shape = (rows + SUB * 2, samples)
     count = len(shifts)
+    first_call = table is None
 
     def body(freq_ref, position_ref, data_ref, *refs):
-        outs, (join_ref, table_ref, buffer_ref, sems) = refs[:count], refs[count:]
+        table_ref, outs = refs[0], refs[1:]
+        buffer_ref, sems = refs[-2:]
         copies = []
         for i, shift in enumerate(shifts):
             first = pl.multiple_of((position_ref[0] ^ shift) * width, width)
@@ -68,9 +70,11 @@
                 )
             )
             copies[-1].start()
-        fill_table(freq_ref, table_ref, half_count)
-        for k in range(half_count):
-            join_ref[k] = join_matrix(position_ref[0], shifts, k, half_count)
+        if first_call:
+            fill_table(freq_ref, table_ref, half_count)
+        if join_shifts:
+            for k in range(half_count):
+                outs[count][k] = join_matrix(position_ref[0], join_shifts, k, half_count)
         for copy, out_ref, i in zip(copies, outs, range(count)):
             copy.wait()
             sums = jnp.dot(table_ref[...], buffer_ref[i], preferred_element_type=jnp.float32)
@@ -83,20 +87,26 @@
 
     local = pl.BlockSpec(memory_space=pltpu.VMEM)
     shapes = [pltpu.VMEM((rows, width + fold), jnp.bfloat16) for _ in shifts]
-    shapes.append(pltpu.VMEM((half_count, rows * shards, 2 * rows * shards), jnp.bfloat16))
+    if join_shifts:
+        joins = (half_count, rows * shards, 2 * rows * shards)
+        shapes.append(pltpu.VMEM(joins, jnp.bfloat16))
+    operands = [freq_bins, position, snapshots]
+    if first_call:
+        shapes.insert(0, pltpu.VMEM(table_shape, jnp.bfloat16))
+    else:
+        operands.append(near(table))
     smem = pl.BlockSpec(memory_space=pltpu.SMEM)
     return pl.pallas_call(
         body,
-        in_specs=[smem, smem, pl.BlockSpec(memory_space=pl.ANY)],
+        in_specs=[smem, smem, pl.BlockSpec(memory_space=pl.ANY)] + [local] * (len(operands) - 3),
         out_shape=tuple(shapes),
         out_specs=(local,) * len(shapes),
         scratch_shapes=[
-            pltpu.VMEM(table_shape, jnp.bfloat16),
             pltpu.VMEM((count, samples, width), jnp.bfloat16),
             pltpu.SemaphoreType.DMA((count,)),
         ],
         name="block_sums",
-    )(freq_bins, position, snapshots)
+    )(*operands)
 
 
 def join_matrix(position, shifts, k, half_count):
@@ -355,12 +365,20 @@
     half_count = snapshots.shape[0] // HOP
     grid_total = snapshots.shape[1] * lax.axis_size("space")
     position = lax.axis_index("tm").astype(jnp.int32)[None]
-    shifts = spread_order(shards)
-    *parts, joins = block_sums(freq_bins, position, snapshots, shards, shifts)
-    received = []
-    for shift, part in zip(shifts, parts):
-        pairs = [(i, i ^ shift) for i in range(shards)]
-        received.append(lax.ppermute(part, "tm", pairs) if shift else part)
+    order = spread_order(shards)
+    groups = [order[:-1], order[-1:]]
+    shifts = [shift for group in groups for shift in group]
+    received, table, joins = [], None, None
+    for group in groups:
+        done = shifts if group is groups[-1] else ()
+        parts = list(block_sums(freq_bins, position, snapshots, shards, group, table, done))
+        if table is None:
+            table = parts.pop(0)
+        if done:
+            joins = parts.pop()
+        for shift, part in zip(group, parts):
+            pairs = [(i, i ^ shift) for i in range(shards)]
+            received.append(lax.ppermute(part, "tm", pairs) if shift else part)
     columns, gram = join_and_gram(received, joins, half_count, grid_total)
     grams = [gram]
     for flips in exchange_rounds():

time: 44.3 us -> 43.6 us (0.984)
  waiting for transfers between devices: 12.8 us -> 10.1 us
  Pallas kernels: 10.6 us -> 12.7 us
    ppermute x7, waiting for transfers between devices: 5.15 us -> 2.39 us  [on_device(): received.append(lax.ppermute(part, 'tm', pairs) if shift else part)]
    pallas_call x1 -> x2, Pallas kernels: 7.09 us -> 9.22 us  [block_sums(): pl.pallas_call(body, in_specs=[smem, smem, pl.BlockSpec(memory_space=pl.A...]
  transfers between devices with their start and end apart: 14 -> 14, of which waited for: 11 -> 9; matrix products, arithmetic and copies ran while one was open for 0% -> 0% of each run, Pallas kernels for 0% -> 6%
where the time goes in v7:
time: 43.6 us; the launch traced here: 43.5 us
  starting transfers between devices  20 us (46%)
  Pallas kernels  12.7 us (29%)
  waiting for transfers between devices  10.1 us (23%)
  between operations  0.7 us (2%)
    ppermute x7, starting transfers between devices, on_device(): received.append(lax.ppermute(part, 'tm', pairs) if shift else part)  13.9 us
    pallas_call x2, Pallas kernels, block_sums(): pl.pallas_call(body, in_specs=[smem, smem, pl.BlockSpec(memory_space=pl.A...  9.22 us
    ppermute x7, waiting for transfers between devices, swapped(): return lax.ppermute(value, GRID, pairs)  7.66 us
    ppermute x7, starting transfers between devices, swapped(): return lax.ppermute(value, GRID, pairs)  6.13 us
    pallas_call x1, Pallas kernels, whiten(): pl.pallas_call(body, in_specs=[pl.BlockSpec(memory_space=pltpu.VMEM)] * (...  2.92 us
    ppermute x7, waiting for transfers between devices, on_device(): received.append(lax.ppermute(part, 'tm', pairs) if shift else part)  2.39 us
  transfers between devices with their start and end apart: 14, of which 9 were waited for; matrix products, arithmetic and copies ran while one was open for 0% of the time, Pallas kernels for 6%

profile of v7, /device:TPU:0, one launch (start us, length us, event | category | flops | bytes accessed | tf_op | source)
XLA Modules:
  0.0 43.5 jit_solution(2772375430352521363)
XLA Ops:
  0.6 6.5 %block_sums.2 = (bf16[32,512]{1,0:T(8,128)(2,1)S(1)}, bf16[16,2560]{1,0:T(8,128)(2,1)S(1)}, bf16[16,2560]{1,0:T(8,128)(2,1)S(1)}, bf16[16,2560]{1,0:T(8,128)(2,1...) custom-call(s32[2]{0:T(128)} %freq_ref.3, ...), custom_call_target="tpu_custom_call" | custom-call | tf_op jit(solution)/shard_map/block_sums/pallas_call | solution.py:99
  7.1 5.1 %collective-permute-start = (bf16[16,2560]{1,0:T(8,128)(2,1)S(1)}, bf16[16,2560]{1,0:T(8,128)(2,1)S(1)}, u32[]{:S(2)}, u32[]{:S(2)}) collective-permute-start(bf16[16,2560]{1,0:T(8,128)(2,1)S(1)} %get-tuple-element.16), channel_id=1, source_target_pairs={{0,6},{1,7},{2,4},{3,5},{4,2},{5,3},{6,0},{7,1},{8,14},{9,15},{10,... | collective-permute-start | bytes 245768 | tf_op jit(solution)/shard_map/ppermute | solution.py:381
  12.3 1.5 %collective-permute-start.1 = (bf16[16,2560]{1,0:T(8,128)(2,1)S(1)}, bf16[16,2560]{1,0:T(8,128)(2,1)S(1)}, u32[]{:S(2)}, u32[]{:S(2)}) collective-permute-start(bf16[16,2560]{1,0:T(8,128)(2,1)S(1)} %get-tuple-element.17), channel_id=1, source_target_pairs={{0,1},{1,0},{2,3},{3,2},{4,5},{5,4},{6,7},{7,6},{8,9},{9,8},{10,11... | collective-permute-start | bytes 245768 | tf_op jit(solution)/shard_map/ppermute | solution.py:381
  13.8 0.0 collective-permute-start.2
  13.8 0.6 %collective-permute-start.3 = (bf16[16,2560]{1,0:T(8,128)(2,1)S(1)}, bf16[16,2560]{1,0:T(8,128)(2,1)S(1)}, u32[]{:S(2)}, u32[]{:S(2)}) collective-permute-start(bf16[16,2560]{1,0:T(8,128)(2,1)S(1)} %get-tuple-element.19), channel_id=1, source_target_pairs={{0,2},{1,3},{2,0},{3,1},{4,6},{5,7},{6,4},{7,5},{8,10},{9,11},{10,... | collective-permute-start | bytes 245768 | tf_op jit(solution)/shard_map/ppermute | solution.py:381
  14.4 4.7 %collective-permute-start.4 = (bf16[16,2560]{1,0:T(8,128)(2,1)S(1)}, bf16[16,2560]{1,0:T(8,128)(2,1)S(1)}, u32[]{:S(2)}, u32[]{:S(2)}) collective-permute-start(bf16[16,2560]{1,0:T(8,128)(2,1)S(1)} %get-tuple-element.20), channel_id=1, source_target_pairs={{0,7},{1,6},{2,5},{3,4},{4,3},{5,2},{6,1},{7,0},{8,15},{9,14},{10,... | collective-permute-start | bytes 245768 | tf_op jit(solution)/shard_map/ppermute | solution.py:381
  19.1 0.0 collective-permute-done.refs_0_
  19.1 0.0 collective-permute-start.5
  19.1 0.0 collective-permute-done.1.refs_1_
  19.1 1.9 %collective-permute-start.6 = (bf16[16,2560]{1,0:T(8,128)(2,1)S(1)}, bf16[16,2560]{1,0:T(8,128)(2,1)S(1)}, u32[]{:S(2)}, u32[]{:S(2)}) collective-permute-start(bf16[16,2560]{1,0:T(8,128)(2,1)S(1)} %get-tuple-element.22), channel_id=1, source_target_pairs={{0,4},{1,5},{2,6},{3,7},{4,0},{5,1},{6,2},{7,3},{8,12},{9,13},{10,... | collective-permute-start | bytes 245768 | tf_op jit(solution)/shard_map/ppermute | solution.py:381
  21.0 2.7 %block_sums.3 = (bf16[16,2560]{1,0:T(8,128)(2,1)S(1)}, bf16[4,128,256]{2,1,0:T(8,128)(2,1)S(1)}) custom-call(s32[2]{0:T(128)} %freq_ref.3, s32[1]{0:T(128)} %bitcast.position_ref, bf16[512,16384]{1,0:T(8,128)(2,1)} %data_ref.3, bf16[32,512]{1,0:T(8,128)(2,1)S(1)} %get-tuple-element.14.refs_0_), custom_call_target="tpu_custom_call" | custom-call | tf_op jit(solution)/shard_map/block_sums/pallas_call | solution.py:99
  23.8 0.0 collective-permute-done.2.refs_2_
  23.8 0.0 collective-permute-done.3.refs_3_
  23.8 0.0 collective-permute-done.4.refs_4_
  23.8 1.0 %collective-permute-done.5.refs_5_ = bf16[16,2560]{1,0:T(8,128)(2,1)S(1)} collective-permute-done((bf16[16,2560]{1,0:T(8,128)(2,1)S(1)}, bf16[16,2560]{1,0:T(8,128)(2,1)S(1)}, u32[]{:S(2)}, u32[]{:S(2)}) %collective-permute-start.5) | collective-permute-done | bytes 81952 | tf_op jit(solution)/shard_map/ppermute | solution.py:381
  24.8 1.4 %collective-permute-done.6.refs_6_ = bf16[16,2560]{1,0:T(8,128)(2,1)S(1)} collective-permute-done((bf16[16,2560]{1,0:T(8,128)(2,1)S(1)}, bf16[16,2560]{1,0:T(8,128)(2,1)S(1)}, u32[]{:S(2)}, u32[]{:S(2)}) %collective-permute-start.6) | collective-permute-done | bytes 81952 | tf_op jit(solution)/shard_map/ppermute | solution.py:381
  26.2 0.6 %join_and_gram.1 = (bf16[128,2048]{1,0:T(8,128)(2,1)S(1)}, f32[64,128]{1,0:T(8,128)S(1)}) custom-call(bf16[4,128,256]{2,1,0:T(8,128)(2,1)S(1)} %get-tuple-element.15.join_ref, bf16[16,2560]{1,0:T(8,128)(2,1)S(1)} %collective-permute-done.refs_0_, bf16[16,2560]{1,0:T(8,128)(2,1)S(1)} %collective-permute-done.1.refs_1_, ...), custom_call_target="tpu_custom_call" | custom-call | tf_op jit(solution)/shard_map/join_and_gram/pallas_call | solution.py:158
  26.7 0.1 collective-permute-start.7
  26.8 1.2 %collective-permute-done.7 = f32[64,128]{1,0:T(8,128)S(1)} collective-permute-done((f32[64,128]{1,0:T(8,128)S(1)}, f32[64,128]{1,0:T(8,128)S(1)}, u32[]{:S(2)}, u32[]{:S(2)}) %collective-permute-start.7) | collective-permute-done | bytes 32800 | tf_op jit(solution)/shard_map/ppermute | solution.py:198
  28.0 1.3 %collective-permute-start.10 = (f32[64,128]{1,0:T(8,128)S(1)}, f32[64,128]{1,0:T(8,128)S(1)}, u32[]{:S(2)}, u32[]{:S(2)}) collective-permute-start(f32[64,128]{1,0:T(8,128)S(1)} %add.12), channel_id=1, source_target_pairs={{0,9},{1,8},{2,11},{3,10},{4,13},{5,12},{6,15},{7,14},{8,1},{9,0},... | collective-permute-start | bytes 98312 | tf_op jit(solution)/shard_map/ppermute | solution.py:198
  29.3 1.4 %collective-permute-start.9 = (f32[64,128]{1,0:T(8,128)S(1)}, f32[64,128]{1,0:T(8,128)S(1)}, u32[]{:S(2)}, u32[]{:S(2)}) collective-permute-start(f32[64,128]{1,0:T(8,128)S(1)} %add.12), channel_id=1, source_target_pairs={{0,25},{1,24},{2,27},{3,26},{4,29},{5,28},{6,31},{7,30},{8,17},{9,... | collective-permute-start | bytes 98312 | tf_op jit(solution)/shard_map/ppermute | solution.py:198
  30.7 0.3 collective-permute-start.8
  31.0 0.4 collective-permute-done.10
  31.4 2.2 %collective-permute-done.9 = f32[64,128]{1,0:T(8,128)S(1)} collective-permute-done((f32[64,128]{1,0:T(8,128)S(1)}, f32[64,128]{1,0:T(8,128)S(1)}, u32[]{:S(2)}, u32[]{:S(2)}) %collective-permute-start.9) | collective-permute-done | bytes 32800 | tf_op jit(solution)/shard_map/ppermute | solution.py:198
  33.5 0.5 %collective-permute-done.8 = f32[64,128]{1,0:T(8,128)S(1)} collective-permute-done((f32[64,128]{1,0:T(8,128)S(1)}, f32[64,128]{1,0:T(8,128)S(1)}, u32[]{:S(2)}, u32[]{:S(2)}) %collective-permute-start.8) | collective-permute-done | bytes 32800 | tf_op jit(solution)/shard_map/ppermute | solution.py:198
  34.0 0.4 collective-permute-start.13
  34.4 2.3 %collective-permute-start.12 = (f32[64,128]{1,0:T(8,128)S(1)}, f32[64,128]{1,0:T(8,128)S(1)}, u32[]{:S(2)}, u32[]{:S(2)}) collective-permute-start(f32[64,128]{1,0:T(8,128)S(1)} %add_add_fusion.refs_0_), channel_id=1, source_target_pairs={{0,14},{1,15},{2,12},{3,13},{4,10},{5,11},{6,8},{7,9},{8,6},{9,7},... | collective-permute-start | bytes 98312 | tf_op jit(solution)/shard_map/ppermute | solution.py:198
  36.7 0.4 %collective-permute-start.11 = (f32[64,128]{1,0:T(8,128)S(1)}, f32[64,128]{1,0:T(8,128)S(1)}, u32[]{:S(2)}, u32[]{:S(2)}) collective-permute-start(f32[64,128]{1,0:T(8,128)S(1)} %add_add_fusion.refs_0_), channel_id=1, source_target_pairs={{0,10},{1,11},{2,8},{3,9},{4,14},{5,15},{6,12},{7,13},{8,2},{9,3},... | collective-permute-start | bytes 98312 | tf_op jit(solution)/shard_map/ppermute | solution.py:198
  37.1 2.0 %collective-permute-done.13.refs_3_ = f32[64,128]{1,0:T(8,128)S(1)} collective-permute-done((f32[64,128]{1,0:T(8,128)S(1)}, f32[64,128]{1,0:T(8,128)S(1)}, u32[]{:S(2)}, u32[]{:S(2)}) %collective-permute-start.13) | collective-permute-done | bytes 32800 | tf_op jit(solution)/shard_map/ppermute | solution.py:198
  39.1 0.5 %collective-permute-done.12.refs_2_ = f32[64,128]{1,0:T(8,128)S(1)} collective-permute-done((f32[64,128]{1,0:T(8,128)S(1)}, f32[64,128]{1,0:T(8,128)S(1)}, u32[]{:S(2)}, u32[]{:S(2)}) %collective-permute-start.12) | collective-permute-done | bytes 32800 | tf_op jit(solution)/shard_map/ppermute | solution.py:198
  39.6 0.9 %collective-permute-done.11.refs_1_ = f32[64,128]{1,0:T(8,128)S(1)} collective-permute-done((f32[64,128]{1,0:T(8,128)S(1)}, f32[64,128]{1,0:T(8,128)S(1)}, u32[]{:S(2)}, u32[]{:S(2)}) %collective-permute-start.11) | collective-permute-done | bytes 32800 | tf_op jit(solution)/shard_map/ppermute | solution.py:198
  40.6 2.9 %whiten.1 = (f32[2,64,64]{2,1,0:T(8,128)}, f32[2,64,2048]{2,1,0:T(8,128)}) custom-call(f32[64,128]{1,0:T(8,128)S(1)} %add_add_fusion.refs_0_, f32[64,128]{1,0:T(8,128)S(1)} %collective-permute-done.11.refs_1_, f32[64,128]{1,0:T(8,128)S(1)} %collective-permute-done.12.refs_2_, f32[64,128]{1,0:T(8,128)S(1)} %collective-permute-done.13.refs_3_, ...), custom_call_target="tpu_custom_call" | custom-call | tf_op jit(solution)/shard_map/whiten/pallas_call | solution.py:345
  (2 shorter events, 0.0 us)
Async XLA Ops:
  7.1 12.0 %collective-permute-start = (bf16[16,2560]{1,0:T(8,128)(2,1)S(1)}, bf16[16,2560]{1,0:T(8,128)(2,1)S(1)}, u32[]{:S(2)}, u32[]{:S(2)}) collective-permute-start(bf16[16,2560]{1,0:T(8,128)(2,1)S(1)} %get-tuple-element.16), channel_id=1, source_target_pairs={{0,6},{1,7},{2,4},{3,5},{4,2},{5,3},{6,0},{7,1},{8,14},{9,15},{10,... | collective-permute-start | bytes 245768 | tf_op jit(solution)/shard_map/ppermute | solution.py:381
  12.3 6.8 %collective-permute-start.1 = (bf16[16,2560]{1,0:T(8,128)(2,1)S(1)}, bf16[16,2560]{1,0:T(8,128)(2,1)S(1)}, u32[]{:S(2)}, u32[]{:S(2)}) collective-permute-start(bf16[16,2560]{1,0:T(8,128)(2,1)S(1)} %get-tuple-element.17), channel_id=1, source_target_pairs={{0,1},{1,0},{2,3},{3,2},{4,5},{5,4},{6,7},{7,6},{8,9},{9,8},{10,11... | collective-permute-start | bytes 245768 | tf_op jit(solution)/shard_map/ppermute | solution.py:381
  13.8 10.0 %collective-permute-start.2 = (bf16[16,2560]{1,0:T(8,128)(2,1)S(1)}, bf16[16,2560]{1,0:T(8,128)(2,1)S(1)}, u32[]{:S(2)}, u32[]{:S(2)}) collective-permute-start(bf16[16,2560]{1,0:T(8,128)(2,1)S(1)} %get-tuple-element.18), channel_id=1, source_target_pairs={{0,5},{1,4},{2,7},{3,6},{4,1},{5,0},{6,3},{7,2},{8,13},{9,12},{10,... | collective-permute-start | bytes 245768 | tf_op jit(solution)/shard_map/ppermute | solution.py:381
  13.8 10.0 %collective-permute-start.3 = (bf16[16,2560]{1,0:T(8,128)(2,1)S(1)}, bf16[16,2560]{1,0:T(8,128)(2,1)S(1)}, u32[]{:S(2)}, u32[]{:S(2)}) collective-permute-start(bf16[16,2560]{1,0:T(8,128)(2,1)S(1)} %get-tuple-element.19), channel_id=1, source_target_pairs={{0,2},{1,3},{2,0},{3,1},{4,6},{5,7},{6,4},{7,5},{8,10},{9,11},{10,... | collective-permute-start | bytes 245768 | tf_op jit(solution)/shard_map/ppermute | solution.py:381
  14.4 9.4 %collective-permute-start.4 = (bf16[16,2560]{1,0:T(8,128)(2,1)S(1)}, bf16[16,2560]{1,0:T(8,128)(2,1)S(1)}, u32[]{:S(2)}, u32[]{:S(2)}) collective-permute-start(bf16[16,2560]{1,0:T(8,128)(2,1)S(1)} %get-tuple-element.20), channel_id=1, source_target_pairs={{0,7},{1,6},{2,5},{3,4},{4,3},{5,2},{6,1},{7,0},{8,15},{9,14},{10,... | collective-permute-start | bytes 245768 | tf_op jit(solution)/shard_map/ppermute | solution.py:381
  19.1 5.7 %collective-permute-start.5 = (bf16[16,2560]{1,0:T(8,128)(2,1)S(1)}, bf16[16,2560]{1,0:T(8,128)(2,1)S(1)}, u32[]{:S(2)}, u32[]{:S(2)}) collective-permute-start(bf16[16,2560]{1,0:T(8,128)(2,1)S(1)} %get-tuple-element.21), channel_id=1, source_target_pairs={{0,3},{1,2},{2,1},{3,0},{4,7},{5,6},{6,5},{7,4},{8,11},{9,10},{10,... | collective-permute-start | bytes 245768 | tf_op jit(solution)/shard_map/ppermute | solution.py:381
  19.1 7.1 %collective-permute-start.6 = (bf16[16,2560]{1,0:T(8,128)(2,1)S(1)}, bf16[16,2560]{1,0:T(8,128)(2,1)S(1)}, u32[]{:S(2)}, u32[]{:S(2)}) collective-permute-start(bf16[16,2560]{1,0:T(8,128)(2,1)S(1)} %get-tuple-element.22), channel_id=1, source_target_pairs={{0,4},{1,5},{2,6},{3,7},{4,0},{5,1},{6,2},{7,3},{8,12},{9,13},{10,... | collective-permute-start | bytes 245768 | tf_op jit(solution)/shard_map/ppermute | solution.py:381
  26.7 1.3 %collective-permute-start.7 = (f32[64,128]{1,0:T(8,128)S(1)}, f32[64,128]{1,0:T(8,128)S(1)}, u32[]{:S(2)}, u32[]{:S(2)}) collective-permute-start(f32[64,128]{1,0:T(8,128)S(1)} %get-tuple-element.24), channel_id=1, source_target_pairs={{0,8},{1,9},{2,10},{3,11},{4,12},{5,13},{6,14},{7,15},{8,0},{9,1},... | collective-permute-start | bytes 98312 | tf_op jit(solution)/shard_map/ppermute | solution.py:198
  28.0 3.3 %collective-permute-start.10 = (f32[64,128]{1,0:T(8,128)S(1)}, f32[64,128]{1,0:T(8,128)S(1)}, u32[]{:S(2)}, u32[]{:S(2)}) collective-permute-start(f32[64,128]{1,0:T(8,128)S(1)} %add.12), channel_id=1, source_target_pairs={{0,9},{1,8},{2,11},{3,10},{4,13},{5,12},{6,15},{7,14},{8,1},{9,0},... | collective-permute-start | bytes 98312 | tf_op jit(solution)/shard_map/ppermute | solution.py:198
  29.3 4.2 %collective-permute-start.9 = (f32[64,128]{1,0:T(8,128)S(1)}, f32[64,128]{1,0:T(8,128)S(1)}, u32[]{:S(2)}, u32[]{:S(2)}) collective-permute-start(f32[64,128]{1,0:T(8,128)S(1)} %add.12), channel_id=1, source_target_pairs={{0,25},{1,24},{2,27},{3,26},{4,29},{5,28},{6,31},{7,30},{8,17},{9,... | collective-permute-start | bytes 98312 | tf_op jit(solution)/shard_map/ppermute | solution.py:198
  30.7 3.3 %collective-permute-start.8 = (f32[64,128]{1,0:T(8,128)S(1)}, f32[64,128]{1,0:T(8,128)S(1)}, u32[]{:S(2)}, u32[]{:S(2)}) collective-permute-start(f32[64,128]{1,0:T(8,128)S(1)} %add.12), channel_id=1, source_target_pairs={{0,24},{1,25},{2,26},{3,27},{4,28},{5,29},{6,30},{7,31},{8,16},{9,... | collective-permute-start | bytes 98312 | tf_op jit(solution)/shard_map/ppermute | solution.py:198
  34.0 5.1 %collective-permute-start.13 = (f32[64,128]{1,0:T(8,128)S(1)}, f32[64,128]{1,0:T(8,128)S(1)}, u32[]{:S(2)}, u32[]{:S(2)}) collective-permute-start(f32[64,128]{1,0:T(8,128)S(1)} %add_add_fusion.refs_0_), channel_id=1, source_target_pairs={{0,12},{1,13},{2,14},{3,15},{4,8},{5,9},{6,10},{7,11},{8,4},{9,5},... | collective-permute-start | bytes 98312 | tf_op jit(solution)/shard_map/ppermute | solution.py:198
  34.4 5.2 %collective-permute-start.12 = (f32[64,128]{1,0:T(8,128)S(1)}, f32[64,128]{1,0:T(8,128)S(1)}, u32[]{:S(2)}, u32[]{:S(2)}) collective-permute-start(f32[64,128]{1,0:T(8,128)S(1)} %add_add_fusion.refs_0_), channel_id=1, source_target_pairs={{0,14},{1,15},{2,12},{3,13},{4,10},{5,11},{6,8},{7,9},{8,6},{9,7},... | collective-permute-start | bytes 98312 | tf_op jit(solution)/shard_map/ppermute | solution.py:198
  36.7 3.9 %collective-permute-start.11 = (f32[64,128]{1,0:T(8,128)S(1)}, f32[64,128]{1,0:T(8,128)S(1)}, u32[]{:S(2)}, u32[]{:S(2)}) collective-permute-start(f32[64,128]{1,0:T(8,128)S(1)} %add_add_fusion.refs_0_), channel_id=1, source_target_pairs={{0,10},{1,11},{2,8},{3,9},{4,14},{5,15},{6,12},{7,13},{8,2},{9,3},... | collective-permute-start | bytes 98312 | tf_op jit(solution)/shard_map/ppermute | solution.py:198
